TPU v7x, 32 devices: a whole 2x2x4 slice. The times are simulated.
32 devices in a mesh: dp: 2 (over y), fsdp: 16 (over z, x, core).
Axes of the slice: x: 2, y: 2, z: 4, core: 2. Of those that a mesh axis runs over, the one named last changes fastest.
Arguments:
- tokens: bfloat16 [32768, 768], P(('dp', 'fsdp')), may hold values from -6 to 6
- image_counts: int32 [32, 2], P(('dp', 'fsdp')), may hold values from 0 to 5, as said below
- cotangent: bfloat16 [32768, 768], P(('dp', 'fsdp')), may hold values from -6 to 6
- first_gain: bfloat16 [768], P('fsdp'), may hold values from 0.5 to 1.5
- first_shift: bfloat16 [768], P('fsdp'), may hold values from -3 to 3
- query_weight: bfloat16 [768, 768], P('fsdp'), may hold values from -0.21875 to 0.21875
- query_bias: bfloat16 [768], P('fsdp'), may hold values from -3 to 3
- key_weight: bfloat16 [768, 768], P('fsdp'), may hold values from -0.21875 to 0.21875
- value_weight: bfloat16 [768, 768], P('fsdp'), may hold values from -0.21875 to 0.21875
- value_bias: bfloat16 [768], P('fsdp'), may hold values from -3 to 3
- out_weight: bfloat16 [768, 768], P('fsdp'), may hold values from -0.625 to 0.625
- out_bias: bfloat16 [768], P('fsdp'), may hold values from -3 to 3
- second_gain: bfloat16 [768], P('fsdp'), may hold values from 0.5 to 1.5
- second_shift: bfloat16 [768], P('fsdp'), may hold values from -3 to 3
- up_weight: bfloat16 [768, 3072], P('fsdp'), may hold values from -0.21875 to 0.21875
- up_bias: bfloat16 [3072], P('fsdp'), may hold values from -3 to 3
- down_weight: bfloat16 [3072, 768], P('fsdp'), may hold values from -0.109375 to 0.109375
- down_bias: bfloat16 [768], P('fsdp'), may hold values from -3 to 3
Outputs:
- layer_out: bfloat16 [32768, 768], P(('dp', 'fsdp'))
- grad_tokens: float32 [32768, 768], P(('dp', 'fsdp'))
- grad_first_gain: float32 [768], P('fsdp')
- grad_first_shift: float32 [768], P('fsdp')
- grad_query_weight: float32 [768, 768], P('fsdp')
- grad_query_bias: float32 [768], P('fsdp')
- grad_key_weight: float32 [768, 768], P('fsdp')
- grad_value_weight: float32 [768, 768], P('fsdp')
- grad_value_bias: float32 [768], P('fsdp')
- grad_out_weight: float32 [768, 768], P('fsdp')
- grad_out_bias: float32 [768], P('fsdp')
- grad_second_gain: float32 [768], P('fsdp')
- grad_second_shift: float32 [768], P('fsdp')
- grad_up_weight: float32 [768, 3072], P('fsdp')
- grad_up_bias: float32 [3072], P('fsdp')
- grad_down_weight: float32 [3072, 768], P('fsdp')
- grad_down_bias: float32 [768], P('fsdp')
Inputs may be any that keep to these rules, and one draw needn't show every extreme that they name: `image_counts`: row b holds s, the count of 197-row images, and l, the count of 325-row images, of the b-th block of 1024 rows, with 197 s + 325 l <= 1024. In every draw some block holds 3 large images and some other block 5 small ones and no large one.
All inputs are finite; a program needn't handle non-finite values.
Results may differ from a plain program's by a relative error of at most 0.02.
Values may be sent and summed in bfloat16 or wider, within the bound.
A program may use at most 256 MiB of HBM per device.

v0:
```python
import jax
import jax.numpy as jnp
from jax import lax
from jax.sharding import PartitionSpec as P

HEADS = 12
SMALL_ROWS = 197
LARGE_ROWS = 325
QBLOCK = 512


EPS = 1e-06


def layer_norm(values, gain_vec, shift_vec):
    row_mean = jnp.mean(values, axis=-1, keepdims=True)
    centred = values - row_mean
    row_var = jnp.mean(centred * centred, axis=-1, keepdims=True)
    return centred * lax.rsqrt(row_var + EPS) * gain_vec + shift_vec


def gelu_exact(pre_gelu):
    return jax.nn.gelu(pre_gelu, approximate=False)


def image_ids(count_row, row_total):
    places = lax.iota(jnp.int32, row_total)
    small_count = count_row[0]
    large_count = count_row[1]
    offset = small_count * SMALL_ROWS
    live_rows = places < offset + large_count * LARGE_ROWS
    image_of = jnp.where(
        places < offset,
        places // SMALL_ROWS,
        jnp.where(live_rows, small_count + (places - offset) // LARGE_ROWS, -1),
    )
    return (image_of, live_rows)


def product(left, right):
    return jnp.dot(left, right, preferred_element_type=jnp.float32)


def product_t(left, right):
    return lax.dot_general(
        left, right, (((0,), (0,)), ((), ())), preferred_element_type=jnp.float32
    )


def back_right(left, right):
    return lax.dot_general(
        left, right, (((1,), (1,)), ((), ())), preferred_element_type=jnp.float32
    )


def column_sum(values):
    return jnp.sum(values.astype(jnp.float32), axis=0)


def on_device(
    tokens,
    image_counts,
    cotangent,
    first_gain,
    first_shift,
    query_weight,
    query_bias,
    key_weight,
    value_weight,
    value_bias,
    out_weight,
    out_bias,
    second_gain,
    second_shift,
    up_weight,
    up_bias,
    down_weight,
    down_bias,
):
    row_total = tokens.shape[0]
    feat_width = tokens.shape[1]
    head_size = feat_width // HEADS
    score_scale = head_size ** (-0.5)
    query_block = min(QBLOCK, row_total)
    block_count = row_total // query_block
    image_of, live_rows = image_ids(image_counts[0], row_total)
    live_col = live_rows[:, None]
    (
        gain_one,
        shift_one,
        query_full,
        qbias_full,
        key_full,
        value_full,
        vbias_full,
        out_full,
        obias_full,
    ) = (
        lax.all_gather(first_gain, "fsdp", axis=0, tiled=True),
        lax.all_gather(first_shift, "fsdp", axis=0, tiled=True),
        lax.all_gather(query_weight, "fsdp", axis=0, tiled=True),
        lax.all_gather(query_bias, "fsdp", axis=0, tiled=True),
        lax.all_gather(key_weight, "fsdp", axis=0, tiled=True),
        lax.all_gather(value_weight, "fsdp", axis=0, tiled=True),
        lax.all_gather(value_bias, "fsdp", axis=0, tiled=True),
        lax.all_gather(out_weight, "fsdp", axis=0, tiled=True),
        lax.all_gather(out_bias, "fsdp", axis=0, tiled=True),
    )
    inputs = tokens.astype(jnp.float32)
    normed_one, norm_one_back = jax.vjp(
        layer_norm, inputs, gain_one.astype(jnp.float32), shift_one.astype(jnp.float32)
    )
    first_in = normed_one.astype(jnp.bfloat16)
    query_rows = (product(first_in, query_full) + qbias_full.astype(jnp.float32)).astype(
        jnp.bfloat16
    )
    key_rows = product(first_in, key_full).astype(jnp.bfloat16)
    value_rows = (product(first_in, value_full) + vbias_full.astype(jnp.float32)).astype(
        jnp.bfloat16
    )
    query_h = query_rows.reshape(row_total, HEADS, head_size)
    key_h = key_rows.reshape(row_total, HEADS, head_size)
    value_h = value_rows.reshape(row_total, HEADS, head_size)
    starts = jnp.arange(block_count, dtype=jnp.int32) * query_block

    def block_scores(blk_start):
        query_blk = lax.dynamic_slice_in_dim(query_h, blk_start, query_block, 0)
        image_blk = lax.dynamic_slice_in_dim(image_of, blk_start, query_block, 0)
        allowed = image_blk[:, None] == image_of[None, :]
        scores = (
            jnp.einsum("qhd,khd->hqk", query_blk, key_h, preferred_element_type=jnp.float32)
            * score_scale
        )
        return (query_blk, jnp.where(allowed[None], scores, -1e30))

    def attend(blk_start):
        query_blk, scores = block_scores(blk_start)
        row_max = jnp.max(scores, axis=-1, keepdims=True)
        exp_terms = jnp.exp(scores - row_max)
        summed = jnp.sum(exp_terms, axis=-1, keepdims=True)
        attn_probs = (exp_terms / summed).astype(jnp.bfloat16)
        mixed_blk = jnp.einsum(
            "hqk,khd->qhd", attn_probs, value_h, preferred_element_type=jnp.float32
        )
        return (
            mixed_blk.astype(jnp.bfloat16).reshape(query_block, feat_width),
            (row_max + jnp.log(summed))[..., 0],
        )

    mixed_blocks, lse_blocks = lax.map(attend, starts)
    attn_mixed = mixed_blocks.reshape(row_total, feat_width)
    residual = inputs + (product(attn_mixed, out_full) + obias_full.astype(jnp.float32))
    gain_two, shift_two, up_full, ubias_full, down_full, dbias_full = (
        lax.all_gather(second_gain, "fsdp", axis=0, tiled=True),
        lax.all_gather(second_shift, "fsdp", axis=0, tiled=True),
        lax.all_gather(up_weight, "fsdp", axis=0, tiled=True),
        lax.all_gather(up_bias, "fsdp", axis=0, tiled=True),
        lax.all_gather(down_weight, "fsdp", axis=0, tiled=True),
        lax.all_gather(down_bias, "fsdp", axis=0, tiled=True),
    )
    normed_two, norm_two_back = jax.vjp(
        layer_norm, residual, gain_two.astype(jnp.float32), shift_two.astype(jnp.float32)
    )
    second_in = normed_two.astype(jnp.bfloat16)
    pre_gelu = product(second_in, up_full) + ubias_full.astype(jnp.float32)
    activated, gelu_back = jax.vjp(gelu_exact, pre_gelu)
    hidden = activated.astype(jnp.bfloat16)
    result = residual + (product(hidden, down_full) + dbias_full.astype(jnp.float32))
    layer_out = jnp.where(live_col, result, 0.0).astype(jnp.bfloat16)
    up_use, down_use = (
        lax.all_gather(up_weight, "fsdp", axis=0, tiled=True),
        lax.all_gather(down_weight, "fsdp", axis=0, tiled=True),
    )
    query_use, key_use, value_use, out_use = (
        lax.all_gather(query_weight, "fsdp", axis=0, tiled=True),
        lax.all_gather(key_weight, "fsdp", axis=0, tiled=True),
        lax.all_gather(value_weight, "fsdp", axis=0, tiled=True),
        lax.all_gather(out_weight, "fsdp", axis=0, tiled=True),
    )
    grad_out = jnp.where(live_col, cotangent.astype(jnp.float32), 0.0)
    grad_branch = grad_out.astype(jnp.bfloat16)
    grad_down_bias = column_sum(grad_branch)
    grad_down_weight = product_t(hidden, grad_branch)
    grad_hidden = back_right(grad_branch, down_use)
    grad_inner = gelu_back(grad_hidden)[0].astype(jnp.bfloat16)
    grad_up_bias = column_sum(grad_inner)
    grad_up_weight = product_t(second_in, grad_inner)
    grad_second = back_right(grad_inner, up_use)
    grad_after_ln, grad_second_gain, grad_second_shift = norm_two_back(grad_second)
    grad_residual = grad_out + grad_after_ln
    grad_attn = grad_residual.astype(jnp.bfloat16)
    grad_out_bias = column_sum(grad_attn)
    grad_out_weight = product_t(attn_mixed, grad_attn)
    grad_mixed = back_right(grad_attn, out_use).astype(jnp.bfloat16)
    grad_mixed_h = grad_mixed.reshape(row_total, HEADS, head_size)

    def attend_back(carried, block_inputs):
        key_grad, value_grad = carried
        blk_start, lse_blk = block_inputs
        query_blk, scores = block_scores(blk_start)
        grad_blk = lax.dynamic_slice_in_dim(grad_mixed_h, blk_start, query_block, 0)
        attn_probs = jnp.exp(scores - lse_blk[..., None])
        probs_low = attn_probs.astype(jnp.bfloat16)
        grad_probs = jnp.einsum(
            "qhd,khd->hqk", grad_blk, value_h, preferred_element_type=jnp.float32
        )
        value_grad = value_grad + jnp.einsum(
            "hqk,qhd->khd", probs_low, grad_blk, preferred_element_type=jnp.float32
        )
        centre = jnp.sum(attn_probs * grad_probs, axis=-1, keepdims=True)
        grad_scores = (attn_probs * (grad_probs - centre)).astype(jnp.bfloat16)
        query_grad = (
            jnp.einsum("hqk,khd->qhd", grad_scores, key_h, preferred_element_type=jnp.float32)
            * score_scale
        )
        key_grad = (
            key_grad
            + jnp.einsum("hqk,qhd->khd", grad_scores, query_blk, preferred_element_type=jnp.float32)
            * score_scale
        )
        return ((key_grad, value_grad), query_grad)

    zero_heads = jnp.zeros((row_total, HEADS, head_size), jnp.float32)
    (key_sum, value_sum), query_parts = lax.scan(
        attend_back, (zero_heads, zero_heads), (starts, lse_blocks)
    )
    grad_query = query_parts.reshape(row_total, feat_width).astype(jnp.bfloat16)
    grad_key = key_sum.reshape(row_total, feat_width).astype(jnp.bfloat16)
    grad_value = value_sum.reshape(row_total, feat_width).astype(jnp.bfloat16)
    grad_query_bias = column_sum(grad_query)
    grad_value_bias = column_sum(grad_value)
    grad_query_weight = product_t(first_in, grad_query)
    grad_key_weight = product_t(first_in, grad_key)
    grad_value_weight = product_t(first_in, grad_value)
    grad_first = (
        back_right(grad_query, query_use)
        + back_right(grad_key, key_use)
        + back_right(grad_value, value_use)
    )
    grad_in_ln, grad_first_gain, grad_first_shift = norm_one_back(grad_first)
    grad_tokens = grad_residual + grad_in_ln
    owned_part = (
        lax.psum_scatter(
            grad_first_gain.astype(jnp.bfloat16), "fsdp", scatter_dimension=0, tiled=True
        ).astype(jnp.float32),
        lax.psum_scatter(
            grad_first_shift.astype(jnp.bfloat16), "fsdp", scatter_dimension=0, tiled=True
        ).astype(jnp.float32),
        lax.psum_scatter(
            grad_query_weight.astype(jnp.bfloat16), "fsdp", scatter_dimension=0, tiled=True
        ).astype(jnp.float32),
        lax.psum_scatter(
            grad_query_bias.astype(jnp.bfloat16), "fsdp", scatter_dimension=0, tiled=True
        ).astype(jnp.float32),
        lax.psum_scatter(
            grad_key_weight.astype(jnp.bfloat16), "fsdp", scatter_dimension=0, tiled=True
        ).astype(jnp.float32),
        lax.psum_scatter(
            grad_value_weight.astype(jnp.bfloat16), "fsdp", scatter_dimension=0, tiled=True
        ).astype(jnp.float32),
        lax.psum_scatter(
            grad_value_bias.astype(jnp.bfloat16), "fsdp", scatter_dimension=0, tiled=True
        ).astype(jnp.float32),
        lax.psum_scatter(
            grad_out_weight.astype(jnp.bfloat16), "fsdp", scatter_dimension=0, tiled=True
        ).astype(jnp.float32),
        lax.psum_scatter(
            grad_out_bias.astype(jnp.bfloat16), "fsdp", scatter_dimension=0, tiled=True
        ).astype(jnp.float32),
        lax.psum_scatter(
            grad_second_gain.astype(jnp.bfloat16), "fsdp", scatter_dimension=0, tiled=True
        ).astype(jnp.float32),
        lax.psum_scatter(
            grad_second_shift.astype(jnp.bfloat16), "fsdp", scatter_dimension=0, tiled=True
        ).astype(jnp.float32),
        lax.psum_scatter(
            grad_up_weight.astype(jnp.bfloat16), "fsdp", scatter_dimension=0, tiled=True
        ).astype(jnp.float32),
        lax.psum_scatter(
            grad_up_bias.astype(jnp.bfloat16), "fsdp", scatter_dimension=0, tiled=True
        ).astype(jnp.float32),
        lax.psum_scatter(
            grad_down_weight.astype(jnp.bfloat16), "fsdp", scatter_dimension=0, tiled=True
        ).astype(jnp.float32),
        lax.psum_scatter(
            grad_down_bias.astype(jnp.bfloat16), "fsdp", scatter_dimension=0, tiled=True
        ).astype(jnp.float32),
    )
    summed_grads = (
        lax.psum(owned_part[0].astype(jnp.bfloat16), "dp").astype(jnp.float32),
        lax.psum(owned_part[1].astype(jnp.bfloat16), "dp").astype(jnp.float32),
        lax.psum(owned_part[2].astype(jnp.bfloat16), "dp").astype(jnp.float32),
        lax.psum(owned_part[3].astype(jnp.bfloat16), "dp").astype(jnp.float32),
        lax.psum(owned_part[4].astype(jnp.bfloat16), "dp").astype(jnp.float32),
        lax.psum(owned_part[5].astype(jnp.bfloat16), "dp").astype(jnp.float32),
        lax.psum(owned_part[6].astype(jnp.bfloat16), "dp").astype(jnp.float32),
        lax.psum(owned_part[7].astype(jnp.bfloat16), "dp").astype(jnp.float32),
        lax.psum(owned_part[8].astype(jnp.bfloat16), "dp").astype(jnp.float32),
        lax.psum(owned_part[9].astype(jnp.bfloat16), "dp").astype(jnp.float32),
        lax.psum(owned_part[10].astype(jnp.bfloat16), "dp").astype(jnp.float32),
        lax.psum(owned_part[11].astype(jnp.bfloat16), "dp").astype(jnp.float32),
        lax.psum(owned_part[12].astype(jnp.bfloat16), "dp").astype(jnp.float32),
        lax.psum(owned_part[13].astype(jnp.bfloat16), "dp").astype(jnp.float32),
        lax.psum(owned_part[14].astype(jnp.bfloat16), "dp").astype(jnp.float32),
    )
    return (
        layer_out,
        grad_tokens,
        summed_grads[0],
        summed_grads[1],
        summed_grads[2],
        summed_grads[3],
        summed_grads[4],
        summed_grads[5],
        summed_grads[6],
        summed_grads[7],
        summed_grads[8],
        summed_grads[9],
        summed_grads[10],
        summed_grads[11],
        summed_grads[12],
        summed_grads[13],
        summed_grads[14],
    )


def solution(mesh):
    placed = (
        P(("dp", "fsdp"), None),
        P(("dp", "fsdp"), None),
        P(("dp", "fsdp"), None),
        P("fsdp"),
        P("fsdp"),
        P("fsdp", None),
        P("fsdp"),
        P("fsdp", None),
        P("fsdp", None),
        P("fsdp"),
        P("fsdp", None),
        P("fsdp"),
        P("fsdp"),
        P("fsdp"),
        P("fsdp", None),
        P("fsdp"),
        P("fsdp", None),
        P("fsdp"),
    )
    return jax.shard_map(
        on_device,
        mesh=mesh,
        in_specs=placed,
        out_specs=(
            P(("dp", "fsdp"), None),
            P(("dp", "fsdp"), None),
            P("fsdp"),
            P("fsdp"),
            P("fsdp", None),
            P("fsdp"),
            P("fsdp", None),
            P("fsdp", None),
            P("fsdp"),
            P("fsdp", None),
            P("fsdp"),
            P("fsdp"),
            P("fsdp"),
            P("fsdp", None),
            P("fsdp"),
            P("fsdp", None),
            P("fsdp"),
        ),
        check_vma=False,
    )
```

profile of v0, /device:TPU:0, one launch (start us, length us, event | category | flops | bytes accessed | tf_op | source)
XLA Modules:
  0.0 904.1 jit_solution(8462274462983237279)
XLA Ops:
  24.5 63.2 %all-reduce.19 = (bf16[768]{0:T(1024)(128)(2,1)S(1)}, bf16[768]{0:T(1024)(128)(2,1)S(1)}, bf16[768]{0:T(1024)(128)(2,1)S(1)}, bf16[768]{0:T(1024)(128)(2,1)S(1)}...) all-reduce(bf16[768]{0:T(1024)(128)(2,1)S(1)} %dynamic-update-slice, ...), channel_id=1, replica_groups=mesh['dp'=2,'fsdp'=16] {'fsdp'}, use_global_device_ids=true, to_apply=%add.2 | all-reduce | flops 8448 | bytes 33792
  101.3 29.5 %all-gather.7.cloned.1.call-done = bf16[768,768]{1,0:T(8,128)(2,1)} async-done(((bf16[48,768]{1,0:T(8,128)(2,1)}), bf16[768,768]{1,0:T(8,128)(2,1)}) %all-gather.7.cloned.1.call-update) | async-done | bytes 1179664 | tf_op jit(solution)/shard_map/all_gather | solution.py:101
  134.2 85.6 %while.27 = (s32[]{:T(128)}, bf16[2,512,768]{2,1,0:T(8,128)(2,1)}, f32[2,12,512]{2,1,0:T(8,128)S(1)}, s32[2]{0:T(128)S(1)}, s32[1024]{0:T(1024)S(1)}, /*index=5*...) while((s32[]{:T(128)}, bf16[2,512,768]{2,1,0:T(8,128)(2,1)}, ...), condition=%wide.region_5.6_spmd, body=%wide.region_2.5_spmd.sunk | while | flops 1687021568 | bytes 192645360 | solution.py:150
  137.7 10.9 %fusion.131 = (f32[12,512]{1,0:T(8,128)S(1)}, f32[12,512,1024]{2,1,0:T(8,128)}) fusion(pred[512,1024]{1,0:T(8,128)(4,1)S(1)} %broadcast_compare_fusion.4, bf16[1024,12,64]{0,2,1:T(8,128)(2,1)S(1)} %get-tuple-element.465, bf16[1024,12,64]{0,2,1:T(8,128)(2,1)S(1)} %get-tuple-element.464, s32[]{:T(128)S(6)} %select_n.110), kind=kOutput, calls=%fused_computation.3.clone.1 | convolution fusion | flops 824174592 | bytes 28073988 | tf_op jit(solution)/shard_map/while/body/eval_jaxpr/qhd,khd->hqk/dot_general | solution.py:131
  148.5 12.4 %fusion.132 = f32[12,512]{1,0:T(8,128)S(1)} fusion(f32[12,512,1024]{2,1,0:T(8,128)} %get-tuple-element.422, f32[12,512]{1,0:T(8,128)S(1)} %get-tuple-element.423, pred[512,1024]{1,0:T(8,128)(4,1)S(1)} %broadcast_compare_fusion.4), kind=kLoop, calls=%fused_computation.4.clone.1 | loop fusion | flops 25159680 | bytes 25739264 | tf_op jit(solution)/shard_map/while/body/eval_jaxpr/reduce_sum | solution.py:140
  180.0 10.9 %fusion.131 = (f32[12,512]{1,0:T(8,128)S(1)}, f32[12,512,1024]{2,1,0:T(8,128)}) fusion(pred[512,1024]{1,0:T(8,128)(4,1)S(1)} %broadcast_compare_fusion.4, bf16[1024,12,64]{0,2,1:T(8,128)(2,1)S(1)} %get-tuple-element.465, bf16[1024,12,64]{0,2,1:T(8,128)(2,1)S(1)} %get-tuple-element.464, s32[]{:T(128)S(6)} %select_n.110), kind=kOutput, calls=%fused_computation.3.clone.1 | convolution fusion | flops 824174592 | bytes 28073988 | tf_op jit(solution)/shard_map/while/body/eval_jaxpr/qhd,khd->hqk/dot_general | solution.py:131
  190.9 12.7 %fusion.132 = f32[12,512]{1,0:T(8,128)S(1)} fusion(f32[12,512,1024]{2,1,0:T(8,128)} %get-tuple-element.422, f32[12,512]{1,0:T(8,128)S(1)} %get-tuple-element.423, pred[512,1024]{1,0:T(8,128)(4,1)S(1)} %broadcast_compare_fusion.4), kind=kLoop, calls=%fused_computation.4.clone.1 | loop fusion | flops 25159680 | bytes 25739264 | tf_op jit(solution)/shard_map/while/body/eval_jaxpr/reduce_sum | solution.py:140
  226.0 38.0 %multiply_convert_fusion.1 = (bf16[1024,3072]{1,0:T(8,128)(2,1)}, f32[1024,3072]{1,0:T(8,128)}, f32[1024,3072]{1,0:T(8,128)}) fusion(f32[3072]{0:T(1024)S(1)} %copy-done.41, bf16[768,3072]{1,0:T(8,128)(2,1)} %all-gather.15.cloned.1.call-done, f32[1024,768]{0,1:T(8,128)} %copy-done.9, f32[768]{0:T(1024)S(1)} %copy-done.46, f32[768]{0:T(1024)S(1)} %copy-done.37, ...), kind=kOutput, calls=%fused_computation.41 | convolution fusion | flops 5043388416 | bytes 39348224 | tf_op jit(solution)/shard_map/dot_general | solution.py:41
  264.0 14.7 %all-gather.17.cloned.1.call-done = bf16[3072,768]{1,0:T(8,128)(2,1)} async-done(((bf16[192,768]{1,0:T(8,128)(2,1)}), bf16[3072,768]{1,0:T(8,128)(2,1)}) %all-gather.17.cloned.1.call-update) | async-done | bytes 4718608 | tf_op jit(solution)/shard_map/all_gather | solution.py:158
  278.7 19.2 %fusion.78 = (bf16[3072]{0:T(1024)(128)(2,1)}, bf16[1024,3072]{1,0:T(8,128)(2,1)}) fusion(f32[1024,3072]{1,0:T(8,128)} %get-tuple-element.295, bf16[3072,768]{1,0:T(8,128)(2,1)} %all-gather.17.cloned.1.call-done, bf16[1024,768]{0,1:T(8,128)(2,1)} %copy.60, pred[1024]{0:T(1024)(128)(4,1)S(1)} %copy-done.51, f32[1024,3072]{1,0:T(8,128)} %get-tuple-element.307, ...), kind=kOutput, calls=%fused_computation.133 | convolution fusion | flops 4884526080 | bytes 37768192 | tf_op jit(solution)/shard_map/dot_general | solution.py:51
  297.8 10.3 %fusion.77 = (bf16[768]{0:T(1024)(128)(2,1)}, f32[1024,768]{1,0:T(8,128)}) fusion(bf16[1024,3072]{1,0:T(8,128)(2,1)} %get-tuple-element.312, bf16[768,3072]{1,0:T(8,128)(2,1)} %all-gather.15.cloned.1.call-done), kind=kOutput, calls=%fused_computation.132 | convolution fusion | flops 4832623616 | bytes 14157312 | tf_op jit(solution)/shard_map/dot_general | solution.py:51
  327.1 177.8 %while.28 = (s32[]{:T(128)}, f32[1024,12,64]{0,2,1:T(8,128)}, f32[1024,12,64]{0,2,1:T(8,128)}, bf16[2,512,12,64]{1,3,2,0:T(8,128)(2,1)}, s32[2]{0:T(128)S(1)}, /...) while((s32[]{:T(128)}, f32[1024,12,64]{0,2,1:T(8,128)}, ...), condition=%wide.region_12.13_spmd.clone, body=%wide.region_10.12_spmd.clone.sunk | while | flops 4125747200 | bytes 231926080 | solution.py:224
  330.7 13.3 %fusion.143 = f32[12,512,1024]{2,1,0:T(8,128)} fusion(bf16[1024,12,64]{0,2,1:T(8,128)(2,1)S(1)} %get-tuple-element.505, bf16[1024,12,64]{0,2,1:T(8,128)(2,1)} %copy-done.2, s32[]{:T(128)S(6)} %select_n.114), kind=kOutput, calls=%fused_computation.29.clone.1 | convolution fusion | flops 805306368 | bytes 27525124 | tf_op jit(solution)/shard_map/while/body/eval_jaxpr/qhd,khd->hqk/dot_general | solution.py:131
  344.0 13.7 %bitcast_add_fusion.5 = f32[1024,12,64]{0,2,1:T(8,128)} fusion(f32[1024,12,64]{0,2,1:T(8,128)} %get-tuple-element.486, f32[12,512,1024]{2,1,0:T(8,128)} %fusion.143, f32[12,512]{1,0:T(8,128)S(1)} %dynamic-slice_bitcast_fusion.2, pred[512,1024]{1,0:T(8,128)(4,1)S(1)} %broadcast_compare_fusion.5, pred[]{:T(512)S(6)} %compare.3, ...), kind=kOutput, calls=%fused_computation.21.clone.1 | convolution fusion | flops 832045056 | bytes 32800772 | tf_op jit(solution)/shard_map/while/body/eval_jaxpr/hqk,qhd->khd/dot_general | solution.py:207
  357.7 18.3 %multiply_reduce_fusion.5 = (f32[12,512]{1,0:T(8,128)S(1)}, f32[12,512,1024]{2,1,0:T(8,128)}) fusion(f32[12,512,1024]{2,1,0:T(8,128)} %fusion.143, f32[12,512]{1,0:T(8,128)S(1)} %dynamic-slice_bitcast_fusion.2, pred[512,1024]{1,0:T(8,128)(4,1)S(1)} %broadcast_compare_fusion.5, bf16[1024,12,64]{0,2,1:T(8,128)(2,1)} %get-tuple-element.508, ...), kind=kOutput, calls=%fused_computation.16.clone.1 | convolution fusion | flops 836757504 | bytes 53264388 | tf_op jit(solution)/shard_map/while/body/eval_jaxpr/qhd,khd->hqk/dot_general | solution.py:204
  376.0 21.3 %multiply_convert_fusion.3 = bf16[12,512,1024]{2,1,0:T(8,128)(2,1)} fusion(f32[12,512,1024]{2,1,0:T(8,128)} %get-tuple-element.435, f32[12,512,1024]{2,1,0:T(8,128)} %fusion.143, f32[12,512]{1,0:T(8,128)S(1)} %get-tuple-element.436, f32[12,512]{1,0:T(8,128)S(1)} %dynamic-slice_bitcast_fusion.2, pred[512,1024]{1,0:T(8,128)(4,1)S(1)} %broadcast_compare_fusion.5), kind=kLoop, calls=%fused_computation.15.clone.1 | loop fusion | flops 37748736 | bytes 63488000 | tf_op jit(solution)/shard_map/while/body/eval_jaxpr/convert_element_type | solution.py:211
  397.2 9.5 %bitcast_dynamic-update-slice_fusion.5 = bf16[2,512,12,64]{1,3,2,0:T(8,128)(2,1)} fusion(bf16[2,512,12,64]{1,3,2,0:T(8,128)(2,1)} %get-tuple-element.487, s32[]{:T(128)S(6)} %copy.108, bf16[12,512,1024]{2,1,0:T(8,128)(2,1)} %multiply_convert_fusion.3, bf16[1024,12,64]{0,2,1:T(8,128)(2,1)S(1)} %get-tuple-element.505), kind=kOutput, calls=%fused_computation.23.clone.1 | convolution fusion | flops 805699584 | bytes 15728644 | tf_op jit(solution)/shard_map/while/body/eval_jaxpr/hqk,khd->qhd/dot_general | solution.py:213
  406.7 8.6 bitcast_add_fusion.4
  418.4 13.2 %fusion.143 = f32[12,512,1024]{2,1,0:T(8,128)} fusion(bf16[1024,12,64]{0,2,1:T(8,128)(2,1)S(1)} %get-tuple-element.505, bf16[1024,12,64]{0,2,1:T(8,128)(2,1)} %copy-done.2, s32[]{:T(128)S(6)} %select_n.114), kind=kOutput, calls=%fused_computation.29.clone.1 | convolution fusion | flops 805306368 | bytes 27525124 | tf_op jit(solution)/shard_map/while/body/eval_jaxpr/qhd,khd->hqk/dot_general | solution.py:131
  431.6 14.6 %bitcast_add_fusion.5 = f32[1024,12,64]{0,2,1:T(8,128)} fusion(f32[1024,12,64]{0,2,1:T(8,128)} %get-tuple-element.486, f32[12,512,1024]{2,1,0:T(8,128)} %fusion.143, f32[12,512]{1,0:T(8,128)S(1)} %dynamic-slice_bitcast_fusion.2, pred[512,1024]{1,0:T(8,128)(4,1)S(1)} %broadcast_compare_fusion.5, pred[]{:T(512)S(6)} %compare.3, ...), kind=kOutput, calls=%fused_computation.21.clone.1 | convolution fusion | flops 832045056 | bytes 32800772 | tf_op jit(solution)/shard_map/while/body/eval_jaxpr/hqk,qhd->khd/dot_general | solution.py:207
  446.2 18.2 %multiply_reduce_fusion.5 = (f32[12,512]{1,0:T(8,128)S(1)}, f32[12,512,1024]{2,1,0:T(8,128)}) fusion(f32[12,512,1024]{2,1,0:T(8,128)} %fusion.143, f32[12,512]{1,0:T(8,128)S(1)} %dynamic-slice_bitcast_fusion.2, pred[512,1024]{1,0:T(8,128)(4,1)S(1)} %broadcast_compare_fusion.5, bf16[1024,12,64]{0,2,1:T(8,128)(2,1)} %get-tuple-element.508, ...), kind=kOutput, calls=%fused_computation.16.clone.1 | convolution fusion | flops 836757504 | bytes 53264388 | tf_op jit(solution)/shard_map/while/body/eval_jaxpr/qhd,khd->hqk/dot_general | solution.py:204
  464.5 21.2 %multiply_convert_fusion.3 = bf16[12,512,1024]{2,1,0:T(8,128)(2,1)} fusion(f32[12,512,1024]{2,1,0:T(8,128)} %get-tuple-element.435, f32[12,512,1024]{2,1,0:T(8,128)} %fusion.143, f32[12,512]{1,0:T(8,128)S(1)} %get-tuple-element.436, f32[12,512]{1,0:T(8,128)S(1)} %dynamic-slice_bitcast_fusion.2, pred[512,1024]{1,0:T(8,128)(4,1)S(1)} %broadcast_compare_fusion.5), kind=kLoop, calls=%fused_computation.15.clone.1 | loop fusion | flops 37748736 | bytes 63488000 | tf_op jit(solution)/shard_map/while/body/eval_jaxpr/convert_element_type | solution.py:211
  485.7 9.5 %bitcast_dynamic-update-slice_fusion.5 = bf16[2,512,12,64]{1,3,2,0:T(8,128)(2,1)} fusion(bf16[2,512,12,64]{1,3,2,0:T(8,128)(2,1)} %get-tuple-element.487, s32[]{:T(128)S(6)} %copy.108, bf16[12,512,1024]{2,1,0:T(8,128)(2,1)} %multiply_convert_fusion.3, bf16[1024,12,64]{0,2,1:T(8,128)(2,1)S(1)} %get-tuple-element.505), kind=kOutput, calls=%fused_computation.23.clone.1 | convolution fusion | flops 805699584 | bytes 15728644 | tf_op jit(solution)/shard_map/while/body/eval_jaxpr/hqk,khd->qhd/dot_general | solution.py:213
  495.2 9.5 %bitcast_add_fusion.4 = f32[1024,12,64]{0,2,1:T(8,128)} fusion(f32[1024,12,64]{0,2,1:T(8,128)} %get-tuple-element.485, bf16[12,512,1024]{2,1,0:T(8,128)(2,1)} %multiply_convert_fusion.3, pred[]{:T(512)S(6)} %compare.3, bf16[1024,12,64]{0,2,1:T(8,128)(2,1)S(1)} %copy-done.3, s32[]{:T(128)S(6)} %select_n.114), kind=kOutput, calls=%fused_computation.22.clone.1 | convolution fusion | flops 807665664 | bytes 19660804 | tf_op jit(solution)/shard_map/while/body/eval_jaxpr/hqk,qhd->khd/dot_general | solution.py:218
  523.5 10.0 %convolution_convert_fusion.1 = bf16[768,3072]{1,0:T(8,128)(2,1)} fusion(bf16[1024,3072]{1,0:T(8,128)(2,1)} %get-tuple-element.312, f32[1024,768]{0,1:T(8,128)} %copy-done.9, f32[768]{0:T(1024)S(1)} %copy-done.47, f32[768]{0:T(1024)S(1)} %copy-done.38, f32[1024]{0:T(1024)S(1)} %copy-done.40, f32[1024]{0:T(1024)S(1)} %copy-done.30), kind=kOutput, calls=%fused_computation.56 | convolution fusion | flops 4838129664 | bytes 14170112 | tf_op jit(solution)/shard_map/dot_general | solution.py:45
  534.8 9.8 %convolution_convert_fusion = bf16[3072,768]{1,0:T(8,128)(2,1)} fusion(bf16[1024,3072]{1,0:T(8,128)(2,1)} %get-tuple-element.294, bf16[1024,768]{0,1:T(8,128)(2,1)S(1)} %copy-done.15, pred[1024]{0:T(1024)(128)(4,1)S(1)} %copy-done.52), kind=kOutput, calls=%fused_computation.55 | convolution fusion | flops 4836556800 | bytes 12583936 | tf_op jit(solution)/shard_map/dot_general | solution.py:45
  558.4 59.5 %all-reduce.18 = (bf16[768]{0:T(1024)(128)(2,1)S(1)}, bf16[768]{0:T(1024)(128)(2,1)S(1)}, bf16[768]{0:T(1024)(128)(2,1)S(1)}, bf16[768]{0:T(1024)(128)(2,1)S(1)}...) all-reduce(bf16[768]{0:T(1024)(128)(2,1)S(1)} %dynamic-update-slice, ...), channel_id=1, replica_groups=mesh['dp'=2,'fsdp'=16] {'fsdp'}, use_global_device_ids=true, to_apply=%add.8 | all-reduce | flops 9984 | bytes 39936
  617.9 12.3 %reduce-scatter.9.cloned.1.call-done = bf16[48,768]{1,0:T(8,128)(2,1)} async-done(((bf16[768,768]{1,0:T(8,128)(2,1)}), bf16[48,768]{1,0:T(8,128)(2,1)}) %reduce-scatter.9.cloned.1.call-update) | async-done | bytes 73744 | tf_op jit(solution)/shard_map/reduce_scatter | solution.py:255
  630.3 60.5 %reduce-scatter.11.cloned.1.call-done = bf16[48,768]{1,0:T(8,128)(2,1)} async-done(((bf16[768,768]{1,0:T(8,128)(2,1)}), bf16[48,768]{1,0:T(8,128)(2,1)}) %reduce-scatter.11.cloned.1.call-update) | async-done | bytes 73744 | tf_op jit(solution)/shard_map/reduce_scatter | solution.py:258
  690.8 78.4 %reduce-scatter.15.cloned.1.call-done = bf16[48,3072]{1,0:T(8,128)(2,1)} async-done(((bf16[768,3072]{1,0:T(8,128)(2,1)}), bf16[48,3072]{1,0:T(8,128)(2,1)}) %reduce-scatter.15.cloned.1.call-update) | async-done | bytes 294928 | tf_op jit(solution)/shard_map/reduce_scatter | solution.py:276
  769.3 78.8 %reduce-scatter.17.cloned.1.call-done = bf16[192,768]{1,0:T(8,128)(2,1)} async-done(((bf16[3072,768]{1,0:T(8,128)(2,1)}), bf16[192,768]{1,0:T(8,128)(2,1)}) %reduce-scatter.17.cloned.1.call-update) | async-done | bytes 294928 | tf_op jit(solution)/shard_map/reduce_scatter | solution.py:282
  848.1 10.0 %select_convert_fusion = bf16[1024,768]{0,1:T(8,128)(2,1)} fusion(f32[1024,768]{0,1:T(8,128)} %copy-done.9, bf16[1024,3072]{1,0:T(8,128)(2,1)} %get-tuple-element.294, bf16[3072,768]{1,0:T(8,128)(2,1)} %all-gather.17.cloned.1.call-done, f32[768]{0:T(1024)S(1)} %convert_element_type.231, pred[1024]{0:T(1024)(128)(4,1)S(1)} %copy-done.52), kind=kOutput, calls=%fused_computation.80 | convolution fusion | flops 4834983936 | bytes 15732736 | tf_op jit(solution)/shard_map/dot_general | solution.py:41
  (281 shorter events, 164.0 us)
Async XLA Ops:
  7.2 87.2 %all-gather.9.cloned.1.call-start = ((), (), s32[]{:S(2)}) async-start(), calls=%async_computation.7 | async-start | bytes 1253376 | tf_op jit(solution)/shard_map/all_gather | solution.py:103
  7.9 89.4 %all-gather.11.cloned.1.call-start = ((), (), s32[]{:S(2)}) async-start(), calls=%async_computation.8 | async-start | bytes 1253376 | tf_op jit(solution)/shard_map/all_gather | solution.py:104
  8.7 122.2 %all-gather.7.cloned.1.call-start = ((), (), s32[]{:S(2)}) async-start(), calls=%async_computation.6 | async-start | bytes 1253376 | tf_op jit(solution)/shard_map/all_gather | solution.py:101
  9.4 210.4 %all-gather.13.cloned.1.call-start = ((), (), s32[]{:S(2)}) async-start(), calls=%async_computation.9 | async-start | bytes 1253376 | tf_op jit(solution)/shard_map/all_gather | solution.py:106
  10.0 215.9 %all-gather.15.cloned.1.call-start = ((), (), s32[]{:S(2)}) async-start(), calls=%async_computation.10 | async-start | bytes 5013504 | tf_op jit(solution)/shard_map/all_gather | solution.py:156
  10.6 268.1 %all-gather.17.cloned.1.call-start = ((), (), s32[]{:S(2)}) async-start(), calls=%async_computation.11 | async-start | bytes 5013504 | tf_op jit(solution)/shard_map/all_gather | solution.py:158
  11.1 606.8 %reduce-scatter.13.cloned.1.call-start = ((), (), s32[]{:S(2)}) async-start(), calls=%async_computation.15 | async-start | bytes 1253376 | tf_op jit(solution)/shard_map/reduce_scatter | solution.py:264
  87.7 43.1 %copy-start.27 = (f32[768]{0:T(1024)}, f32[768]{0:T(1024)S(1)}, u32[]{:S(2)}) copy-start(f32[768]{0:T(1024)S(1)} %convert_element_type.217) | copy-start | bytes 9220
  87.7 43.1 %copy-start.48 = (f32[768]{0:T(1024)}, f32[768]{0:T(1024)S(1)}, u32[]{:S(2)}) copy-start(f32[768]{0:T(1024)S(1)} %convert_element_type.218) | copy-start | bytes 9220
  92.0 5.3 copy-start.4
  92.2 38.6 %copy-start.25 = (f32[1024]{0:T(1024)}, f32[1024]{0:T(1024)S(1)}, u32[]{:S(2)}) copy-start(f32[1024]{0:T(1024)S(1)} %broadcast_multiply_fusion.1) | copy-start | bytes 12292
  92.7 38.1 %copy-start.31 = (f32[1024]{0:T(1024)}, f32[1024]{0:T(1024)S(1)}, u32[]{:S(2)}) copy-start(f32[1024]{0:T(1024)S(1)} %fusion.57) | copy-start | bytes 12292
  134.2 85.7 %copy-start.50 = (f32[768]{0:T(1024)S(1)}, f32[768]{0:T(1024)}, u32[]{:S(2)}) copy-start(f32[768]{0:T(1024)} %convert_element_type.225) | copy-start | bytes 9220
  137.7 23.3 %copy-start.8 = (bf16[1024,12,64]{0,2,1:T(8,128)(2,1)S(1)}, bf16[1024,12,64]{0,2,1:T(8,128)(2,1)}, u32[]{:S(2)}) copy-start(bf16[1024,12,64]{0,2,1:T(8,128)(2,1)} %get-tuple-element.466) | copy-start | bytes 4718596 | tf_op jit(solution)/shard_map/while
  148.5 15.6 %copy-start = (f32[12,512,1024]{2,1,0:T(8,128)S(1)}, f32[12,512,1024]{2,1,0:T(8,128)}, u32[]{:S(2)}) copy-start(f32[12,512,1024]{2,1,0:T(8,128)} %get-tuple-element.422) | copy-start | bytes 75497472 | tf_op jit(solution)/shard_map/while
  180.0 23.7 %copy-start.8 = (bf16[1024,12,64]{0,2,1:T(8,128)(2,1)S(1)}, bf16[1024,12,64]{0,2,1:T(8,128)(2,1)}, u32[]{:S(2)}) copy-start(bf16[1024,12,64]{0,2,1:T(8,128)(2,1)} %get-tuple-element.466) | copy-start | bytes 4718596 | tf_op jit(solution)/shard_map/while
  190.9 16.1 %copy-start = (f32[12,512,1024]{2,1,0:T(8,128)S(1)}, f32[12,512,1024]{2,1,0:T(8,128)}, u32[]{:S(2)}) copy-start(f32[12,512,1024]{2,1,0:T(8,128)} %get-tuple-element.422) | copy-start | bytes 75497472 | tf_op jit(solution)/shard_map/while
  223.9 92.3 %copy-start.29 = (f32[1024]{0:T(1024)}, f32[1024]{0:T(1024)S(1)}, u32[]{:S(2)}) copy-start(f32[1024]{0:T(1024)S(1)} %broadcast_multiply_fusion) | copy-start | bytes 12292
  225.9 90.3 %copy-start.39 = (f32[1024]{0:T(1024)}, f32[1024]{0:T(1024)S(1)}, u32[]{:S(2)}) copy-start(f32[1024]{0:T(1024)S(1)} %fusion.58) | copy-start | bytes 12292
  225.9 52.8 %copy-start.51 = (pred[1024]{0:T(1024)(128)(4,1)S(1)}, pred[1024]{0:T(1024)(128)(4,1)}, u32[]{:S(2)}) copy-start(pred[1024]{0:T(1024)(128)(4,1)} %iota_compare_fusion.1) | copy-start | bytes 3076
  322.8 295.1 %reduce-scatter.7.cloned.1.call-start = ((), (), s32[]{:S(2)}) async-start(), calls=%async_computation.12 | async-start | bytes 1253376 | tf_op jit(solution)/shard_map/reduce_scatter | solution.py:249
  330.7 13.3 %copy-start.16 = (bf16[1024,12,64]{0,2,1:T(8,128)(2,1)S(1)}, bf16[1024,12,64]{0,2,1:T(8,128)(2,1)}, u32[]{:S(2)}) copy-start(bf16[1024,12,64]{0,2,1:T(8,128)(2,1)} %get-tuple-element.507) | copy-start | bytes 4718596 | tf_op jit(solution)/shard_map/while
  397.2 9.5 %copy-start.3 = (bf16[1024,12,64]{0,2,1:T(8,128)(2,1)S(1)}, bf16[1024,12,64]{0,2,1:T(8,128)(2,1)}, u32[]{:S(2)}) copy-start(bf16[1024,12,64]{0,2,1:T(8,128)(2,1)} %copy-done.2) | copy-start | bytes 4718596 | tf_op jit(solution)/shard_map/while
  418.4 13.2 %copy-start.16 = (bf16[1024,12,64]{0,2,1:T(8,128)(2,1)S(1)}, bf16[1024,12,64]{0,2,1:T(8,128)(2,1)}, u32[]{:S(2)}) copy-start(bf16[1024,12,64]{0,2,1:T(8,128)(2,1)} %get-tuple-element.507) | copy-start | bytes 4718596 | tf_op jit(solution)/shard_map/while
  485.7 9.5 %copy-start.3 = (bf16[1024,12,64]{0,2,1:T(8,128)(2,1)S(1)}, bf16[1024,12,64]{0,2,1:T(8,128)(2,1)}, u32[]{:S(2)}) copy-start(bf16[1024,12,64]{0,2,1:T(8,128)(2,1)} %copy-done.2) | copy-start | bytes 4718596 | tf_op jit(solution)/shard_map/while
  504.9 4.8 copy-start.5
  512.5 117.8 %reduce-scatter.9.cloned.1.call-start = ((), (), s32[]{:S(2)}) async-start(), calls=%async_computation.13 | async-start | bytes 1253376 | tf_op jit(solution)/shard_map/reduce_scatter | solution.py:255
  517.1 173.7 %reduce-scatter.11.cloned.1.call-start = ((), (), s32[]{:S(2)}) async-start(), calls=%async_computation.14 | async-start | bytes 1253376 | tf_op jit(solution)/shard_map/reduce_scatter | solution.py:258
  523.4 245.9 %reduce-scatter.15.cloned.1.call-start = ((), (), s32[]{:S(2)}) async-start(), calls=%async_computation.16 | async-start | bytes 5013504 | tf_op jit(solution)/shard_map/reduce_scatter | solution.py:276
  533.5 314.6 %reduce-scatter.17.cloned.1.call-start = ((), (), s32[]{:S(2)}) async-start(), calls=%async_computation.17 | async-start | bytes 5013504 | tf_op jit(solution)/shard_map/reduce_scatter | solution.py:282
  544.6 342.8 %all-reduce.24.cloned.1.call-start = ((), (), s32[]{:S(2)}) async-start(), calls=%async_computation.18 | async-start | bytes 1769472 | tf_op jit(solution)/shard_map/psum | solution.py:292
  858.2 13.1 %copy-start.36 = (f32[1024]{0:T(1024)S(1)}, f32[1024]{0:T(1024)}, u32[]{:S(2)}) copy-start(f32[1024]{0:T(1024)} %copy-done.35) | copy-start | bytes 12292
  (43 other events, 113.7 us)
Sparse Core Ops, SparseCore 0:
  10.3 41.0 all-gather.8
  53.7 37.5 all-gather.10
  93.5 37.2 all-gather.6
  133.0 37.2 all-gather.12
  172.4 52.2 all-gather.14
  226.8 51.7 all-gather.16
  322.9 56.6 reduce-scatter.12
  512.6 56.8 reduce-scatter.6
  573.1 57.1 reduce-scatter.8
  633.7 57.0 reduce-scatter.10
  694.7 74.5 reduce-scatter.14
  773.5 74.5 reduce-scatter.16
  850.8 36.6 all-reduce.23
where the time goes:
time: 912 us; the launch traced here: 904 us
  matrix products  300 us (33%)
  waiting for transfers between devices  285 us (31%)
  blocking collectives  128 us (14%)
  other arithmetic  107 us (12%)
  local copies, waits for them, and re-layouts  56.2 us (6%)
  between operations  18.8 us (2%)
    unnamed x2, blocking collectives  123 us
    reduce_scatter x1, waiting for transfers between devices, on_device(): lax.psum_scatter(grad_down_weight.astype(jnp.bfloat16), 'fsdp', scatter_d...  78.8 us
    reduce_scatter x1, waiting for transfers between devices, on_device(): lax.psum_scatter(grad_up_weight.astype(jnp.bfloat16), 'fsdp', scatter_dim...  78.4 us
    dot_general x6, matrix products, product(): return jnp.dot(left, right, preferred_element_type=jnp.float32)  62.2 us
    reduce_scatter x1, waiting for transfers between devices, on_device(): lax.psum_scatter(grad_value_weight.astype(jnp.bfloat16), 'fsdp', scatter_...  60.5 us
    dot_general x4, matrix products, block_scores(): jnp.einsum('qhd,khd->hqk', query_blk, key_h, preferred_element_type=jnp.f...  48.3 us
    convert_element_type x2, other arithmetic, attend_back(): grad_scores = (attn_probs * (grad_probs - centre)).astype(jnp.bfloat16)  42.5 us
    dot_general x6, matrix products, back_right(): lax.dot_general(left, right, (((1,), (1,)), ((), ())), preferred_element_...  40.4 us
  transfers between devices with their start and end apart: 13, of which 7 were waited for; matrix products, arithmetic and copies ran while one was open for 44% of the time, Pallas kernels for 0%

commit v1 on v0

v1 whole, which is shorter than its diff:
```python
import functools
import math

import jax
import jax.numpy as jnp
from jax import lax
from jax.experimental import pallas as pl
from jax.experimental.pallas import tpu as pltpu
from jax.sharding import PartitionSpec as P

EPS = 1e-06
NT = (((1,), (1,)), ((), ()))
TN = (((0,), (0,)), ((), ()))


SMALL_ROWS=197; LARGE_ROWS=325
QB=256
KB=128
NEG=-1e30

def image_ends(small, large, rows):
    ends=[]
    for i in range(1, rows//SMALL_ROWS+1):
        e = jnp.minimum(i, small)*SMALL_ROWS + jnp.maximum(i-small,0)*LARGE_ROWS
        ends.append(jnp.where(i<=small+large, e, 2*rows))
    return ends

def image_of(places, ends):
    idx = jnp.zeros(places.shape, jnp.int32)
    for e in ends:
        idx = idx + (places>=e).astype(jnp.int32)
    return idx

def key_range(ends, first, last, rows):
    lo = jnp.int32(0); hi = jnp.int32(rows)
    for e in ends:
        lo = jnp.maximum(lo, jnp.where(e<=first, e, 0))
        hi = jnp.minimum(hi, jnp.where(e>last, e, rows))
    return lo, hi

def widths_of(rows):
    ws = [w*KB for w in range(3, rows//KB)]
    ws = [w for w in ws if w<=768]
    return ws+[rows]

def with_window(counts_ref, rows, first, body):
    small=counts_ref[0]; large=counts_ref[1]
    ends=image_ends(small, large, rows)
    lo,hi=key_range(ends, first, first+QB-1, rows)
    base=lo//KB
    need=(hi+KB-1)//KB - base
    done=jnp.int32(0)
    for w in widths_of(rows):
        n=w//KB
        use = (need<=n) & (need>done)
        start = jnp.minimum(base, (rows-w)//KB)*KB
        @pl.when(use)
        def _(start=start, w=w):
            body(pl.multiple_of(start,KB), w, ends)
        done=jnp.int32(n)

def fwd_kernel(counts_ref, q_ref, k_ref, v_ref, o_ref, lse_ref):
    rows=q_ref.shape[0]
    lane=lax.broadcasted_iota(jnp.int32,(QB,128),1)
    def block(b, _):
        first=pl.multiple_of(b*QB,QB)
        def body(start, w, ends):
            q=q_ref[pl.ds(first,QB),:]
            k=k_ref[pl.ds(start,w),:]
            v=v_ref[pl.ds(start,w),:]
            rid=image_of(first+lax.broadcasted_iota(jnp.int32,(QB,1),0), ends)
            cid=image_of(start+lax.broadcasted_iota(jnp.int32,(1,w),1), ends)
            bias=jnp.where(rid==cid, 0.0, NEG)
            outs=[];lses=[]
            for e in range(2):
                qm=jnp.where((lane<64)==(e==0), q, jnp.zeros_like(q))
                s=lax.dot_general(qm,k,(((1,),(1,)),((),())),preferred_element_type=jnp.float32)+bias
                m=jnp.max(s,axis=1,keepdims=True)
                p=jnp.exp(s-m)
                l=jnp.sum(p,axis=1,keepdims=True)
                o=jnp.dot(p.astype(jnp.bfloat16),v,preferred_element_type=jnp.float32)
                outs.append(o*(1.0/l)); lses.append(m+jnp.log(l))
            o_ref[pl.ds(first,QB),:]=jnp.where(lane<64,outs[0],outs[1]).astype(jnp.bfloat16)
            both=jnp.where(lane<64,jnp.broadcast_to(lses[0],(QB,128)),jnp.broadcast_to(lses[1],(QB,128)))
            t=both.T
            lse_ref[0,0:1,pl.ds(first,QB)]=t[0:1,:]
            lse_ref[0,1:2,pl.ds(first,QB)]=t[64:65,:]
        with_window(counts_ref, rows, first, body)
        return 0
    lax.fori_loop(0,rows//QB,block,0)

def attn_fwd(counts,q,k,v):
    rows,feat=q.shape
    pairs=feat//128
    spec=pl.BlockSpec((rows,128),lambda p,c:(0,p))
    return pl.pallas_call(fwd_kernel,
        grid_spec=pltpu.PrefetchScalarGridSpec(num_scalar_prefetch=1,grid=(pairs,),
            in_specs=[spec]*3,out_specs=[spec,pl.BlockSpec((1,2,rows),lambda p,c:(p,0,0))]),
        out_shape=[jax.ShapeDtypeStruct((rows,feat),jnp.bfloat16),jax.ShapeDtypeStruct((pairs,2,rows),jnp.float32)],
        name="attend",
        )(counts,q,k,v)

def bwd_kernel(counts_ref, q_ref, k_ref, v_ref, do_ref, lse_ref, dq_ref, dk_ref, dv_ref, dk_acc, dv_acc):
    rows=q_ref.shape[0]
    lane=lax.broadcasted_iota(jnp.int32,(QB,128),1)
    dk_acc[...]=jnp.zeros_like(dk_acc)
    dv_acc[...]=jnp.zeros_like(dv_acc)
    nt=(((1,),(1,)),((),()))
    tn=(((0,),(0,)),((),()))
    def block(b,_):
        first=pl.multiple_of(b*QB,QB)
        def body(start,w,ends):
            q=q_ref[pl.ds(first,QB),:]
            do=do_ref[pl.ds(first,QB),:]
            k=k_ref[pl.ds(start,w),:]
            v=v_ref[pl.ds(start,w),:]
            rid=image_of(start+lax.broadcasted_iota(jnp.int32,(w,1),0), ends)
            cid=image_of(first+lax.broadcasted_iota(jnp.int32,(1,QB),1), ends)
            bias=jnp.where(rid==cid,0.0,NEG)
            dqs=[]
            dks=None;dvs=None
            for e in range(2):
                mask=(lane<64)==(e==0)
                qm=jnp.where(mask,q,jnp.zeros_like(q))
                dom=jnp.where(mask,do,jnp.zeros_like(do))
                s=lax.dot_general(k,qm,nt,preferred_element_type=jnp.float32)+bias
                p=jnp.exp(s-lse_ref[0,e:e+1,pl.ds(first,QB)])
                dp=lax.dot_general(v,dom,nt,preferred_element_type=jnp.float32)
                delta=jnp.sum(p*dp,axis=0,keepdims=True)
                ds=(p*(dp-delta)).astype(jnp.bfloat16)
                pb=p.astype(jnp.bfloat16)
                dv_e=jnp.dot(pb,dom,preferred_element_type=jnp.float32)
                dk_e=jnp.dot(ds,qm,preferred_element_type=jnp.float32)
                dq_e=lax.dot_general(ds,k,tn,preferred_element_type=jnp.float32)
                dvs=dv_e if dvs is None else dvs+dv_e
                dks=dk_e if dks is None else dks+dk_e
                dqs.append(dq_e)
            dv_acc[pl.ds(start,w),:]+=dvs
            dk_acc[pl.ds(start,w),:]+=dks
            dq_ref[pl.ds(first,QB),:]=(jnp.where(lane<64,dqs[0],dqs[1])*0.125).astype(jnp.bfloat16)
        with_window(counts_ref,rows,first,body)
        return 0
    lax.fori_loop(0,rows//QB,block,0)
    dk_ref[...]=dk_acc[...].astype(jnp.bfloat16)
    dv_ref[...]=dv_acc[...].astype(jnp.bfloat16)

def attn_bwd(counts,q,k,v,do,lse):
    rows,feat=q.shape
    pairs=feat//128
    spec=pl.BlockSpec((rows,128),lambda p,c:(0,p))
    return pl.pallas_call(bwd_kernel,
        grid_spec=pltpu.PrefetchScalarGridSpec(num_scalar_prefetch=1,grid=(pairs,),
            in_specs=[spec]*4+[pl.BlockSpec((1,2,rows),lambda p,c:(p,0,0))],out_specs=[spec]*3,
            scratch_shapes=[pltpu.VMEM((rows,128),jnp.float32)]*2),
        out_shape=[jax.ShapeDtypeStruct((rows,feat),jnp.bfloat16)]*3,
        name="attend_back",
        )(counts,q,k,v,do,lse)

f32=jnp.float32; bf16=jnp.bfloat16
RB=256
INV_SQRT2=1/math.sqrt(2.0); INV_SQRT2PI=1/math.sqrt(2*math.pi)

def dot(a,b): return jnp.dot(a,b,preferred_element_type=f32)
def dot_nt(a,b): return lax.dot_general(a,b,NT,preferred_element_type=f32)
def dot_tn(a,b): return lax.dot_general(a,b,TN,preferred_element_type=f32)

def norm_parts(x):
    mean=jnp.mean(x,axis=-1,keepdims=True)
    cen=x-mean
    var=jnp.mean(cen*cen,axis=-1,keepdims=True)
    q=lax.rsqrt(var+EPS)
    return cen*q, q

def live_mask(counts_ref, first, n):
    end=counts_ref[0]*197+counts_ref[1]*325
    r=first+lax.broadcasted_iota(jnp.int32,(n,1),0)
    return r<end

def mid_kernel(counts_ref, mixed_ref, tokens_ref, cot_ref, outw_ref, vec_ref, up_ref, ub_ref, down_ref,
        layer_ref, gres_ref, gmix_ref, gup_ref, gub_ref, gdown_ref, gout_ref, gvec_ref,
        res_s, si_s, gb_s, accout_s, accgs_s, hid_s, gi_s):
    rows=tokens_ref.shape[0]
    j=pl.program_id(0); nj=pl.num_programs(0)
    obias=vec_ref[0:1,:]; gain=vec_ref[1:2,:]; shift=vec_ref[2:3,:]; dbias=vec_ref[3:4,:]
    @pl.when(j==0)
    def _():
        def step(i,_):
            first=pl.multiple_of(i*RB,RB); sl=pl.ds(first,RB)
            res=tokens_ref[sl,:].astype(f32)+(dot(mixed_ref[sl,:],outw_ref[...])+obias)
            res_s[sl,:]=res
            xhat,_q=norm_parts(res)
            si_s[sl,:]=(xhat*gain+shift).astype(bf16)
            live=live_mask(counts_ref,first,RB)
            gb_s[sl,:]=jnp.where(live,cot_ref[sl,:],jnp.zeros((),bf16))
            return 0
        lax.fori_loop(0,rows//RB,step,0)
        accout_s[...]=jnp.zeros_like(accout_s)
        accgs_s[...]=jnp.zeros_like(accgs_s)
    gub=jnp.zeros(gub_ref.shape,f32)
    for i in range(rows//RB):
        sl=slice(i*RB,(i+1)*RB)
        pre=dot(si_s[sl,:],up_ref[...])+ub_ref[...]
        cdf=0.5+0.5*lax.erf(pre*INV_SQRT2)
        pdf=jnp.exp(-0.5*pre*pre)*INV_SQRT2PI
        hid_s[sl,:]=(pre*cdf).astype(bf16)
        gh=dot_nt(gb_s[sl,:],down_ref[...])
        gi=(gh*(cdf+pre*pdf)).astype(bf16)
        gi_s[sl,:]=gi
        gub=gub+jnp.sum(gi.astype(f32),axis=0,keepdims=True)
    gub_ref[...]=gub
    accout_s[...]+=dot(hid_s[...],down_ref[...])
    accgs_s[...]+=dot_nt(gi_s[...],up_ref[...])
    gdown_ref[...]=dot_tn(hid_s[...],gb_s[...]).astype(bf16)
    gup_ref[...]=dot_tn(si_s[...],gi_s[...]).astype(bf16)
    @pl.when(j==nj-1)
    def _():
        gvec_ref[...]=jnp.zeros_like(gvec_ref)
        def step(i,_):
            first=pl.multiple_of(i*RB,RB); sl=pl.ds(first,RB)
            live=live_mask(counts_ref,first,RB)
            res=res_s[sl,:]
            layer=res+(accout_s[sl,:]+dbias)
            layer_ref[sl,:]=jnp.where(live,layer,0.0).astype(bf16)
            xhat,q=norm_parts(res)
            gs=accgs_s[sl,:]
            t=gs*gain
            gb=gb_s[sl,:].astype(f32)
            gres=gb+q*(t-jnp.mean(t,axis=-1,keepdims=True)-xhat*jnp.mean(t*xhat,axis=-1,keepdims=True))
            gres_ref[sl,:]=gres
            ga=gres.astype(bf16)
            mixed_unused=None
            si_s[sl,:]=ga
            gvec_ref[0:1,:]+=jnp.sum(gb,axis=0,keepdims=True)
            gvec_ref[1:2,:]+=jnp.sum(gs*xhat,axis=0,keepdims=True)
            gvec_ref[2:3,:]+=jnp.sum(gs,axis=0,keepdims=True)
            gvec_ref[3:4,:]+=jnp.sum(ga.astype(f32),axis=0,keepdims=True)
            gmix_ref[sl,:]=dot_nt(ga,outw_ref[...]).astype(bf16)
            return 0
        lax.fori_loop(0,rows//RB,step,0)
        gout_ref[...]=dot_tn(mixed_ref[...],si_s[...]).astype(bf16)

def middle(counts,mixed,tokens,cot,outw,vec,up,ub,down,FB=512):
    rows,D=tokens.shape; FF=up.shape[1]
    nj=FF//FB
    full=lambda a: pl.BlockSpec(a.shape,lambda j,c:(0,)*len(a.shape),pipeline_mode=pl.Buffered(1))
    fo=lambda s: pl.BlockSpec(s,lambda j,c:(0,)*len(s),pipeline_mode=pl.Buffered(1))
    return pl.pallas_call(mid_kernel,
        grid_spec=pltpu.PrefetchScalarGridSpec(num_scalar_prefetch=1,grid=(nj,),
            in_specs=[full(mixed),full(tokens),full(cot),full(outw),full(vec),
                pl.BlockSpec((D,FB),lambda j,c:(0,j)),pl.BlockSpec((1,FB),lambda j,c:(0,j)),pl.BlockSpec((FB,D),lambda j,c:(j,0))],
            out_specs=[fo((rows,D)),fo((rows,D)),fo((rows,D)),
                pl.BlockSpec((D,FB),lambda j,c:(0,j)),pl.BlockSpec((1,FB),lambda j,c:(0,j)),pl.BlockSpec((FB,D),lambda j,c:(j,0)),
                fo((D,D)),fo((8,D))],
            scratch_shapes=[pltpu.VMEM((rows,D),f32),pltpu.VMEM((rows,D),bf16),pltpu.VMEM((rows,D),bf16),
                pltpu.VMEM((rows,D),f32),pltpu.VMEM((rows,D),f32),pltpu.VMEM((rows,FB),bf16),pltpu.VMEM((rows,FB),bf16)]),
        out_shape=[jax.ShapeDtypeStruct((rows,D),bf16),jax.ShapeDtypeStruct((rows,D),f32),jax.ShapeDtypeStruct((rows,D),bf16),
            jax.ShapeDtypeStruct((D,FF),bf16),jax.ShapeDtypeStruct((1,FF),f32),jax.ShapeDtypeStruct((FF,D),bf16),
            jax.ShapeDtypeStruct((D,D),bf16),jax.ShapeDtypeStruct((8,D),f32)],
        compiler_params=pltpu.CompilerParams(vmem_limit_bytes=60*2**20),
        name="feed_forward",
        )(counts,mixed,tokens,cot,outw,vec,up,ub,down)


def qkv_kernel(tokens_ref, vec_ref, qw_ref, kw_ref, vw_ref, fi_ref, q_ref, k_ref, v_ref):
    rows=tokens_ref.shape[0]
    gain=vec_ref[0:1,:]; shift=vec_ref[1:2,:]; qb=vec_ref[2:3,:]; vb=vec_ref[3:4,:]
    for i in range(rows//RB):
        sl=slice(i*RB,(i+1)*RB)
        xhat,_=norm_parts(tokens_ref[sl,:].astype(f32))
        fi=(xhat*gain+shift).astype(bf16)
        fi_ref[sl,:]=fi
        q_ref[sl,:]=((dot(fi,qw_ref[...])+qb).astype(bf16).astype(f32)*0.125).astype(bf16)
        k_ref[sl,:]=dot(fi,kw_ref[...]).astype(bf16)
        v_ref[sl,:]=(dot(fi,vw_ref[...])+vb).astype(bf16)

def project(tokens,vec,qw,kw,vw):
    rows,D=tokens.shape
    return pl.pallas_call(qkv_kernel,out_shape=[jax.ShapeDtypeStruct((rows,D),bf16)]*4,
        compiler_params=pltpu.CompilerParams(vmem_limit_bytes=60*2**20),name="project")(tokens,vec,qw,kw,vw)

def back_kernel(tokens_ref, vec_ref, gres_ref, fi_ref, dq_ref, dk_ref, dv_ref, qw_ref, kw_ref, vw_ref,
        gtok_ref, gq_ref, gk_ref, gv_ref, gvec_ref):
    rows=tokens_ref.shape[0]
    gain=vec_ref[0:1,:]
    gvec=[jnp.zeros((1,tokens_ref.shape[1]),f32)]*4
    for i in range(rows//RB):
        sl=slice(i*RB,(i+1)*RB)
        dq=dq_ref[sl,:];dk=dk_ref[sl,:];dv=dv_ref[sl,:]
        gs=dot_nt(dq,qw_ref[...])+dot_nt(dk,kw_ref[...])+dot_nt(dv,vw_ref[...])
        xhat,q=norm_parts(tokens_ref[sl,:].astype(f32))
        t=gs*gain
        gtok_ref[sl,:]=gres_ref[sl,:]+q*(t-jnp.mean(t,axis=-1,keepdims=True)-xhat*jnp.mean(t*xhat,axis=-1,keepdims=True))
        for n,a in enumerate((gs*xhat,gs,dq.astype(f32),dv.astype(f32))):
            gvec[n]=gvec[n]+jnp.sum(a,axis=0,keepdims=True)
    gvec_ref[...]=jnp.zeros_like(gvec_ref)
    for n in range(4): gvec_ref[n:n+1,:]=gvec[n]
    fi=fi_ref[...]
    gq_ref[...]=dot_tn(fi,dq_ref[...]).astype(bf16)
    gk_ref[...]=dot_tn(fi,dk_ref[...]).astype(bf16)
    gv_ref[...]=dot_tn(fi,dv_ref[...]).astype(bf16)

def project_back(tokens,vec,gres,fi,dq,dk,dv,qw,kw,vw):
    rows,D=tokens.shape
    s=jax.ShapeDtypeStruct
    return pl.pallas_call(back_kernel,out_shape=[s((rows,D),f32),s((D,D),bf16),s((D,D),bf16),s((D,D),bf16),s((8,D),f32)],
        compiler_params=pltpu.CompilerParams(vmem_limit_bytes=60*2**20),name="project_back")(tokens,vec,gres,fi,dq,dk,dv,qw,kw,vw)

FSDP="fsdp"

def on_device(tokens, image_counts, cotangent, first_gain, first_shift, query_weight, query_bias, key_weight,
              value_weight, value_bias, out_weight, out_bias, second_gain, second_shift, up_weight, up_bias,
              down_weight, down_bias):
    rows, feat = tokens.shape
    own = query_weight.shape[0]
    n = feat // own
    counts = image_counts[0]
    gather = lambda a: lax.all_gather(a, FSDP, axis=0, tiled=False)
    small = jnp.concatenate([jnp.stack([first_gain, first_shift, query_bias, value_bias, out_bias, second_gain, second_shift, down_bias]),
        up_bias.reshape(-1, own)])
    small_all = gather(small)
    attn_all = gather(jnp.stack([query_weight, key_weight, value_weight, out_weight]))
    full = lambda i: attn_all[:, i].reshape(feat, feat)
    qw, kw, vw, ow = full(0), full(1), full(2), full(3)
    up = gather(up_weight).reshape(feat, -1)
    down = gather(down_weight).reshape(-1, feat)
    wide = jnp.transpose(small_all[:, :8], (1, 0, 2)).reshape(8, feat).astype(f32)
    ub = small_all[:, 8:].reshape(1, -1).astype(f32)
    vec1 = wide[0:4]
    vec2 = wide[4:8]
    fi, q, k, v = project(tokens, vec1, qw, kw, vw)
    mixed, lse = attn_fwd(counts, q, k, v)
    layer_out, gres, gmix, gup, gub, gdown, gout, gv2 = middle(counts, mixed, tokens, cotangent, ow, vec2, up, ub, down)
    dq, dk, dv = attn_bwd(counts, q, k, v, gmix, lse)
    gtok, gq, gk, gv, gv1 = project_back(tokens, vec1, gres, fi, dq, dk, dv, qw, kw, vw)
    scatter = lambda a: lax.psum_scatter(a, FSDP, scatter_dimension=0, tiled=False)
    pair = lambda a: lax.psum(a, "dp").astype(f32)
    su = scatter(gup.reshape(n, own, -1))
    sd = scatter(gdown.reshape(n, -1, feat))
    sa = scatter(jnp.stack([g.reshape(n, own, feat) for g in (gq, gk, gv, gout)], axis=1))
    smalls = jnp.concatenate([gv1[0:4], gv2[0:4]]).reshape(8, n, own)
    smalls = jnp.concatenate([jnp.transpose(smalls, (1, 0, 2)), gub.reshape(n, -1, own)], axis=1).astype(bf16)
    ss = scatter(smalls)
    su, sd, sa, ss = (pair(a) for a in (su, sd, sa, ss))
    return (layer_out, gtok, ss[0], ss[1], sa[0], ss[2], sa[1], sa[2], ss[3], sa[3], ss[7], ss[5], ss[6], su,
            ss[8:].reshape(-1), sd, ss[4])


def solution(mesh):
    rows = P(("dp", "fsdp"), None)
    mat = P("fsdp", None)
    vec = P("fsdp")
    return jax.shard_map(
        on_device,
        mesh=mesh,
        in_specs=(rows, rows, rows, vec, vec, mat, vec, mat, mat, vec, mat, vec, vec, vec, mat, vec, mat, vec),
        out_specs=(rows, rows, vec, vec, mat, vec, mat, mat, vec, mat, vec, vec, vec, mat, vec, mat, vec),
        check_vma=False,
    )
```

time: 912 us -> 559 us (0.61)
  matrix products: 300 us -> 0 us
  Pallas kernels: 0 us -> 131 us
  blocking collectives: 128 us -> 28.5 us
  other arithmetic: 107 us -> 9.21 us
  waiting for transfers between devices: 285 us -> 363 us
  local copies, waits for them, and re-layouts: 56.2 us -> 12 us
    dot_general x32 -> x0, matrix products: 300 us -> none  [the longest x6 62.2 us: product(): return jnp.dot(left, right, preferred_element_type=jnp.float32)]
    pallas_call x0 -> x5, Pallas kernels: none -> 131 us  [the longest x1 47.4 us: middle(): pl.pallas_call(mid_kernel, grid_spec=pltpu.PrefetchScalarGridSpec(num_sca...]
    unnamed x2 -> x0, blocking collectives: 123 us -> none
    all_gather x6 -> x3, waiting for transfers between devices: 44.3 us -> 101 us  [on_device(): gather = lambda a: lax.all_gather(a, FSDP, axis=0, tiled=False)]
    convert_element_type x27 -> x6, other arithmetic: 59.6 us -> 2.79 us  [the longest x4 2.77 us: on_device(): pair = lambda a: lax.psum(a, 'dp').astype(f32)]
    reduce_sum x11 -> x0, other arithmetic: 38.3 us -> none  [the longest x2 25.2 us: attend(): summed = jnp.sum(exp_terms, axis=-1, keepdims=True)]
    unnamed x137 -> x8, local copies, waits for them, and re-layouts: 30.1 us -> 0.01 us
    psum x1, waiting for transfers between devices: 6.65 us -> 32.2 us  [on_device(): pair = lambda a: lax.psum(a, 'dp').astype(f32)]
  transfers between devices with their start and end apart: 13 -> 8, of which waited for: 7 -> 8; matrix products, arithmetic and copies ran while one was open for 44% -> 3% of each run, Pallas kernels for 0% -> 15%
where the time goes in v1:
time: 559 us; the launch traced here: 558 us
  waiting for transfers between devices  363 us (65%)
  Pallas kernels  131 us (23%)
  blocking collectives  28.5 us (5%)
  between operations  14.2 us (3%)
  local copies, waits for them, and re-layouts  12 us (2%)
  other arithmetic  9.21 us (2%)
    reduce_scatter x4, waiting for transfers between devices, on_device(): lax.psum_scatter(a, FSDP, scatter_dimension=0, tiled=False)  228 us
    all_gather x3, waiting for transfers between devices, on_device(): gather = lambda a: lax.all_gather(a, FSDP, axis=0, tiled=False)  101 us
    pallas_call x1, Pallas kernels, middle(): pl.pallas_call(mid_kernel, grid_spec=pltpu.PrefetchScalarGridSpec(num_sca...  47.4 us
    pallas_call x1, Pallas kernels, attn_bwd(): pl.pallas_call(bwd_kernel, grid_spec=pltpu.PrefetchScalarGridSpec(num_sca...  36.8 us
    psum x1, waiting for transfers between devices, on_device(): pair = lambda a: lax.psum(a, 'dp').astype(f32)  32.2 us
    all_gather x1, blocking collectives, on_device(): gather = lambda a: lax.all_gather(a, FSDP, axis=0, tiled=False)  23.5 us
    pallas_call x1, Pallas kernels, attn_fwd(): pl.pallas_call(fwd_kernel, grid_spec=pltpu.PrefetchScalarGridSpec(num_sca...  23.5 us
    pallas_call x1, Pallas kernels, project_back(): pl.pallas_call(back_kernel, out_shape=[s((rows, D), f32), s((D, D), bf16)...  14.8 us
  transfers between devices with their start and end apart: 8, of which 8 were waited for; matrix products, arithmetic and copies ran while one was open for 3% of the time, Pallas kernels for 15%

profile of v1, /device:TPU:0, one launch (start us, length us, event | category | flops | bytes accessed | tf_op | source)
XLA Modules:
  0.0 558.2 jit_solution(84455198461741081)
XLA Ops:
  7.2 1.7 pad_maximum_fusion.1
  9.1 0.7 all-gather.11.cloned.1.call-update
  9.8 0.7 all-gather.13.cloned.1.call-update
  10.5 0.7 reshape.79
  11.3 0.8 concatenate.11
  12.1 23.5 %all-gather.4 = bf16[16,12,48]{2,1,0:T(8,128)(2,1)S(1)} all-gather(bf16[1,12,48]{2,1,0:T(8,128)(2,1)S(1)} %bitcast.96), channel_id=2, replica_groups=mesh['dp'=2,'fsdp'=16] {'fsdp'}, dimensions={0}, use_global_device_ids=true | all-gather | bytes 19584 | tf_op jit(solution)/shard_map/all_gather | solution.py:317
  35.6 0.7 reshape.87.ub_ref
  36.3 0.7 slice.85.vec_ref
  37.0 0.7 slice.79.vec_ref
  37.7 29.4 %all-gather.9.cloned.1.call-done = bf16[64,48,768]{2,1,0:T(8,128)(2,1)} async-done(((bf16[4,48,768]{2,1,0:T(8,128)(2,1)}), bf16[64,48,768]{2,1,0:T(8,128)(2,1)}) %all-gather.9.cloned.1.call-update) | async-done | bytes 4718608 | tf_op jit(solution)/shard_map/all_gather | solution.py:317
  67.1 4.6 fusion
  71.7 8.3 %project.1 = (bf16[1024,768]{1,0:T(8,128)(2,1)}, bf16[1024,768]{1,0:T(8,128)(2,1)}, bf16[1024,768]{1,0:T(8,128)(2,1)}, bf16[1024,768]{1,0:T(8,128)(2,1)}) custom-call(bf16[1024,768]{1,0:T(8,128)(2,1)} %tokens_ref.5, f32[4,768]{1,0:T(4,128)} %slice.79.vec_ref, bf16[768,768]{1,0:T(8,128)(2,1)} %bitcast.78, bf16[768,768]{1,0:T(8,128)(2,1)} %bitcast.76, ...), custom_call_target="tpu_custom_call" | custom-call | tf_op jit(solution)/shard_map/project/pallas_call | solution.py:278
  80.0 23.5 %attend.1 = (bf16[1024,768]{1,0:T(8,128)(2,1)}, f32[6,2,1024]{2,1,0:T(2,128)}) custom-call(s32[2]{0:T(128)} %bitcast.97, bf16[1024,768]{1,0:T(8,128)(2,1)} %get-tuple-element.39.q_ref, bf16[1024,768]{1,0:T(8,128)(2,1)} %get-tuple-element.40.k_ref, bf16[1024,768]{1,0:T(8,128)(2,1)} %get-tuple-element.41.v_ref), custom_call_target="tpu_custom_call" | custom-call | tf_op jit(solution)/shard_map/attend/pallas_call | solution.py:96
  103.4 17.8 %all-gather.11.cloned.1.call-done.up_ref = bf16[768,3072]{1,0:T(8,128)(2,1)} async-done(((bf16[48,3072]{1,0:T(8,128)(2,1)}), bf16[768,3072]{1,0:T(8,128)(2,1)}) %all-gather.11.cloned.1.call-update) | async-done | bytes 4718608 | tf_op jit(solution)/shard_map/all_gather | solution.py:317
  121.2 54.1 %all-gather.13.cloned.1.call-done.down_ref = bf16[3072,768]{1,0:T(8,128)(2,1)} async-done(((bf16[192,768]{1,0:T(8,128)(2,1)}), bf16[3072,768]{1,0:T(8,128)(2,1)}) %all-gather.13.cloned.1.call-update) | async-done | bytes 4718608 | tf_op jit(solution)/shard_map/all_gather | solution.py:317
  175.3 47.4 %feed_forward.1 = (bf16[1024,768]{1,0:T(8,128)(2,1)}, f32[1024,768]{1,0:T(8,128)}, bf16[1024,768]{1,0:T(8,128)(2,1)}, bf16[768,3072]{1,0:T(8,128)(2,1)}, f32[1,3...) custom-call(s32[2]{0:T(128)} %bitcast.98, ...), custom_call_target="tpu_custom_call" | custom-call | tf_op jit(solution)/shard_map/feed_forward/pallas_call | solution.py:247
  223.4 36.8 %attend_back.1 = (bf16[1024,768]{1,0:T(8,128)(2,1)}, bf16[1024,768]{1,0:T(8,128)(2,1)}, bf16[1024,768]{1,0:T(8,128)(2,1)}) custom-call(s32[2]{0:T(128)} %bitcast.99, bf16[1024,768]{1,0:T(8,128)(2,1)} %get-tuple-element.39.q_ref, bf16[1024,768]{1,0:T(8,128)(2,1)} %get-tuple-element.40.k_ref, bf16[1024,768]{1,0:T(8,128)(2,1)} %get-tuple-element.41.v_ref, ...), custom_call_target="tpu_custom_call" | custom-call | tf_op jit(solution)/shard_map/attend_back/pallas_call | solution.py:151
  260.2 14.8 %project_back.1 = (f32[1024,768]{1,0:T(8,128)}, bf16[768,768]{1,0:T(8,128)(2,1)}, bf16[768,768]{1,0:T(8,128)(2,1)}, bf16[768,768]{1,0:T(8,128)(2,1)}, f32[8,768]{1,0:T(8,128)}) custom-call(bf16[1024,768]{1,0:T(8,128)(2,1)} %tokens_ref.5, f32[4,768]{1,0:T(4,128)} %slice.79.vec_ref, f32[1024,768]{1,0:T(8,128)} %get-tuple-element.44.gres_ref, ...), custom_call_target="tpu_custom_call" | custom-call | tf_op jit(solution)/shard_map/project_back/pallas_call | solution.py:305
  275.0 4.0 pad_maximum_fusion
  279.1 0.7 slice.142
  279.8 0.7 slice.141
  280.8 0.7 pad_maximum_fusion.2
  281.5 15.4 %reduce-scatter.9.cloned.1.call-done = bf16[1,48,3072]{2,1,0:T(8,128)(2,1)} async-done(((bf16[16,48,3072]{2,1,0:T(8,128)(2,1)}), bf16[1,48,3072]{2,1,0:T(8,128)(2,1)}) %reduce-scatter.9.cloned.1.call-update) | async-done | bytes 294928 | tf_op jit(solution)/shard_map/reduce_scatter | solution.py:335
  297.0 78.8 %reduce-scatter.11.cloned.1.call-done = bf16[1,192,768]{2,1,0:T(8,128)(2,1)} async-done(((bf16[16,192,768]{2,1,0:T(8,128)(2,1)}), bf16[1,192,768]{2,1,0:T(8,128)(2,1)}) %reduce-scatter.11.cloned.1.call-update) | async-done | bytes 294928 | tf_op jit(solution)/shard_map/reduce_scatter | solution.py:335
  375.8 78.3 %reduce-scatter.7.cloned.1.call-done = bf16[1,4,48,768]{3,2,1,0:T(8,128)(2,1)} async-done(((bf16[16,4,48,768]{3,2,1,0:T(8,128)(2,1)}), bf16[1,4,48,768]{3,2,1,0:T(8,128)(2,1)}) %reduce-scatter.7.cloned.1.call-update) | async-done | bytes 294928 | tf_op jit(solution)/shard_map/reduce_scatter | solution.py:335
  454.1 55.2 %reduce-scatter.5.cloned.1.call-done = bf16[1,12,48]{2,1,0:T(8,128)(2,1)} async-done(((bf16[16,12,48]{2,1,0:T(8,128)(2,1)}), bf16[1,12,48]{2,1,0:T(8,128)(2,1)}) %reduce-scatter.5.cloned.1.call-update) | async-done | bytes 1168 | tf_op jit(solution)/shard_map/reduce_scatter | solution.py:335
  509.3 5.0 psum.28
  515.6 32.2 %all-reduce.3.cloned.1.call-done = (bf16[4,48,768]{2,1,0:T(8,128)(2,1)}, bf16[48,3072]{1,0:T(8,128)(2,1)}, bf16[192,768]{1,0:T(8,128)(2,1)}) async-done(((bf16[4,48,768]{2,1,0:T(8,128)(2,1)}, bf16[48,3072]{1,0:T(8,128)(2,1)}, bf16[192,768]{1,0:T(8,128)(2,1)}), (bf16[4,48,768]{2,1,0:T(8,128)(2,1)}, bf16[48,3072]{1,0:T(8,128)(2,1)}, bf16[192,768]{1,0:T(8,128)(2,1)})) %all-reduce.3.cloned.1.call-update) | async-done | bytes 884752 | tf_op jit(solution)/shard_map/psum | solution.py:336
  547.8 1.1 convert_element_type.30
  548.8 0.8 slice_bitcast_fusion
  549.6 0.9 convert_element_type.31
  550.5 0.9 convert_element_type.32
  (36 shorter events, 2.4 us)
Async XLA Ops:
  7.2 59.9 %all-gather.9.cloned.1.call-start = ((), (), s32[]{:S(2)}) async-start(), calls=%async_computation.8 | async-start | bytes 5013504 | tf_op jit(solution)/shard_map/all_gather | solution.py:317
  9.0 112.2 %all-gather.11.cloned.1.call-start = ((), (), s32[]{:S(2)}) async-start(), calls=%async_computation.9 | async-start | bytes 5013504 | tf_op jit(solution)/shard_map/all_gather | solution.py:317
  9.8 165.5 %all-gather.13.cloned.1.call-start = ((), (), s32[]{:S(2)}) async-start(), calls=%async_computation.10 | async-start | bytes 5013504 | tf_op jit(solution)/shard_map/all_gather | solution.py:317
  10.5 286.5 %reduce-scatter.9.cloned.1.call-start = ((), (), s32[]{:S(2)}) async-start(), calls=%async_computation.6 | async-start | bytes 5013504 | tf_op jit(solution)/shard_map/reduce_scatter | solution.py:335
  222.8 153.0 %reduce-scatter.11.cloned.1.call-start = ((), (), s32[]{:S(2)}) async-start(), calls=%async_computation.7 | async-start | bytes 5013504 | tf_op jit(solution)/shard_map/reduce_scatter | solution.py:335
  223.4 230.8 %reduce-scatter.7.cloned.1.call-start = ((), (), s32[]{:S(2)}) async-start(), calls=%async_computation.5 | async-start | bytes 5013504 | tf_op jit(solution)/shard_map/reduce_scatter | solution.py:335
  260.2 14.8 %copy-start = (bf16[768,768]{1,0:T(8,128)(2,1)S(1)}, bf16[768,768]{1,0:T(8,128)(2,1)}, u32[]{:S(2)}) copy-start(bf16[768,768]{1,0:T(8,128)(2,1)} %get-tuple-element.58) | copy-start | bytes 3538948
  279.0 1.6 copy-start.3
  279.0 230.3 %reduce-scatter.5.cloned.1.call-start = ((), (), s32[]{:S(2)}) async-start(), calls=%async_computation.4 | async-start | bytes 69632 | tf_op jit(solution)/shard_map/reduce_scatter | solution.py:335
  281.5 266.3 %all-reduce.3.cloned.1.call-start = ((), (), s32[]{:S(2)}) async-start(), calls=%async_computation.11 | async-start | bytes 1769472 | tf_op jit(solution)/shard_map/psum | solution.py:336
  547.7 1.9 copy-start.2
  547.7 2.8 copy-start.1
Sparse Core Ops, SparseCore 0:
  10.9 56.1 all-gather.8
  69.4 51.7 all-gather.10
  123.5 51.7 all-gather.12
  222.9 74.0 reduce-scatter.8
  301.2 74.5 reduce-scatter.10
  379.5 74.5 reduce-scatter.6
  458.4 50.8 reduce-scatter.4
  511.8 35.9 all-reduce.2

commit v2 on v1

--- a/solution.py
+++ b/solution.py
@@ -305,29 +305,306 @@
     return pl.pallas_call(back_kernel,out_shape=[s((rows,D),f32),s((D,D),bf16),s((D,D),bf16),s((D,D),bf16),s((8,D),f32)],
         compiler_params=pltpu.CompilerParams(vmem_limit_bytes=60*2**20),name="project_back")(tokens,vec,gres,fi,dq,dk,dv,qw,kw,vw)
 
+
+MESH = pl.DeviceIdType.MESH
+
+
+class Place:
+    def __init__(self, dp_total, fsdp_total):
+        half = fsdp_total // 2
+        self.outer_total = 4 if half % 4 == 0 else half
+        self.inner_total = half // self.outer_total
+        self.d = lax.axis_index("dp")
+        self.f = lax.axis_index("fsdp")
+        self.core = self.f % 2
+        self.inner = (self.f // 2) % self.inner_total
+        self.outer = self.f // (2 * self.inner_total)
+        self.side = self.d % 2
+        self.twin = self.d + 1 - 2 * self.side
+
+    def index(self, outer, inner, core):
+        return (outer * self.inner_total + inner) * 2 + core
+
+    def slot(self, s, t, core=None):
+        return self.index((self.outer + s) % self.outer_total, (self.inner + t) % self.inner_total,
+                          self.core if core is None else core)
+
+    def neighbours(self):
+        out = [(self.d, self.slot(s, 0)) for s in range(1, self.outer_total)]
+        out += [(self.d, self.slot(0, t)) for t in range(1, self.inner_total)]
+        out += [(self.twin, self.f), (self.d, self.slot(0, 0, 1 - self.core))]
+        return out
+
+
+def greet(place):
+    barrier = pltpu.get_barrier_semaphore()
+    others = place.neighbours()
+    for other in others:
+        pl.semaphore_signal(barrier, inc=1, device_id=other, device_id_type=MESH)
+    pl.semaphore_wait(barrier, len(others))
+
+
+class Gather:
+    def __init__(self, place, view, rows, edge, sems, base):
+        self.place, self.view, self.rows, self.edge = place, view, rows, edge
+        self.send_sem, self.recv_sem = sems
+        A, B = place.outer_total, place.inner_total
+        self.base = base
+        self.keys = {}
+        for s in range(1, A):
+            self.keys["z", s] = len(self.keys)
+        for s in range(A):
+            for t in range(1, B):
+                self.keys["x", s, t] = len(self.keys)
+        if edge:
+            for s in range(A):
+                for t in range(B):
+                    if s or t:
+                        self.keys["y", s, t] = len(self.keys)
+        for s in range(A):
+            for t in range(B):
+                self.keys["c", s, t] = len(self.keys)
+        self.sent = []
+
+    @staticmethod
+    def count(A, B, edge):
+        return (A - 1) + A * (B - 1) + (A * B - 1 if edge else 0) + A * B
+
+    def part(self, slot, kind):
+        if not self.edge:
+            return self.view(slot, 0, self.rows)
+        p = self.place.side
+        if kind == "plane":
+            return self.view(slot, p * self.edge, self.rows - self.edge)
+        if kind == "mine":
+            return self.view(slot, p * (self.rows - self.edge), self.edge)
+        if kind == "theirs":
+            return self.view(slot, (1 - p) * (self.rows - self.edge), self.edge)
+        return self.view(slot, 0, self.rows)
+
+    def copy(self, key, ref, to):
+        i = self.base + self.keys[key]
+        return pltpu.make_async_remote_copy(src_ref=ref, dst_ref=ref, send_sem=self.send_sem.at[i],
+                                            recv_sem=self.recv_sem.at[i], device_id=to, device_id_type=MESH)
+
+    def send(self, key, ref, to):
+        c = self.copy(key, ref, to)
+        c.start()
+        self.sent.append(c)
+
+    def got(self, key, ref):
+        self.copy(key, ref, (self.place.d, self.place.f)).wait_recv()
+
+    def start_outer(self):
+        p = self.place
+        for s in range(1, p.outer_total):
+            self.send(("z", s), self.part(p.f, "plane"), (p.d, p.slot(-s, 0)))
+
+    def pass_inner(self, s):
+        p = self.place
+        for t in range(1, p.inner_total):
+            self.send(("x", s, t), self.part(p.slot(s, 0), "plane"), (p.d, p.slot(0, -t)))
+
+    def pass_twin(self, s, t):
+        p = self.place
+        if self.edge:
+            self.send(("y", s, t), self.part(p.slot(s, t), "mine"), (p.twin, p.f))
+
+    def pass_core(self, s, t):
+        p = self.place
+        self.send(("c", s, t), self.part(p.slot(s, t), "all"), (p.d, p.slot(0, 0, 1 - p.core)))
+
+    def start_inner(self):
+        self.pass_inner(0)
+        self.pass_core(0, 0)
+
+    def from_outer(self):
+        p = self.place
+        for s in range(1, p.outer_total):
+            self.got(("z", s), self.part(p.slot(s, 0), "plane"))
+            self.pass_inner(s)
+            self.pass_twin(s, 0)
+
+    def from_inner(self):
+        p = self.place
+        for s in range(p.outer_total):
+            for t in range(1, p.inner_total):
+                self.got(("x", s, t), self.part(p.slot(s, t), "plane"))
+                self.pass_twin(s, t)
+
+    def from_twin(self):
+        p = self.place
+        for s in range(p.outer_total):
+            for t in range(p.inner_total):
+                if s or t:
+                    if self.edge:
+                        self.got(("y", s, t), self.part(p.slot(s, t), "theirs"))
+                    self.pass_core(s, t)
+
+    def from_core(self):
+        p = self.place
+        for s in range(p.outer_total):
+            for t in range(p.inner_total):
+                self.got(("c", s, t), self.part(p.slot(s, t, 1 - p.core), "all"))
+
+    def finish(self):
+        for c in self.sent:
+            c.wait_send()
+
+
+def local(src, dst, sem):
+    c = pltpu.make_async_copy(src, dst, sem)
+    c.start()
+    return c
+
+
+def gather_kernel(dp_total, fsdp_total, tokens_ref, small_ref, qo_ref, ko_ref, vo_ref, oo_ref, uo_ref, do_ref,
+                  fi_ref, q_ref, k_ref, v_ref, vec_ref, qkv_all, o_all, up_all, down_all, small_all,
+                  w_s, small_s, send_sem, recv_sem, loc_sem):
+    place = Place(dp_total, fsdp_total)
+    A, B = place.outer_total, place.inner_total
+    n = fsdp_total
+    own = qo_ref.shape[0]
+    down_own = do_ref.shape[0]
+    ff = uo_ref.shape[1]
+    me = place.f
+    greet(place)
+    fill = [local(small_ref, small_all.at[me], loc_sem.at[0])]
+    for i, r in enumerate((qo_ref, ko_ref, vo_ref)):
+        fill.append(local(r, qkv_all.at[me, pl.ds(i * own, own)], loc_sem.at[1 + i]))
+    fill.append(local(oo_ref, o_all.at[me], loc_sem.at[4]))
+    fill.append(local(uo_ref, up_all.at[me], loc_sem.at[5]))
+    fill.append(local(do_ref, down_all.at[me], loc_sem.at[6]))
+    sems = (send_sem, recv_sem)
+    third = own // 3
+
+    def rows_view(ref, offset=0, cols=None):
+        def view(slot, start, rows):
+            at = pl.ds(pl.multiple_of(offset + start, 8), rows)
+            return ref.at[slot, at] if cols is None else ref.at[slot, at, cols]
+        return view
+
+    specs = [(rows_view(small_all), small_all.shape[1], 0),
+             (rows_view(qkv_all), 3 * own, own),
+             (rows_view(o_all), own, third),
+             (rows_view(up_all, 0, pl.ds(0, ff // 2)), own, third),
+             (rows_view(up_all, 0, pl.ds(ff // 2, ff // 2)), own, third),
+             (rows_view(down_all, 0), down_own // 2, down_own // 6),
+             (rows_view(down_all, down_own // 2), down_own // 2, down_own // 6)]
+    units = []
+    base = 0
+    for view, rows, edge in specs:
+        units.append(Gather(place, view, rows, edge, sems, base))
+        base += Gather.count(A, B, edge)
+    for c in fill:
+        c.wait()
+    for u in units:
+        u.start_outer()
+    sm, u0, rest = units[0], units[1], units[2:]
+    sm.start_inner()
+    u0.start_inner()
+    sm.from_outer()
+    sm.from_inner()
+    sm.from_twin()
+    u0.from_outer()
+    rest[0].start_inner()
+    rest[1].start_inner()
+    sm.from_core()
+    cs = local(small_all, small_s, loc_sem.at[0])
+    u0.from_inner()
+    rest[0].from_outer()
+    cs.wait()
+    total = jnp.zeros(vec_ref.shape, f32)
+    for i in range(n):
+        total = total + small_s[i].astype(f32)
+    vec_ref[...] = total
+    u0.from_twin()
+    rest[1].from_outer()
+    u0.from_core()
+    cw = local(qkv_all, w_s, loc_sem.at[1])
+    rest[2].start_inner()
+    rest[0].from_inner()
+    cw.wait()
+    rows = tokens_ref.shape[0]
+    todo = [rest[2].from_outer, rest[0].from_twin, rest[1].from_inner, rest[3].start_inner,
+            rest[3].from_outer, rest[1].from_twin, rest[0].from_core, rest[2].from_inner, rest[4].start_inner,
+            rest[4].from_outer, rest[2].from_twin, rest[1].from_core, rest[3].from_inner, rest[3].from_twin,
+            rest[4].from_inner, rest[2].from_core, rest[4].from_twin, rest[3].from_core, rest[4].from_core]
+    gain = vec_ref[0:1, :]
+    shift = vec_ref[1:2, :]
+    qbias = vec_ref[2:3, :]
+    vbias = vec_ref[3:4, :]
+    feat = tokens_ref.shape[1]
+    for i in range(rows // RB):
+        sl = slice(i * RB, (i + 1) * RB)
+        xhat, _ = norm_parts(tokens_ref[sl, :].astype(f32))
+        fi = (xhat * gain + shift).astype(bf16)
+        fi_ref[sl, :] = fi
+        weight = lambda i: w_s[:, i * own:(i + 1) * own, :].reshape(feat, feat)
+        q_ref[sl, :] = ((dot(fi, weight(0)) + qbias).astype(bf16).astype(f32) * 0.125).astype(bf16)
+        k_ref[sl, :] = dot(fi, weight(1)).astype(bf16)
+        v_ref[sl, :] = (dot(fi, weight(2)) + vbias).astype(bf16)
+        for _ in range(2):
+            todo.pop(0)()
+    for t in todo:
+        t()
+    for u in units:
+        u.finish()
+
+
+def gather_project(sizes, tokens, small, qw, kw, vw, ow, up, down):
+    dp_total, n = sizes
+    rows, feat = tokens.shape
+    own = qw.shape[0]
+    half = n // 2
+    A = 4 if half % 4 == 0 else half
+    B = half // A
+    copies = Gather.count(A, B, 0) + 6 * Gather.count(A, B, 1)
+    s = jax.ShapeDtypeStruct
+    vm = pl.BlockSpec(memory_space=pltpu.VMEM)
+    anyspec = pl.BlockSpec(memory_space=pl.ANY)
+    return pl.pallas_call(
+        functools.partial(gather_kernel, dp_total, n),
+        in_specs=[vm] * 8,
+        out_specs=[vm] * 5 + [anyspec] * 5,
+        out_shape=[s((rows, feat), bf16)] * 4 + [s(small.shape, f32), s((n, 3 * own, feat), bf16), s((n, own, feat), bf16),
+                   s((n,) + up.shape, bf16), s((n,) + down.shape, bf16), s((n,) + small.shape, bf16)],
+        scratch_shapes=[pltpu.VMEM((n, 3 * own, feat), bf16), pltpu.VMEM((n,) + small.shape, bf16),
+                        pltpu.SemaphoreType.DMA((copies,)), pltpu.SemaphoreType.DMA((copies,)),
+                        pltpu.SemaphoreType.DMA((8,))],
+        compiler_params=pltpu.CompilerParams(collective_id=1, has_side_effects=True, vmem_limit_bytes=60 * 2**20),
+        name="gather_project",
+    )(tokens, small, qw, kw, vw, ow, up, down)
+
 FSDP="fsdp"
 
-def on_device(tokens, image_counts, cotangent, first_gain, first_shift, query_weight, query_bias, key_weight,
+def spread(vectors, index, total):
+    own = vectors.shape[-1]
+    at = lax.broadcasted_iota(jnp.int32, (1, total, own), 1)
+    wide = jnp.where(at == index, vectors[:, None, :], jnp.zeros((), vectors.dtype))
+    return wide.reshape(vectors.shape[0], total * own)
+
+def on_device(sizes, tokens, image_counts, cotangent, first_gain, first_shift, query_weight, query_bias, key_weight,
               value_weight, value_bias, out_weight, out_bias, second_gain, second_shift, up_weight, up_bias,
               down_weight, down_bias):
     rows, feat = tokens.shape
     own = query_weight.shape[0]
     n = feat // own
     counts = image_counts[0]
-    gather = lambda a: lax.all_gather(a, FSDP, axis=0, tiled=False)
-    small = jnp.concatenate([jnp.stack([first_gain, first_shift, query_bias, value_bias, out_bias, second_gain, second_shift, down_bias]),
-        up_bias.reshape(-1, own)])
-    small_all = gather(small)
-    attn_all = gather(jnp.stack([query_weight, key_weight, value_weight, out_weight]))
-    full = lambda i: attn_all[:, i].reshape(feat, feat)
-    qw, kw, vw, ow = full(0), full(1), full(2), full(3)
-    up = gather(up_weight).reshape(feat, -1)
-    down = gather(down_weight).reshape(-1, feat)
-    wide = jnp.transpose(small_all[:, :8], (1, 0, 2)).reshape(8, feat).astype(f32)
-    ub = small_all[:, 8:].reshape(1, -1).astype(f32)
-    vec1 = wide[0:4]
-    vec2 = wide[4:8]
-    fi, q, k, v = project(tokens, vec1, qw, kw, vw)
+    me = lax.axis_index(FSDP)
+    eight = jnp.stack([first_gain, first_shift, query_bias, value_bias, out_bias, second_gain, second_shift, down_bias])
+    small = jnp.concatenate([spread(eight, me, n), spread(up_bias[None], me, n).reshape(-1, feat)])
+    small = jnp.concatenate([small, jnp.zeros((16 - small.shape[0], feat), bf16)])
+    fi, q, k, v, vec, qkv_all, o_all, up_all, down_all, _ = gather_project(
+        sizes, tokens, small, query_weight, key_weight, value_weight, out_weight, up_weight, down_weight)
+    full = lambda i: qkv_all[:, i * own:(i + 1) * own].reshape(feat, feat)
+    qw, kw, vw = full(0), full(1), full(2)
+    ow = o_all.reshape(feat, feat)
+    up = up_all.reshape(feat, -1)
+    down = down_all.reshape(-1, feat)
+    vec1 = vec[0:8]
+    vec2 = vec[4:12]
+    ub = vec[8:12].reshape(1, -1)
     mixed, lse = attn_fwd(counts, q, k, v)
     layer_out, gres, gmix, gup, gub, gdown, gout, gv2 = middle(counts, mixed, tokens, cotangent, ow, vec2, up, ub, down)
     dq, dk, dv = attn_bwd(counts, q, k, v, gmix, lse)
@@ -350,7 +627,7 @@
     mat = P("fsdp", None)
     vec = P("fsdp")
     return jax.shard_map(
-        on_device,
+        functools.partial(on_device, (mesh.shape["dp"], mesh.shape["fsdp"])),
         mesh=mesh,
         in_specs=(rows, rows, rows, vec, vec, mat, vec, mat, mat, vec, mat, vec, vec, vec, mat, vec, mat, vec),
         out_specs=(rows, rows, vec, vec, mat, vec, mat, mat, vec, mat, vec, vec, vec, mat, vec, mat, vec),

time: 559 us -> 511 us (0.914)
  waiting for transfers between devices: 363 us -> 261 us
  Pallas kernels: 131 us -> 212 us
  blocking collectives: 28.5 us -> 5.05 us
    all_gather x3 -> x0, waiting for transfers between devices: 101 us -> none  [on_device(): gather = lambda a: lax.all_gather(a, FSDP, axis=0, tiled=False)]
    pallas_call x1, Pallas kernels: 8.29 us -> 89.1 us  [gather_project(): pl.pallas_call(functools.partial(gather_kernel, dp_total, n), in_specs=[v...]
    all_gather x1 -> x0, blocking collectives: 23.5 us -> none  [on_device(): gather = lambda a: lax.all_gather(a, FSDP, axis=0, tiled=False)]
  transfers between devices with their start and end apart: 8 -> 5, of which waited for: 8 -> 5; matrix products, arithmetic and copies ran while one was open for 3% -> 2% of each run, Pallas kernels for 15% -> 10%
where the time goes in v2:
time: 511 us
  waiting for transfers between devices  261 us (51%)
  Pallas kernels  212 us (41%)
  between operations  13.9 us (3%)
  local copies, waits for them, and re-layouts  10.5 us (2%)
  other arithmetic  8.1 us (2%)
    reduce_scatter x4, waiting for transfers between devices, on_device(): lax.psum_scatter(a, FSDP, scatter_dimension=0, tiled=False)  228 us
    pallas_call x1, Pallas kernels, gather_project(): pl.pallas_call(functools.partial(gather_kernel, dp_total, n), in_specs=[v...  89.1 us
    pallas_call x1, Pallas kernels, middle(): pl.pallas_call(mid_kernel, grid_spec=pltpu.PrefetchScalarGridSpec(num_sca...  47.5 us
    pallas_call x1, Pallas kernels, attn_bwd(): pl.pallas_call(bwd_kernel, grid_spec=pltpu.PrefetchScalarGridSpec(num_sca...  37.1 us
    psum x1, waiting for transfers between devices, on_device(): pair = lambda a: lax.psum(a, 'dp').astype(f32)  32 us
    pallas_call x1, Pallas kernels, attn_fwd(): pl.pallas_call(fwd_kernel, grid_spec=pltpu.PrefetchScalarGridSpec(num_sca...  23.4 us
    pallas_call x1, Pallas kernels, project_back(): pl.pallas_call(back_kernel, out_shape=[s((rows, D), f32), s((D, D), bf16)...  14.8 us
  transfers between devices with their start and end apart: 5, of which 5 were waited for; matrix products, arithmetic and copies ran while one was open for 2% of the time, Pallas kernels for 10%

profile of v2, /device:TPU:0, one launch (start us, length us, event | category | flops | bytes accessed | tf_op | source)
XLA Modules:
  0.0 510.7 jit_solution(15101121695075248298)
XLA Ops:
  7.2 0.7 broadcast_in_dim.50
  8.2 0.1 iota.12
  8.3 0.8 stack.38
  9.1 0.1 broadcast_in_dim.48
  9.3 0.6 pad_maximum_fusion.2.small_ref
  9.9 89.1 %gather_project.1 = (bf16[1024,768]{1,0:T(8,128)(2,1)}, bf16[1024,768]{1,0:T(8,128)(2,1)}, bf16[1024,768]{1,0:T(8,128)(2,1)}, bf16[1024,768]{1,0:T(8,128)(2,1)},...) custom-call(bf16[1024,768]{1,0:T(8,128)(2,1)} %tokens_ref.5, ...), custom_call_target="tpu_custom_call" | custom-call | tf_op jit(solution)/shard_map/gather_project/pallas_call | solution.py:566
  99.0 0.7 slice_bitcast_fusion.4
  99.8 1.5 fusion.1
  101.3 0.6 copy.40
  101.9 23.4 %attend.1 = (bf16[1024,768]{1,0:T(8,128)(2,1)}, f32[6,2,1024]{2,1,0:T(2,128)}) custom-call(s32[2]{0:T(128)} %bitcast.83, bf16[1024,768]{1,0:T(8,128)(2,1)} %get-tuple-element.44.q_ref, bf16[1024,768]{1,0:T(8,128)(2,1)} %get-tuple-element.45.k_ref, bf16[1024,768]{1,0:T(8,128)(2,1)} %get-tuple-element.46.v_ref), custom_call_target="tpu_custom_call" | custom-call | tf_op jit(solution)/shard_map/attend/pallas_call | solution.py:96
  125.3 47.5 %feed_forward.1 = (bf16[1024,768]{1,0:T(8,128)(2,1)}, f32[1024,768]{1,0:T(8,128)}, bf16[1024,768]{1,0:T(8,128)(2,1)}, bf16[768,3072]{1,0:T(8,128)(2,1)}, f32[1,3...) custom-call(s32[2]{0:T(128)} %bitcast.84, ...), custom_call_target="tpu_custom_call" | custom-call | tf_op jit(solution)/shard_map/feed_forward/pallas_call | solution.py:247
  172.9 0.7 reduce-scatter.11.cloned.1.call-update
  173.6 37.1 %attend_back.1 = (bf16[1024,768]{1,0:T(8,128)(2,1)}, bf16[1024,768]{1,0:T(8,128)(2,1)}, bf16[1024,768]{1,0:T(8,128)(2,1)}) custom-call(s32[2]{0:T(128)} %bitcast.85, bf16[1024,768]{1,0:T(8,128)(2,1)} %get-tuple-element.44.q_ref, bf16[1024,768]{1,0:T(8,128)(2,1)} %get-tuple-element.45.k_ref, bf16[1024,768]{1,0:T(8,128)(2,1)} %get-tuple-element.46.v_ref, ...), custom_call_target="tpu_custom_call" | custom-call | tf_op jit(solution)/shard_map/attend_back/pallas_call | solution.py:151
  210.7 1.9 fusion
  212.6 14.8 %project_back.1 = (f32[1024,768]{1,0:T(8,128)}, bf16[768,768]{1,0:T(8,128)(2,1)}, bf16[768,768]{1,0:T(8,128)(2,1)}, bf16[768,768]{1,0:T(8,128)(2,1)}, f32[8,768]{1,0:T(8,128)}) custom-call(bf16[1024,768]{1,0:T(8,128)(2,1)} %tokens_ref.5, f32[8,768]{1,0:T(8,128)} %get-tuple-element.81.vec_ref, f32[1024,768]{1,0:T(8,128)} %get-tuple-element.53.gres_ref, ...), custom_call_target="tpu_custom_call" | custom-call | tf_op jit(solution)/shard_map/project_back/pallas_call | solution.py:305
  227.5 4.0 pad_maximum_fusion
  231.5 0.7 slice.117
  232.3 0.7 slice.116
  233.2 0.1 reshape.98
  233.3 0.7 pad_maximum_fusion.1
  234.0 15.8 %reduce-scatter.9.cloned.1.call-done = bf16[1,48,3072]{2,1,0:T(8,128)(2,1)} async-done(((bf16[16,48,3072]{2,1,0:T(8,128)(2,1)}), bf16[1,48,3072]{2,1,0:T(8,128)(2,1)}) %reduce-scatter.9.cloned.1.call-update) | async-done | bytes 294928 | tf_op jit(solution)/shard_map/reduce_scatter | solution.py:612
  249.8 79.0 %reduce-scatter.11.cloned.1.call-done = bf16[1,192,768]{2,1,0:T(8,128)(2,1)} async-done(((bf16[16,192,768]{2,1,0:T(8,128)(2,1)}), bf16[1,192,768]{2,1,0:T(8,128)(2,1)}) %reduce-scatter.11.cloned.1.call-update) | async-done | bytes 294928 | tf_op jit(solution)/shard_map/reduce_scatter | solution.py:612
  328.8 78.5 %reduce-scatter.7.cloned.1.call-done = bf16[1,4,48,768]{3,2,1,0:T(8,128)(2,1)} async-done(((bf16[16,4,48,768]{3,2,1,0:T(8,128)(2,1)}), bf16[1,4,48,768]{3,2,1,0:T(8,128)(2,1)}) %reduce-scatter.7.cloned.1.call-update) | async-done | bytes 294928 | tf_op jit(solution)/shard_map/reduce_scatter | solution.py:612
  407.3 55.1 %reduce-scatter.5.cloned.1.call-done = bf16[1,12,48]{2,1,0:T(8,128)(2,1)} async-done(((bf16[16,12,48]{2,1,0:T(8,128)(2,1)}), bf16[1,12,48]{2,1,0:T(8,128)(2,1)}) %reduce-scatter.5.cloned.1.call-update) | async-done | bytes 1168 | tf_op jit(solution)/shard_map/reduce_scatter | solution.py:612
  462.4 5.0 psum.28
  467.4 0.6 reshape.101
  468.1 0.5 slice_bitcast_fusion.5
  468.6 32.0 %all-reduce.3.cloned.1.call-done = (bf16[4,48,768]{2,1,0:T(8,128)(2,1)}, bf16[48,3072]{1,0:T(8,128)(2,1)}, bf16[192,768]{1,0:T(8,128)(2,1)}) async-done(((bf16[4,48,768]{2,1,0:T(8,128)(2,1)}, bf16[48,3072]{1,0:T(8,128)(2,1)}, bf16[192,768]{1,0:T(8,128)(2,1)}), (bf16[4,48,768]{2,1,0:T(8,128)(2,1)}, bf16[48,3072]{1,0:T(8,128)(2,1)}, bf16[192,768]{1,0:T(8,128)(2,1)})) %all-reduce.3.cloned.1.call-update) | async-done | bytes 884752 | tf_op jit(solution)/shard_map/psum | solution.py:613
  500.6 1.1 convert_element_type.14
  501.7 0.8 slice_bitcast_fusion
  502.5 0.9 convert_element_type.15
  503.3 0.9 convert_element_type.16
  (34 shorter events, 0.8 us)
Async XLA Ops:
  7.2 242.6 %reduce-scatter.9.cloned.1.call-start = ((), (), s32[]{:S(2)}) async-start(), calls=%async_computation.6 | async-start | bytes 5013504 | tf_op jit(solution)/shard_map/reduce_scatter | solution.py:612
  172.8 155.9 %reduce-scatter.11.cloned.1.call-start = ((), (), s32[]{:S(2)}) async-start(), calls=%async_computation.7 | async-start | bytes 5013504 | tf_op jit(solution)/shard_map/reduce_scatter | solution.py:612
  173.6 233.7 %reduce-scatter.7.cloned.1.call-start = ((), (), s32[]{:S(2)}) async-start(), calls=%async_computation.5 | async-start | bytes 5013504 | tf_op jit(solution)/shard_map/reduce_scatter | solution.py:612
  173.6 37.1 %copy-start = (bf16[16,144,768]{2,1,0:T(8,128)(2,1)S(1)}, bf16[16,144,768]{2,1,0:T(8,128)(2,1)}, u32[]{:S(2)}) copy-start(bf16[16,144,768]{2,1,0:T(8,128)(2,1)} %get-tuple-element.60) | copy-start | bytes 10616836
  212.6 14.8 %copy-start.1 = (bf16[768,768]{1,0:T(8,128)(2,1)S(1)}, bf16[768,768]{1,0:T(8,128)(2,1)}, u32[]{:S(2)}) copy-start(bf16[768,768]{1,0:T(8,128)(2,1)} %get-tuple-element.68) | copy-start | bytes 3538948
  231.5 1.6 copy-start.4
  231.5 230.9 %reduce-scatter.5.cloned.1.call-start = ((), (), s32[]{:S(2)}) async-start(), calls=%async_computation.4 | async-start | bytes 69632 | tf_op jit(solution)/shard_map/reduce_scatter | solution.py:612
  234.0 266.6 %all-reduce.3.cloned.1.call-start = ((), (), s32[]{:S(2)}) async-start(), calls=%async_computation.8 | async-start | bytes 1769472 | tf_op jit(solution)/shard_map/psum | solution.py:613
  500.6 1.9 copy-start.3
  500.6 2.8 copy-start.2
Sparse Core Ops, SparseCore 0:
  172.9 76.8 reduce-scatter.8
  254.2 74.5 reduce-scatter.10
  332.6 74.5 reduce-scatter.6
  411.4 50.9 reduce-scatter.4
  464.7 35.8 all-reduce.2

commit v3 on v2

--- a/solution.py
+++ b/solution.py
@@ -321,6 +321,7 @@
         self.outer = self.f // (2 * self.inner_total)
         self.side = self.d % 2
         self.twin = self.d + 1 - 2 * self.side
+        self.pairs = dp_total // 2
 
     def index(self, outer, inner, core):
         return (outer * self.inner_total + inner) * 2 + core
@@ -576,6 +577,286 @@
         name="gather_project",
     )(tokens, small, qw, kw, vw, ow, up, down)
 
+
+def plan_neighbours(place):
+    out = place.neighbours()
+    out += [(place.side + 2 * ((place.d // 2 + k) % place.pairs), place.f) for k in range(1, place.pairs)]
+    return out
+
+
+def greet_all(place):
+    barrier = pltpu.get_barrier_semaphore()
+    others = plan_neighbours(place)
+    for other in others:
+        pl.semaphore_signal(barrier, inc=1, device_id=other, device_id_type=MESH)
+    pl.semaphore_wait(barrier, len(others))
+
+
+def scatter_copies(A, B, pairs):
+    return 1 + 1 + (B - 1) + (A - 1) + 1 + (pairs - 1)
+
+
+def scatter_shapes(A, B, pairs, rows, width, edge):
+    out = [pltpu.VMEM((A, B, rows, width), bf16), pltpu.VMEM((A, B, rows, edge), bf16),
+           pltpu.VMEM((B - 1, A, rows, width), bf16), pltpu.VMEM((A - 1, rows, width), bf16),
+           pltpu.VMEM((rows, width), bf16)]
+    if pairs > 1:
+        out += [pltpu.VMEM((rows, width), bf16), pltpu.VMEM((pairs - 1, rows, width), bf16)]
+    return out
+
+
+class Scatter:
+    def __init__(self, place, terms, bufs, edge, out, sems, base):
+        self.place, self.terms, self.edge, self.out = place, terms, edge, out
+        self.sums, self.from_twin_buf, self.from_inner_buf, self.from_outer_buf, self.last_buf = bufs[:5]
+        self.pair_bufs = bufs[5:]
+        self.width = terms.shape[-1]
+        self.rows = terms.shape[-2]
+        self.send_sem, self.recv_sem = sems
+        self.base = base
+        self.sent = []
+        p = place.side
+        e, w = edge, self.width
+        at = lambda start, size: pl.ds(pl.multiple_of(start, 128), size)
+        self.plane = at(p * e, w - e)
+        self.mine = at(p * (w - e), e)
+        self.theirs = at((1 - p) * (w - e), e)
+        self.twin_plane = at((1 - p) * e, w - e)
+        self.middle = pl.ds(e, w - 2 * e)
+
+    def copy(self, i, src, dst, to):
+        return pltpu.make_async_remote_copy(src_ref=src, dst_ref=dst, send_sem=self.send_sem.at[self.base + i],
+                                            recv_sem=self.recv_sem.at[self.base + i], device_id=to, device_id_type=MESH)
+
+    def send(self, i, src, dst, to):
+        c = self.copy(i, src, dst, to)
+        c.start()
+        self.sent.append(c)
+
+    def got(self, i, dst):
+        self.copy(i, dst, dst, (self.place.d, self.place.f)).wait_recv()
+
+    def start(self):
+        p = self.place
+        self.send(0, self.terms.at[:, :, 1 - p.core], self.sums, (p.d, p.slot(0, 0, 1 - p.core)))
+
+    def from_core(self):
+        p = self.place
+        self.got(0, self.sums)
+        B = p.inner_total
+
+        def add(i, _):
+            a, b = i // B, i % B
+            self.sums[a, b] = (self.sums[a, b].astype(f32) + self.terms[a, b, p.core].astype(f32)).astype(bf16)
+            return 0
+
+        lax.fori_loop(0, p.outer_total * B, add, 0)
+        self.send(1, self.sums.at[:, :, :, self.theirs], self.from_twin_buf, (p.twin, p.f))
+
+    def from_twin(self):
+        p = self.place
+        B = p.inner_total
+        self.got(1, self.from_twin_buf)
+
+        def add(i, _):
+            a, b = i // B, i % B
+            self.sums[a, b, :, self.mine] = (self.sums[a, b, :, self.mine].astype(f32)
+                                             + self.from_twin_buf[a, b].astype(f32)).astype(bf16)
+            return 0
+
+        lax.fori_loop(0, p.outer_total * B, add, 0)
+        for t in range(1, B):
+            to = (p.inner + B - t) % B
+            self.send(1 + t, self.sums.at[:, to, :, self.plane], self.from_inner_buf.at[t - 1, :, :, self.plane],
+                      (p.d, p.slot(0, -t)))
+
+    def from_inner(self):
+        p = self.place
+        A, B = p.outer_total, p.inner_total
+        for t in range(1, B):
+            self.got(1 + t, self.from_inner_buf.at[t - 1, :, :, self.plane])
+
+        def add(a, _):
+            total = self.sums[a, p.inner, :, self.plane].astype(f32)
+            for t in range(1, B):
+                total = total + self.from_inner_buf[t - 1, a, :, self.plane].astype(f32)
+            self.sums[a, p.inner, :, self.plane] = total.astype(bf16)
+            return 0
+
+        lax.fori_loop(0, A, add, 0)
+        for s in range(1, A):
+            to = (p.outer + A - s) % A
+            self.send(B + s, self.sums.at[to, p.inner, :, self.plane], self.from_outer_buf.at[s - 1, :, self.plane],
+                      (p.d, p.slot(-s, 0)))
+
+    def from_outer(self):
+        p = self.place
+        A, B = p.outer_total, p.inner_total
+        for s in range(1, A):
+            self.got(B + s, self.from_outer_buf.at[s - 1, :, self.plane])
+        total = self.sums[p.outer, p.inner, :, self.plane].astype(f32)
+        for s in range(1, A):
+            total = total + self.from_outer_buf[s - 1, :, self.plane].astype(f32)
+        self.sums[p.outer, p.inner, :, self.plane] = total.astype(bf16)
+        self.send(A + B, self.sums.at[p.outer, p.inner, :, self.plane], self.last_buf.at[:, self.plane],
+                  (p.twin, p.f))
+
+    def from_last(self):
+        p = self.place
+        A, B = p.outer_total, p.inner_total
+        self.got(A + B, self.last_buf.at[:, self.twin_plane])
+        own = lambda cols: self.sums[p.outer, p.inner, :, cols].astype(f32)
+        last = lambda cols: self.last_buf[:, cols].astype(f32)
+        if p.pairs == 1:
+            self.out[:, self.mine] = own(self.mine)
+            self.out[:, self.middle] = own(self.middle) + last(self.middle)
+            self.out[:, self.theirs] = last(self.theirs)
+            return
+        half, others = self.pair_bufs
+        half[:, self.mine] = own(self.mine).astype(bf16)
+        half[:, self.middle] = (own(self.middle) + last(self.middle)).astype(bf16)
+        half[:, self.theirs] = last(self.theirs).astype(bf16)
+        for k in range(1, p.pairs):
+            to = p.side + 2 * ((p.d // 2 + p.pairs - k) % p.pairs)
+            self.send(A + B + k, half, others.at[k - 1], (to, p.f))
+
+    def from_pairs(self):
+        p = self.place
+        if p.pairs == 1:
+            return
+        half, others = self.pair_bufs
+        total = half[...].astype(f32)
+        for k in range(1, p.pairs):
+            self.got(p.outer_total + p.inner_total + k, others.at[k - 1])
+            total = total + others[k - 1].astype(f32)
+        self.out[...] = total
+
+    def steps(self):
+        return [self.start, self.from_core, self.from_twin, self.from_inner, self.from_outer, self.from_last,
+                self.from_pairs]
+
+    def finish(self):
+        for c in self.sent:
+            c.wait_send()
+
+
+class Total:
+    def __init__(self, place, value, bufs, out, sems, base):
+        self.place, self.value, self.bufs, self.out = place, value, bufs, out
+        self.send_sem, self.recv_sem = sems
+        p = place
+        core = [(p.d, p.slot(0, 0, 1 - p.core))]
+        inner = [(p.d, p.slot(0, t)) for t in range(1, p.inner_total)]
+        outer = [(p.d, p.slot(s, 0)) for s in range(1, p.outer_total)]
+        twin = [(p.twin, p.f)]
+        pairs = [(p.side + 2 * ((p.d // 2 + k) % p.pairs), p.f) for k in range(1, p.pairs)]
+        back = [(p.d, p.slot(0, -t)) for t in range(1, p.inner_total)]
+        self.rounds = [r for r in (core, inner, outer, twin, pairs) if r]
+        self.base = base
+        self.sent = []
+
+    @staticmethod
+    def copies(A, B, pairs):
+        return 1 + (B - 1) + (A - 1) + 1 + (pairs - 1)
+
+    @staticmethod
+    def shapes(A, B, pairs, shape):
+        n = Total.copies(A, B, pairs)
+        return [pltpu.VMEM((n,) + shape, f32), pltpu.VMEM((5,) + shape, f32)]
+
+    def send_round(self, r):
+        landing, held = self.bufs
+        i = sum(len(x) for x in self.rounds[:r])
+        for k, to in enumerate(self.rounds[r]):
+            c = pltpu.make_async_remote_copy(src_ref=held.at[r], dst_ref=landing.at[i + k],
+                                             send_sem=self.send_sem.at[self.base + i + k],
+                                             recv_sem=self.recv_sem.at[self.base + i + k], device_id=to,
+                                             device_id_type=MESH)
+            c.start()
+            self.sent.append(c)
+
+    def start(self):
+        self.bufs[1][0] = self.value[...]
+        self.send_round(0)
+
+    def step(self, r):
+        landing, held = self.bufs
+        i = sum(len(x) for x in self.rounds[:r])
+        p = self.place
+        total = held[r]
+        for k in range(len(self.rounds[r])):
+            pltpu.make_async_remote_copy(src_ref=held.at[r], dst_ref=landing.at[i + k],
+                                         send_sem=self.send_sem.at[self.base + i + k],
+                                         recv_sem=self.recv_sem.at[self.base + i + k], device_id=(p.d, p.f),
+                                         device_id_type=MESH).wait_recv()
+            total = total + landing[i + k]
+        if r + 1 < len(self.rounds):
+            held[r + 1] = total
+            self.send_round(r + 1)
+        else:
+            self.out[...] = total
+
+    def steps(self):
+        return [self.start] + [functools.partial(self.step, r) for r in range(len(self.rounds))]
+
+    def finish(self):
+        for c in self.sent:
+            c.wait_send()
+
+
+def reduce_kernel(dp_total, n, edges, *refs):
+    place = Place(dp_total, n)
+    A, B, pairs = place.outer_total, place.inner_total, place.pairs
+    k = len(edges)
+    small_ref = refs[0]
+    terms = refs[1:1 + k]
+    small_out = refs[1 + k]
+    outs = refs[2 + k:2 + 2 * k]
+    rest = refs[2 + 2 * k:]
+    per = 5 if pairs == 1 else 7
+    send_sem, recv_sem = rest[-2:]
+    sems = (send_sem, recv_sem)
+    greet_all(place)
+    base = 0
+    units = []
+    for i in range(k):
+        units.append(Scatter(place, terms[i], rest[i * per:(i + 1) * per], edges[i], outs[i], sems, base))
+        base += scatter_copies(A, B, pairs)
+    small = Total(place, small_ref, rest[k * per:k * per + 2], small_out, sems, base)
+    chains = [u.steps() for u in units] + [small.steps()]
+    depth = max(len(c) for c in chains)
+    for tick in range(len(chains) + depth):
+        for i, c in enumerate(chains):
+            if 0 <= tick - i < len(c):
+                c[tick - i]()
+    for u in units + [small]:
+        u.finish()
+
+
+def reduce_all(sizes, small, terms, edges):
+    dp_total, n = sizes
+    half = n // 2
+    A = 4 if half % 4 == 0 else half
+    B = half // A
+    pairs = dp_total // 2
+    k = len(terms)
+    terms = [t.reshape(A, B, 2, *t.shape[1:]) for t in terms]
+    scratch = []
+    for t, e in zip(terms, edges):
+        scratch += scatter_shapes(A, B, pairs, t.shape[-2], t.shape[-1], e)
+    scratch += Total.shapes(A, B, pairs, small.shape)
+    copies = k * scatter_copies(A, B, pairs) + Total.copies(A, B, pairs)
+    scratch += [pltpu.SemaphoreType.DMA((copies,))] * 2
+    vm = pl.BlockSpec(memory_space=pltpu.VMEM)
+    return pl.pallas_call(
+        functools.partial(reduce_kernel, dp_total, n, edges),
+        in_specs=[vm] * (k + 1), out_specs=[vm] * (k + 1),
+        out_shape=[jax.ShapeDtypeStruct(small.shape, f32)] + [jax.ShapeDtypeStruct(t.shape[-2:], f32) for t in terms],
+        scratch_shapes=scratch,
+        compiler_params=pltpu.CompilerParams(collective_id=2, has_side_effects=True, vmem_limit_bytes=62 * 2**20),
+        name="reduce_gradients",
+    )(small, *terms)
+
 FSDP="fsdp"
 
 def spread(vectors, index, total):
@@ -609,17 +890,20 @@
     layer_out, gres, gmix, gup, gub, gdown, gout, gv2 = middle(counts, mixed, tokens, cotangent, ow, vec2, up, ub, down)
     dq, dk, dv = attn_bwd(counts, q, k, v, gmix, lse)
     gtok, gq, gk, gv, gv1 = project_back(tokens, vec1, gres, fi, dq, dk, dv, qw, kw, vw)
-    scatter = lambda a: lax.psum_scatter(a, FSDP, scatter_dimension=0, tiled=False)
-    pair = lambda a: lax.psum(a, "dp").astype(f32)
-    su = scatter(gup.reshape(n, own, -1))
-    sd = scatter(gdown.reshape(n, -1, feat))
-    sa = scatter(jnp.stack([g.reshape(n, own, feat) for g in (gq, gk, gv, gout)], axis=1))
-    smalls = jnp.concatenate([gv1[0:4], gv2[0:4]]).reshape(8, n, own)
-    smalls = jnp.concatenate([jnp.transpose(smalls, (1, 0, 2)), gub.reshape(n, -1, own)], axis=1).astype(bf16)
-    ss = scatter(smalls)
-    su, sd, sa, ss = (pair(a) for a in (su, sd, sa, ss))
-    return (layer_out, gtok, ss[0], ss[1], sa[0], ss[2], sa[1], sa[2], ss[3], sa[3], ss[7], ss[5], ss[6], su,
-            ss[8:].reshape(-1), sd, ss[4])
+    smalls = jnp.concatenate([gv1[0:4], gv2[0:4], gub.reshape(-1, feat)])
+    smalls = jnp.concatenate([smalls, jnp.zeros((16 - smalls.shape[0], feat), f32)])
+    cut = lambda g: g.reshape(n, -1, g.shape[1])
+    gdown3 = cut(gdown)
+    gup3 = cut(gup)
+    half_down = gdown3.shape[1] // 2
+    half_up = gup3.shape[2] // 2
+    terms = [gdown3[:, :half_down], gdown3[:, half_down:], gup3[:, :, :half_up], gup3[:, :, half_up:], cut(gout), cut(gq), cut(gk), cut(gv)]
+    edges = (128, 128, 384, 384, 256, 256, 256, 256)
+    total, d0, d1, u0, u1, go, gq, gk, gv = reduce_all(sizes, smalls, terms, edges)
+    mine = lax.dynamic_index_in_dim(total[:8].reshape(8, n, own), me, 1, keepdims=False)
+    ub_mine = lax.dynamic_index_in_dim(total[8:12].reshape(n, -1), me, 0, keepdims=False)
+    return (layer_out, gtok, mine[0], mine[1], gq, mine[2], gk, gv, mine[3], go, mine[7], mine[5], mine[6],
+            jnp.concatenate([u0, u1], axis=1), ub_mine, jnp.concatenate([d0, d1]), mine[4])
 
 
 def solution(mesh):

time: 511 us -> 360 us (0.70)
  waiting for transfers between devices: 261 us -> 0 us
  Pallas kernels: 212 us -> 329 us
  between operations: 13.9 us -> 1.27 us
  local copies, waits for them, and re-layouts: 10.5 us -> 18.3 us
    reduce_scatter x4 -> x0, waiting for transfers between devices: 228 us -> none  [on_device(): lax.psum_scatter(a, FSDP, scatter_dimension=0, tiled=False)]
    pallas_call x0 -> x1, Pallas kernels: none -> 112 us  [reduce_all(): pl.pallas_call(functools.partial(reduce_kernel, dp_total, n, edges), in_s...]
    psum x1 -> x0, waiting for transfers between devices: 32 us -> none  [on_device(): pair = lambda a: lax.psum(a, 'dp').astype(f32)]
    slice x3 -> x6, local copies, waits for them, and re-layouts: 1.49 us -> 8.6 us  [the longest x1 5.08 us: on_device(): gdown3[:, half_down:]]
  transfers between devices with their start and end apart: 5 -> 0, of which waited for: 5 -> 0; matrix products, arithmetic and copies ran while one was open for 2% -> 0% of each run, Pallas kernels for 10% -> 0%
where the time goes in v3:
time: 360 us; the launch traced here: 355 us
  Pallas kernels  329 us (91%)
  local copies, waits for them, and re-layouts  18.3 us (5%)
  other arithmetic  5.9 us (2%)
    pallas_call x1, Pallas kernels, reduce_all(): pl.pallas_call(functools.partial(reduce_kernel, dp_total, n, edges), in_s...  112 us
    pallas_call x1, Pallas kernels, gather_project(): pl.pallas_call(functools.partial(gather_kernel, dp_total, n), in_specs=[v...  89.1 us
    pallas_call x1, Pallas kernels, middle(): pl.pallas_call(mid_kernel, grid_spec=pltpu.PrefetchScalarGridSpec(num_sca...  47.5 us
    pallas_call x1, Pallas kernels, attn_bwd(): pl.pallas_call(bwd_kernel, grid_spec=pltpu.PrefetchScalarGridSpec(num_sca...  40.1 us
    pallas_call x1, Pallas kernels, attn_fwd(): pl.pallas_call(fwd_kernel, grid_spec=pltpu.PrefetchScalarGridSpec(num_sca...  25.9 us
    pallas_call x1, Pallas kernels, project_back(): pl.pallas_call(back_kernel, out_shape=[s((rows, D), f32), s((D, D), bf16)...  14.7 us

profile of v3, /device:TPU:0, one launch (start us, length us, event | category | flops | bytes accessed | tf_op | source)
XLA Modules:
  0.0 354.7 jit_solution(2982285826620224838)
XLA Ops:
  0.7 0.1 broadcast_in_dim.48
  0.8 0.8 stack.35
  1.6 0.1 broadcast_in_dim.51
  1.8 0.1 iota.12
  1.9 0.7 broadcast_in_dim.53
  2.6 0.1 broadcast_in_dim.54
  2.7 0.6 pad_maximum_fusion.2.small_ref
  3.3 89.1 %gather_project.1 = (bf16[1024,768]{1,0:T(8,128)(2,1)}, bf16[1024,768]{1,0:T(8,128)(2,1)}, bf16[1024,768]{1,0:T(8,128)(2,1)}, bf16[1024,768]{1,0:T(8,128)(2,1)},...) custom-call(bf16[1024,768]{1,0:T(8,128)(2,1)} %tokens_ref.5, ...), custom_call_target="tpu_custom_call" | custom-call | tf_op jit(solution)/shard_map/gather_project/pallas_call | solution.py:567
  92.4 25.9 %attend.1 = (bf16[1024,768]{1,0:T(8,128)(2,1)}, f32[6,2,1024]{2,1,0:T(2,128)}) custom-call(s32[2]{0:T(128)} %bitcast.67, bf16[1024,768]{1,0:T(8,128)(2,1)} %get-tuple-element.53.q_ref, bf16[1024,768]{1,0:T(8,128)(2,1)} %get-tuple-element.54.k_ref, bf16[1024,768]{1,0:T(8,128)(2,1)} %get-tuple-element.55.v_ref), custom_call_target="tpu_custom_call" | custom-call | tf_op jit(solution)/shard_map/attend/pallas_call | solution.py:96
  118.3 0.6 fusion.11
  119.0 0.6 copy.35
  119.6 47.5 %feed_forward.1 = (bf16[1024,768]{1,0:T(8,128)(2,1)}, f32[1024,768]{1,0:T(8,128)}, bf16[1024,768]{1,0:T(8,128)(2,1)}, bf16[768,3072]{1,0:T(8,128)(2,1)}, f32[1,3...) custom-call(s32[2]{0:T(128)} %bitcast.68, ...), custom_call_target="tpu_custom_call" | custom-call | tf_op jit(solution)/shard_map/feed_forward/pallas_call | solution.py:247
  167.0 40.1 %attend_back.1 = (bf16[1024,768]{1,0:T(8,128)(2,1)}, bf16[1024,768]{1,0:T(8,128)(2,1)}, bf16[1024,768]{1,0:T(8,128)(2,1)}) custom-call(s32[2]{0:T(128)} %bitcast.69, bf16[1024,768]{1,0:T(8,128)(2,1)} %get-tuple-element.53.q_ref, bf16[1024,768]{1,0:T(8,128)(2,1)} %get-tuple-element.54.k_ref, bf16[1024,768]{1,0:T(8,128)(2,1)} %get-tuple-element.55.v_ref, ...), custom_call_target="tpu_custom_call" | custom-call | tf_op jit(solution)/shard_map/attend_back/pallas_call | solution.py:151
  207.1 1.8 fusion.10
  209.0 14.7 %project_back.1 = (f32[1024,768]{1,0:T(8,128)}, bf16[768,768]{1,0:T(8,128)(2,1)}, bf16[768,768]{1,0:T(8,128)(2,1)}, bf16[768,768]{1,0:T(8,128)(2,1)}, f32[8,768]{1,0:T(8,128)}) custom-call(bf16[1024,768]{1,0:T(8,128)(2,1)} %tokens_ref.5, f32[8,768]{1,0:T(8,128)} %get-tuple-element.104.vec_ref, f32[1024,768]{1,0:T(8,128)} %get-tuple-element.62.gres_ref, ...), custom_call_target="tpu_custom_call" | custom-call | tf_op jit(solution)/shard_map/project_back/pallas_call | solution.py:305
  223.6 0.7 slice.80
  224.4 0.5 broadcast.29
  224.9 0.7 reduce.3
  225.7 0.7 maximum_maximum_fusion.refs_0_
  226.4 5.1 %fusion.9 = (bf16[16,96,768]{2,1,0:T(8,128)(2,1)}, bf16[16,96,768]{2,1,0:T(8,128)(2,1)}) fusion(bf16[16,192,768]{2,1,0:T(8,128)(2,1)} %bitcast.57), kind=kLoop, calls=%fused_computation.26 | loop fusion | bytes 9437184 | tf_op jit(solution)/shard_map/slice | solution.py:900
  231.5 2.8 fusion.8
  234.2 112.1 %reduce_gradients.1 = (f32[16,768]{1,0:T(8,128)}, f32[96,768]{1,0:T(8,128)}, f32[96,768]{1,0:T(8,128)}, f32[48,1536]{1,0:T(8,128)}, f32[48,1536]{1,0:T(8,128)}, ...) custom-call(f32[16,768]{1,0:T(8,128)} %maximum_maximum_fusion.refs_0_, ...), custom_call_target="tpu_custom_call" | custom-call | tf_op jit(solution)/shard_map/reduce_gradients/pallas_call | solution.py:851
  346.5 2.0 pad_maximum_fusion.1
  348.4 1.9 pad_maximum_fusion
  350.3 0.1 reshape.131
  350.4 0.6 fusion
  351.0 0.1 reshape.132
  351.1 0.6 constant_dynamic-slice_fusion.7
  351.7 0.7 copy.40
  352.3 0.7 copy.41
  353.0 0.7 copy.42
  353.6 0.7 copy.43
  (37 shorter events, 0.3 us)
Async XLA Ops:
  92.4 25.9 %copy-start.5 = (f32[16,768]{1,0:T(8,128)S(1)}, f32[16,768]{1,0:T(8,128)}, u32[]{:S(2)}) copy-start(f32[16,768]{1,0:T(8,128)} %get-tuple-element.58) | copy-start | bytes 147460
  167.0 40.1 %copy-start = (bf16[16,144,768]{2,1,0:T(8,128)(2,1)S(1)}, bf16[16,144,768]{2,1,0:T(8,128)(2,1)}, u32[]{:S(2)}) copy-start(bf16[16,144,768]{2,1,0:T(8,128)(2,1)} %get-tuple-element.69) | copy-start | bytes 10616836
  209.0 15.9 %copy-start.7 = (f32[1,3072]{1,0:T(1,128)S(1)}, f32[1,3072]{1,0:T(1,128)}, u32[]{:S(2)}) copy-start(f32[1,3072]{1,0:T(1,128)} %get-tuple-element.73) | copy-start | bytes 36868
  209.0 16.6 %copy-start.8 = (f32[8,768]{1,0:T(8,128)S(1)}, f32[8,768]{1,0:T(8,128)}, u32[]{:S(2)}) copy-start(f32[8,768]{1,0:T(8,128)} %get-tuple-element.72) | copy-start | bytes 73732
  226.4 5.1 %slice-start = ((s8[4718592]{0:T(1024)(128)(4,1)}), s8[4194304]{0:T(1024)(128)(4,1)S(1)}, s32[]{:S(2)}) async-start(s8[4718592]{0:T(1024)(128)(4,1)} %bitcast.54), calls=%async_computation | async-start | bytes 8388608
  226.4 5.1 %slice-start.1 = ((s8[4718592]{0:T(1024)(128)(4,1)}), s8[524288]{0:T(1024)(128)(4,1)S(1)}, s32[]{:S(2)}) async-start(s8[4718592]{0:T(1024)(128)(4,1)} %bitcast.54), calls=%async_computation.1 | async-start | bytes 1048576
  346.4 3.9 %copy-start.6 = (f32[16,768]{1,0:T(8,128)S(1)}, f32[16,768]{1,0:T(8,128)}, u32[]{:S(2)}) copy-start(f32[16,768]{1,0:T(8,128)} %get-tuple-element.80) | copy-start | bytes 147460
  346.4 5.2 %copy-start.4 = (f32[48,768]{1,0:T(8,128)S(1)}, f32[48,768]{1,0:T(8,128)}, u32[]{:S(2)}) copy-start(f32[48,768]{1,0:T(8,128)} %get-tuple-element.127) | copy-start | bytes 442372
  346.4 5.9 %copy-start.3 = (f32[48,768]{1,0:T(8,128)S(1)}, f32[48,768]{1,0:T(8,128)}, u32[]{:S(2)}) copy-start(f32[48,768]{1,0:T(8,128)} %get-tuple-element.129) | copy-start | bytes 442372
  346.4 6.6 %copy-start.2 = (f32[48,768]{1,0:T(8,128)S(1)}, f32[48,768]{1,0:T(8,128)}, u32[]{:S(2)}) copy-start(f32[48,768]{1,0:T(8,128)} %get-tuple-element.130) | copy-start | bytes 442372
  346.4 7.2 %copy-start.1 = (f32[48,768]{1,0:T(8,128)S(1)}, f32[48,768]{1,0:T(8,128)}, u32[]{:S(2)}) copy-start(f32[48,768]{1,0:T(8,128)} %get-tuple-element.132) | copy-start | bytes 442372

commit v4 on v3

--- a/solution.py
+++ b/solution.py
@@ -312,8 +312,10 @@
 class Place:
     def __init__(self, dp_total, fsdp_total):
         half = fsdp_total // 2
-        self.outer_total = 4 if half % 4 == 0 else half
-        self.inner_total = half // self.outer_total
+        self.outer_total = 4
+        self.inner_total = half // 4
+        assert half % 4 == 0
+        self.pairs = dp_total // 2
         self.d = lax.axis_index("dp")
         self.f = lax.axis_index("fsdp")
         self.core = self.f % 2
@@ -321,7 +323,17 @@
         self.outer = self.f // (2 * self.inner_total)
         self.side = self.d % 2
         self.twin = self.d + 1 - 2 * self.side
-        self.pairs = dp_total // 2
+        self.flip = self.outer // 2
+        self.mirror = self.unmirror(self.outer)
+
+    def unmirror(self, at):
+        return at + self.flip * (3 - 2 * at)
+
+    def arrival(self, step):
+        return self.unmirror(step - self.mirror if step == 1 else step)
+
+    def at_outer(self, outer):
+        return (self.d, self.index(outer, self.inner, self.core))
 
     def index(self, outer, inner, core):
         return (outer * self.inner_total + inner) * 2 + core
@@ -337,9 +349,8 @@
         return out
 
 
-def greet(place):
+def greet(others):
     barrier = pltpu.get_barrier_semaphore()
-    others = place.neighbours()
     for other in others:
         pl.semaphore_signal(barrier, inc=1, device_id=other, device_id_type=MESH)
     pl.semaphore_wait(barrier, len(others))
@@ -351,25 +362,18 @@
         self.send_sem, self.recv_sem = sems
         A, B = place.outer_total, place.inner_total
         self.base = base
-        self.keys = {}
-        for s in range(1, A):
-            self.keys["z", s] = len(self.keys)
-        for s in range(A):
-            for t in range(1, B):
-                self.keys["x", s, t] = len(self.keys)
+        keys = [("z", s) for s in range(1, A)] + [("Z", s) for s in range(1, A)]
+        keys += [("x", s, t) for s in range(A) for t in range(1, B)]
         if edge:
-            for s in range(A):
-                for t in range(B):
-                    if s or t:
-                        self.keys["y", s, t] = len(self.keys)
-        for s in range(A):
-            for t in range(B):
-                self.keys["c", s, t] = len(self.keys)
+            keys += [("y", s, t) for s in range(A) for t in range(B) if s or t]
+        keys += [("c", s, t) for s in range(A) for t in range(B)]
+        self.keys = {key: i for i, key in enumerate(keys)}
         self.sent = []
+        self.sent_inside = []
 
     @staticmethod
     def count(A, B, edge):
-        return (A - 1) + A * (B - 1) + (A * B - 1 if edge else 0) + A * B
+        return 2 * (A - 1) + A * (B - 1) + (A * B - 1 if edge else 0) + A * B
 
     def part(self, slot, kind):
         if not self.edge:
@@ -385,72 +389,102 @@
 
     def copy(self, key, ref, to):
         i = self.base + self.keys[key]
+        into = i
+        if key[0] == "Z":
+            into = self.base + self.keys["z", 2 if key[1] == 2 else 3]
         return pltpu.make_async_remote_copy(src_ref=ref, dst_ref=ref, send_sem=self.send_sem.at[i],
-                                            recv_sem=self.recv_sem.at[i], device_id=to, device_id_type=MESH)
-
-    def send(self, key, ref, to):
-        c = self.copy(key, ref, to)
-        c.start()
-        self.sent.append(c)
+                                            recv_sem=self.recv_sem.at[into], device_id=to, device_id_type=MESH)
+
+    def send(self, key, make):
+        self.copy(key, *make()).start()
+        self.sent.append((key, make))
+
+    def send_inside(self, key, make):
+        @pl.when(self.place.mirror == 1)
+        def _():
+            self.copy(key, *make()).start()
+
+        self.sent_inside.append((key, make))
 
     def got(self, key, ref):
         self.copy(key, ref, (self.place.d, self.place.f)).wait_recv()
 
+    def slot_of(self, step, t, core):
+        p = self.place
+        outer = p.outer if step == 0 else p.arrival(step)
+        return p.index(outer, (p.inner + t) % p.inner_total, core)
+
     def start_outer(self):
         p = self.place
-        for s in range(1, p.outer_total):
-            self.send(("z", s), self.part(p.f, "plane"), (p.d, p.slot(-s, 0)))
-
-    def pass_inner(self, s):
-        p = self.place
-        for t in range(1, p.inner_total):
-            self.send(("x", s, t), self.part(p.slot(s, 0), "plane"), (p.d, p.slot(0, -t)))
-
-    def pass_twin(self, s, t):
-        p = self.place
-        if self.edge:
-            self.send(("y", s, t), self.part(p.slot(s, t), "mine"), (p.twin, p.f))
-
-    def pass_core(self, s, t):
-        p = self.place
-        self.send(("c", s, t), self.part(p.slot(s, t), "all"), (p.d, p.slot(0, 0, 1 - p.core)))
+        self.send(("z", 1), lambda: (self.part(p.f, "plane"), p.at_outer(p.unmirror(1 - p.mirror))))
+        self.send_inside(("z", 2), lambda: (self.part(p.f, "plane"), p.at_outer(p.unmirror(2))))
 
     def start_inner(self):
         self.pass_inner(0)
         self.pass_core(0, 0)
 
+    def start(self):
+        self.start_outer()
+        self.start_inner()
+
+    def from_outer_step(self, step):
+        p = self.place
+        self.got(("z", step), self.part(self.slot_of(step, 0, p.core), "plane"))
+        self.send_inside(("Z", step), lambda: (self.part(self.slot_of(step, 0, p.core), "plane"),
+                                               p.at_outer(p.unmirror(2 if step == 1 else 0))))
+        self.pass_inner(step)
+        self.pass_twin(step, 0)
+
     def from_outer(self):
-        p = self.place
-        for s in range(1, p.outer_total):
-            self.got(("z", s), self.part(p.slot(s, 0), "plane"))
-            self.pass_inner(s)
-            self.pass_twin(s, 0)
+        for step in range(1, self.place.outer_total):
+            self.from_outer_step(step)
+
+    def pass_inner(self, step):
+        p = self.place
+        for t in range(1, p.inner_total):
+            self.send(("x", step, t), lambda t=t: (self.part(self.slot_of(step, 0, p.core), "plane"),
+                                                   (p.d, p.slot(0, -t))))
+
+    def pass_twin(self, step, t):
+        p = self.place
+        if self.edge:
+            self.send(("y", step, t), lambda: (self.part(self.slot_of(step, t, p.core), "mine"), (p.twin, p.f)))
+
+    def pass_core(self, step, t):
+        p = self.place
+        self.send(("c", step, t), lambda: (self.part(self.slot_of(step, t, p.core), "all"),
+                                           (p.d, p.slot(0, 0, 1 - p.core))))
 
     def from_inner(self):
         p = self.place
-        for s in range(p.outer_total):
+        for step in range(p.outer_total):
             for t in range(1, p.inner_total):
-                self.got(("x", s, t), self.part(p.slot(s, t), "plane"))
-                self.pass_twin(s, t)
+                self.got(("x", step, t), self.part(self.slot_of(step, t, p.core), "plane"))
+                self.pass_twin(step, t)
 
     def from_twin(self):
         p = self.place
-        for s in range(p.outer_total):
+        for step in range(p.outer_total):
             for t in range(p.inner_total):
-                if s or t:
+                if step or t:
                     if self.edge:
-                        self.got(("y", s, t), self.part(p.slot(s, t), "theirs"))
-                    self.pass_core(s, t)
+                        self.got(("y", step, t), self.part(self.slot_of(step, t, p.core), "theirs"))
+                    self.pass_core(step, t)
 
     def from_core(self):
         p = self.place
-        for s in range(p.outer_total):
+        for step in range(p.outer_total):
             for t in range(p.inner_total):
-                self.got(("c", s, t), self.part(p.slot(s, t, 1 - p.core), "all"))
+                self.got(("c", step, t), self.part(self.slot_of(step, t, 1 - p.core), "all"))
 
     def finish(self):
-        for c in self.sent:
-            c.wait_send()
+        for key, make in self.sent:
+            self.copy(key, *make()).wait_send()
+
+        @pl.when(self.place.mirror == 1)
+        def _():
+            for key, make in self.sent_inside:
+                self.copy(key, *make()).wait_send()
 
 
 def local(src, dst, sem):
@@ -459,137 +493,188 @@
     return c
 
 
-def gather_kernel(dp_total, fsdp_total, tokens_ref, small_ref, qo_ref, ko_ref, vo_ref, oo_ref, uo_ref, do_ref,
-                  fi_ref, q_ref, k_ref, v_ref, vec_ref, qkv_all, o_all, up_all, down_all, small_all,
-                  w_s, small_s, send_sem, recv_sem, loc_sem):
+def attend_block(counts_ref, q_ref, k_ref, v_ref, mixed_ref, lse_ref, pair, block):
+    rows = q_ref.shape[0]
+    lane = lax.broadcasted_iota(jnp.int32, (QB, 128), 1)
+    first = pl.multiple_of(block * QB, QB)
+    cols = pl.ds(pl.multiple_of(pair * 128, 128), 128)
+    q = q_ref[pl.ds(first, QB), cols]
+    k = k_ref[:, cols]
+    v = v_ref[:, cols]
+    ends = image_ends(counts_ref[0], counts_ref[1], rows)
+    rid = image_of(first + lax.broadcasted_iota(jnp.int32, (QB, 1), 0), ends)
+    cid = image_of(lax.broadcasted_iota(jnp.int32, (1, rows), 1), ends)
+    bias = jnp.where(rid == cid, 0.0, NEG)
+    outs = []
+    lses = []
+    for e in range(2):
+        qm = jnp.where((lane < 64) == (e == 0), q, jnp.zeros_like(q))
+        s = dot_nt(qm, k) + bias
+        m = jnp.max(s, axis=1, keepdims=True)
+        p = jnp.exp(s - m)
+        l = jnp.sum(p, axis=1, keepdims=True)
+        o = dot(p.astype(bf16), v)
+        outs.append(o * (1.0 / l))
+        lses.append(m + jnp.log(l))
+    mixed_ref[pl.ds(first, QB), cols] = jnp.where(lane < 64, outs[0], outs[1]).astype(bf16)
+    both = jnp.where(lane < 64, jnp.broadcast_to(lses[0], (QB, 128)), jnp.broadcast_to(lses[1], (QB, 128)))
+    t = both.T
+    lse_ref[pair, 0:1, pl.ds(first, QB)] = t[0:1, :]
+    lse_ref[pair, 1:2, pl.ds(first, QB)] = t[64:65, :]
+
+
+def gather_units(place, own, down_own, ff, small_all, qkv_all, o_all, up_all, down_all, sems):
+    A, B = place.outer_total, place.inner_total
+
+    def rows_view(ref, offset=0, cols=None):
+        def view(slot, start, rows):
+            at = pl.ds(pl.multiple_of(offset + start, 8), rows)
+            return ref.at[slot, at] if cols is None else ref.at[slot, at, cols]
+        return view
+
+    third = own // 3
+    half = down_own // 2
+    five = half * 5 // 12 // 8 * 8
+    specs = [(rows_view(small_all), small_all.shape[1], 0),
+             (rows_view(qkv_all), 3 * own, own),
+             (rows_view(o_all), own, third),
+             (rows_view(up_all, 0, pl.ds(0, ff // 2)), own, third),
+             (rows_view(up_all, 0, pl.ds(ff // 2, ff // 2)), own, third),
+             (rows_view(down_all, 0), half, five),
+             (rows_view(down_all, half), half, five)]
+    units = []
+    base = 0
+    for view, rows, edge in specs:
+        units.append(Gather(place, view, rows, edge, sems, base))
+        base += Gather.count(A, B, edge)
+    return units
+
+
+def gather_kernel(dp_total, fsdp_total, counts_ref, tokens_ref, small_ref, qo_ref, ko_ref, vo_ref, oo_ref, uo_ref,
+                  do_ref, fi_ref, q_ref, k_ref, v_ref, vec_ref, mixed_ref, lse_ref, qkv_all, o_all, up_all, down_all,
+                  small_all, w_s, small_s, send_sem, recv_sem, loc_sem):
     place = Place(dp_total, fsdp_total)
-    A, B = place.outer_total, place.inner_total
     n = fsdp_total
     own = qo_ref.shape[0]
-    down_own = do_ref.shape[0]
-    ff = uo_ref.shape[1]
     me = place.f
-    greet(place)
+    greet(place.neighbours())
     fill = [local(small_ref, small_all.at[me], loc_sem.at[0])]
     for i, r in enumerate((qo_ref, ko_ref, vo_ref)):
         fill.append(local(r, qkv_all.at[me, pl.ds(i * own, own)], loc_sem.at[1 + i]))
     fill.append(local(oo_ref, o_all.at[me], loc_sem.at[4]))
     fill.append(local(uo_ref, up_all.at[me], loc_sem.at[5]))
     fill.append(local(do_ref, down_all.at[me], loc_sem.at[6]))
-    sems = (send_sem, recv_sem)
-    third = own // 3
-
-    def rows_view(ref, offset=0, cols=None):
-        def view(slot, start, rows):
-            at = pl.ds(pl.multiple_of(offset + start, 8), rows)
-            return ref.at[slot, at] if cols is None else ref.at[slot, at, cols]
-        return view
-
-    specs = [(rows_view(small_all), small_all.shape[1], 0),
-             (rows_view(qkv_all), 3 * own, own),
-             (rows_view(o_all), own, third),
-             (rows_view(up_all, 0, pl.ds(0, ff // 2)), own, third),
-             (rows_view(up_all, 0, pl.ds(ff // 2, ff // 2)), own, third),
-             (rows_view(down_all, 0), down_own // 2, down_own // 6),
-             (rows_view(down_all, down_own // 2), down_own // 2, down_own // 6)]
-    units = []
-    base = 0
-    for view, rows, edge in specs:
-        units.append(Gather(place, view, rows, edge, sems, base))
-        base += Gather.count(A, B, edge)
+    units = gather_units(place, own, do_ref.shape[0], uo_ref.shape[1], small_all, qkv_all, o_all, up_all, down_all,
+                         (send_sem, recv_sem))
     for c in fill:
         c.wait()
-    for u in units:
-        u.start_outer()
-    sm, u0, rest = units[0], units[1], units[2:]
-    sm.start_inner()
-    u0.start_inner()
+    sm, u = units[0], units[1:]
+    for x in (sm, u[0], u[1]):
+        x.start()
     sm.from_outer()
     sm.from_inner()
     sm.from_twin()
-    u0.from_outer()
-    rest[0].start_inner()
-    rest[1].start_inner()
+    u[2].start()
+    u[0].from_outer()
     sm.from_core()
-    cs = local(small_all, small_s, loc_sem.at[0])
-    u0.from_inner()
-    rest[0].from_outer()
-    cs.wait()
+    take = local(small_all, small_s, loc_sem.at[0])
+    u[0].from_inner()
+    take.wait()
     total = jnp.zeros(vec_ref.shape, f32)
     for i in range(n):
         total = total + small_s[i].astype(f32)
     vec_ref[...] = total
-    u0.from_twin()
-    rest[1].from_outer()
-    u0.from_core()
-    cw = local(qkv_all, w_s, loc_sem.at[1])
-    rest[2].start_inner()
-    rest[0].from_inner()
-    cw.wait()
-    rows = tokens_ref.shape[0]
-    todo = [rest[2].from_outer, rest[0].from_twin, rest[1].from_inner, rest[3].start_inner,
-            rest[3].from_outer, rest[1].from_twin, rest[0].from_core, rest[2].from_inner, rest[4].start_inner,
-            rest[4].from_outer, rest[2].from_twin, rest[1].from_core, rest[3].from_inner, rest[3].from_twin,
-            rest[4].from_inner, rest[2].from_core, rest[4].from_twin, rest[3].from_core, rest[4].from_core]
-    gain = vec_ref[0:1, :]
-    shift = vec_ref[1:2, :]
-    qbias = vec_ref[2:3, :]
-    vbias = vec_ref[3:4, :]
-    feat = tokens_ref.shape[1]
-    for i in range(rows // RB):
-        sl = slice(i * RB, (i + 1) * RB)
-        xhat, _ = norm_parts(tokens_ref[sl, :].astype(f32))
-        fi = (xhat * gain + shift).astype(bf16)
+    u[3].start()
+    u[1].from_outer()
+    u[0].from_twin()
+    u[0].from_core()
+    take = local(qkv_all, w_s, loc_sem.at[1])
+    u[1].from_inner()
+    take.wait()
+    rows, feat = tokens_ref.shape
+
+    def project_rows(i, _):
+        sl = pl.ds(pl.multiple_of(i * RB, RB), RB)
+        xhat, _q = norm_parts(tokens_ref[sl, :].astype(f32))
+        fi = (xhat * vec_ref[0:1, :] + vec_ref[1:2, :]).astype(bf16)
         fi_ref[sl, :] = fi
         weight = lambda i: w_s[:, i * own:(i + 1) * own, :].reshape(feat, feat)
-        q_ref[sl, :] = ((dot(fi, weight(0)) + qbias).astype(bf16).astype(f32) * 0.125).astype(bf16)
+        q_ref[sl, :] = ((dot(fi, weight(0)) + vec_ref[2:3, :]).astype(bf16).astype(f32) * 0.125).astype(bf16)
         k_ref[sl, :] = dot(fi, weight(1)).astype(bf16)
-        v_ref[sl, :] = (dot(fi, weight(2)) + vbias).astype(bf16)
-        for _ in range(2):
-            todo.pop(0)()
-    for t in todo:
-        t()
-    for u in units:
-        u.finish()
-
-
-def gather_project(sizes, tokens, small, qw, kw, vw, ow, up, down):
+        v_ref[sl, :] = (dot(fi, weight(2)) + vec_ref[3:4, :]).astype(bf16)
+        return 0
+
+    half = rows // RB // 2
+    lax.fori_loop(0, half, project_rows, 0)
+    u[2].from_outer()
+    lax.fori_loop(half, 2 * half, project_rows, 0)
+    u[4].start()
+    u[1].from_twin()
+    u[2].from_inner()
+    blocks = rows // QB
+    step = lambda unit, s: functools.partial(unit.from_outer_step, s)
+    batches = [
+        [step(u[3], 1), u[5].start],
+        [step(u[3], 2), u[1].from_core],
+        [step(u[3], 3), u[2].from_twin],
+        [u[3].from_inner],
+        [step(u[4], 1), u[2].from_core],
+        [step(u[4], 2), u[3].from_twin],
+        [step(u[4], 3)],
+        [u[4].from_inner, u[3].from_core],
+        [step(u[5], 1)],
+        [step(u[5], 2), u[4].from_twin],
+        [step(u[5], 3)],
+        [u[5].from_inner, u[4].from_core],
+        [u[5].from_twin],
+        [],
+        [u[5].from_core]]
+    pieces = feat // 128 * blocks
+
+    def piece(i, _):
+        attend_block(counts_ref, q_ref, k_ref, v_ref, mixed_ref, lse_ref, i // blocks, i % blocks)
+        for k, batch in enumerate(batches):
+            if batch:
+                @pl.when(i == (k + 1) * (pieces - 1) // len(batches))
+                def _(batch=batch):
+                    for one in batch:
+                        one()
+        return 0
+
+    lax.fori_loop(0, pieces, piece, 0)
+    for x in units:
+        x.finish()
+
+
+def gather_attend(sizes, counts, tokens, small, qw, kw, vw, ow, up, down):
     dp_total, n = sizes
     rows, feat = tokens.shape
     own = qw.shape[0]
-    half = n // 2
-    A = 4 if half % 4 == 0 else half
-    B = half // A
+    A, B = 4, n // 8
+    pairs = feat // 128
     copies = Gather.count(A, B, 0) + 6 * Gather.count(A, B, 1)
     s = jax.ShapeDtypeStruct
     vm = pl.BlockSpec(memory_space=pltpu.VMEM)
     anyspec = pl.BlockSpec(memory_space=pl.ANY)
     return pl.pallas_call(
         functools.partial(gather_kernel, dp_total, n),
-        in_specs=[vm] * 8,
-        out_specs=[vm] * 5 + [anyspec] * 5,
-        out_shape=[s((rows, feat), bf16)] * 4 + [s(small.shape, f32), s((n, 3 * own, feat), bf16), s((n, own, feat), bf16),
+        in_specs=[pl.BlockSpec(memory_space=pltpu.SMEM)] + [vm] * 8,
+        out_specs=[vm] * 7 + [anyspec] * 5,
+        out_shape=[s((rows, feat), bf16)] * 4 + [s(small.shape, f32), s((rows, feat), bf16), s((pairs, 2, rows), f32),
+                   s((n, 3 * own, feat), bf16), s((n, own, feat), bf16),
                    s((n,) + up.shape, bf16), s((n,) + down.shape, bf16), s((n,) + small.shape, bf16)],
         scratch_shapes=[pltpu.VMEM((n, 3 * own, feat), bf16), pltpu.VMEM((n,) + small.shape, bf16),
                         pltpu.SemaphoreType.DMA((copies,)), pltpu.SemaphoreType.DMA((copies,)),
                         pltpu.SemaphoreType.DMA((8,))],
         compiler_params=pltpu.CompilerParams(collective_id=1, has_side_effects=True, vmem_limit_bytes=60 * 2**20),
-        name="gather_project",
-    )(tokens, small, qw, kw, vw, ow, up, down)
+        name="gather_attend",
+    )(counts, tokens, small, qw, kw, vw, ow, up, down)
 
 
 def plan_neighbours(place):
     out = place.neighbours()
     out += [(place.side + 2 * ((place.d // 2 + k) % place.pairs), place.f) for k in range(1, place.pairs)]
     return out
-
-
-def greet_all(place):
-    barrier = pltpu.get_barrier_semaphore()
-    others = plan_neighbours(place)
-    for other in others:
-        pl.semaphore_signal(barrier, inc=1, device_id=other, device_id_type=MESH)
-    pl.semaphore_wait(barrier, len(others))
 
 
 def scatter_copies(A, B, pairs):
@@ -816,7 +901,7 @@
     per = 5 if pairs == 1 else 7
     send_sem, recv_sem = rest[-2:]
     sems = (send_sem, recv_sem)
-    greet_all(place)
+    greet(plan_neighbours(place))
     base = 0
     units = []
     for i in range(k):
@@ -876,8 +961,8 @@
     eight = jnp.stack([first_gain, first_shift, query_bias, value_bias, out_bias, second_gain, second_shift, down_bias])
     small = jnp.concatenate([spread(eight, me, n), spread(up_bias[None], me, n).reshape(-1, feat)])
     small = jnp.concatenate([small, jnp.zeros((16 - small.shape[0], feat), bf16)])
-    fi, q, k, v, vec, qkv_all, o_all, up_all, down_all, _ = gather_project(
-        sizes, tokens, small, query_weight, key_weight, value_weight, out_weight, up_weight, down_weight)
+    fi, q, k, v, vec, mixed, lse, qkv_all, o_all, up_all, down_all, _ = gather_attend(
+        sizes, counts, tokens, small, query_weight, key_weight, value_weight, out_weight, up_weight, down_weight)
     full = lambda i: qkv_all[:, i * own:(i + 1) * own].reshape(feat, feat)
     qw, kw, vw = full(0), full(1), full(2)
     ow = o_all.reshape(feat, feat)
@@ -886,7 +971,6 @@
     vec1 = vec[0:8]
     vec2 = vec[4:12]
     ub = vec[8:12].reshape(1, -1)
-    mixed, lse = attn_fwd(counts, q, k, v)
     layer_out, gres, gmix, gup, gub, gdown, gout, gv2 = middle(counts, mixed, tokens, cotangent, ow, vec2, up, ub, down)
     dq, dk, dv = attn_bwd(counts, q, k, v, gmix, lse)
     gtok, gq, gk, gv, gv1 = project_back(tokens, vec1, gres, fi, dq, dk, dv, qw, kw, vw)

time: 360 us -> 343 us (0.953); the launches traced: 355 us -> 343 us
  Pallas kernels: 329 us -> 316 us
    pallas_call x2 -> x1, Pallas kernels: 115 us -> 107 us  [gather_attend(): pl.pallas_call(functools.partial(gather_kernel, dp_total, n), in_specs=[p...]
where the time goes in v4:
time: 343 us
  Pallas kernels  316 us (92%)
  local copies, waits for them, and re-layouts  19.9 us (6%)
  other arithmetic  5.9 us (2%)
    pallas_call x1, Pallas kernels, reduce_all(): pl.pallas_call(functools.partial(reduce_kernel, dp_total, n, edges), in_s...  110 us
    pallas_call x1, Pallas kernels, gather_attend(): pl.pallas_call(functools.partial(gather_kernel, dp_total, n), in_specs=[p...  107 us
    pallas_call x1, Pallas kernels, middle(): pl.pallas_call(mid_kernel, grid_spec=pltpu.PrefetchScalarGridSpec(num_sca...  47.6 us
    pallas_call x1, Pallas kernels, attn_bwd(): pl.pallas_call(bwd_kernel, grid_spec=pltpu.PrefetchScalarGridSpec(num_sca...  37 us
    pallas_call x1, Pallas kernels, project_back(): pl.pallas_call(back_kernel, out_shape=[s((rows, D), f32), s((D, D), bf16)...  14.7 us

profile of v4, /device:TPU:0, one launch (start us, length us, event | category | flops | bytes accessed | tf_op | source)
XLA Modules:
  0.0 343.1 jit_solution(17359826489769554026)
XLA Ops:
  0.7 0.1 broadcast_in_dim.48
  0.8 0.8 stack.35
  1.6 0.1 broadcast_in_dim.51
  1.8 0.1 iota.12
  1.9 0.7 broadcast_in_dim.53
  2.6 0.1 broadcast_in_dim.54
  2.7 0.6 pad_maximum_fusion.2.small_ref
  3.3 107.0 %gather_attend.1 = (bf16[1024,768]{1,0:T(8,128)(2,1)}, bf16[1024,768]{1,0:T(8,128)(2,1)}, bf16[1024,768]{1,0:T(8,128)(2,1)}, bf16[1024,768]{1,0:T(8,128)(2,1)}, ...) custom-call(s32[2]{0:T(128)} %bitcast.67, ...), custom_call_target="tpu_custom_call" | custom-call | tf_op jit(solution)/shard_map/gather_attend/pallas_call | solution.py:659
  110.3 1.5 fusion.11
  111.8 0.7 slice_bitcast_fusion
  112.6 0.6 copy.35
  113.2 47.6 %feed_forward.1 = (bf16[1024,768]{1,0:T(8,128)(2,1)}, f32[1024,768]{1,0:T(8,128)}, bf16[1024,768]{1,0:T(8,128)(2,1)}, bf16[768,3072]{1,0:T(8,128)(2,1)}, f32[1,3...) custom-call(s32[2]{0:T(128)} %bitcast.68, ...), custom_call_target="tpu_custom_call" | custom-call | tf_op jit(solution)/shard_map/feed_forward/pallas_call | solution.py:247
  160.8 37.0 %attend_back.1 = (bf16[1024,768]{1,0:T(8,128)(2,1)}, bf16[1024,768]{1,0:T(8,128)(2,1)}, bf16[1024,768]{1,0:T(8,128)(2,1)}) custom-call(s32[2]{0:T(128)} %bitcast.69, bf16[1024,768]{1,0:T(8,128)(2,1)} %get-tuple-element.61.q_ref, bf16[1024,768]{1,0:T(8,128)(2,1)} %get-tuple-element.62.k_ref, bf16[1024,768]{1,0:T(8,128)(2,1)} %get-tuple-element.63.v_ref, ...), custom_call_target="tpu_custom_call" | custom-call | tf_op jit(solution)/shard_map/attend_back/pallas_call | solution.py:151
  197.8 1.9 fusion.10
  199.7 14.7 %project_back.1 = (f32[1024,768]{1,0:T(8,128)}, bf16[768,768]{1,0:T(8,128)(2,1)}, bf16[768,768]{1,0:T(8,128)(2,1)}, bf16[768,768]{1,0:T(8,128)(2,1)}, f32[8,768]{1,0:T(8,128)}) custom-call(bf16[1024,768]{1,0:T(8,128)(2,1)} %tokens_ref.5, f32[8,768]{1,0:T(8,128)} %get-tuple-element.104.vec_ref, f32[1024,768]{1,0:T(8,128)} %get-tuple-element.59.gres_ref, ...), custom_call_target="tpu_custom_call" | custom-call | tf_op jit(solution)/shard_map/project_back/pallas_call | solution.py:305
  214.4 0.7 slice.80
  215.1 0.5 broadcast.29
  215.6 0.7 reduce.3
  216.4 0.7 maximum_maximum_fusion.refs_0_
  217.1 5.1 %fusion.9 = (bf16[16,96,768]{2,1,0:T(8,128)(2,1)}, bf16[16,96,768]{2,1,0:T(8,128)(2,1)}) fusion(bf16[16,192,768]{2,1,0:T(8,128)(2,1)} %bitcast.57), kind=kLoop, calls=%fused_computation.26 | loop fusion | bytes 9437184 | tf_op jit(solution)/shard_map/slice | solution.py:984
  222.2 2.8 fusion.8
  225.0 110.2 %reduce_gradients.1 = (f32[16,768]{1,0:T(8,128)}, f32[96,768]{1,0:T(8,128)}, f32[96,768]{1,0:T(8,128)}, f32[48,1536]{1,0:T(8,128)}, f32[48,1536]{1,0:T(8,128)}, ...) custom-call(f32[16,768]{1,0:T(8,128)} %maximum_maximum_fusion.refs_0_, ...), custom_call_target="tpu_custom_call" | custom-call | tf_op jit(solution)/shard_map/reduce_gradients/pallas_call | solution.py:936
  335.2 2.0 pad_maximum_fusion.1
  337.2 1.9 pad_maximum_fusion
  339.1 0.1 reshape.131
  339.2 0.6 fusion
  339.8 0.1 reshape.132
  339.9 0.6 constant_dynamic-slice_fusion.7
  340.4 0.7 copy.40
  341.1 0.7 copy.41
  341.8 0.7 copy.42
  342.4 0.7 copy.43
  (34 shorter events, 0.3 us)
Async XLA Ops:
  160.8 37.0 %copy-start = (bf16[16,144,768]{2,1,0:T(8,128)(2,1)S(1)}, bf16[16,144,768]{2,1,0:T(8,128)(2,1)}, u32[]{:S(2)}) copy-start(bf16[16,144,768]{2,1,0:T(8,128)(2,1)} %get-tuple-element.69) | copy-start | bytes 10616836
  199.7 15.9 %copy-start.6 = (f32[1,3072]{1,0:T(1,128)S(1)}, f32[1,3072]{1,0:T(1,128)}, u32[]{:S(2)}) copy-start(f32[1,3072]{1,0:T(1,128)} %get-tuple-element.73) | copy-start | bytes 36868
  199.7 16.6 %copy-start.7 = (f32[8,768]{1,0:T(8,128)S(1)}, f32[8,768]{1,0:T(8,128)}, u32[]{:S(2)}) copy-start(f32[8,768]{1,0:T(8,128)} %get-tuple-element.72) | copy-start | bytes 73732
  217.1 5.1 %slice-start = ((s8[4718592]{0:T(1024)(128)(4,1)}), s8[4194304]{0:T(1024)(128)(4,1)S(1)}, s32[]{:S(2)}) async-start(s8[4718592]{0:T(1024)(128)(4,1)} %bitcast.54), calls=%async_computation | async-start | bytes 8388608
  217.1 5.1 %slice-start.1 = ((s8[4718592]{0:T(1024)(128)(4,1)}), s8[524288]{0:T(1024)(128)(4,1)S(1)}, s32[]{:S(2)}) async-start(s8[4718592]{0:T(1024)(128)(4,1)} %bitcast.54), calls=%async_computation.1 | async-start | bytes 1048576
  335.2 3.9 %copy-start.5 = (f32[16,768]{1,0:T(8,128)S(1)}, f32[16,768]{1,0:T(8,128)}, u32[]{:S(2)}) copy-start(f32[16,768]{1,0:T(8,128)} %get-tuple-element.80) | copy-start | bytes 147460
  335.2 5.2 %copy-start.4 = (f32[48,768]{1,0:T(8,128)S(1)}, f32[48,768]{1,0:T(8,128)}, u32[]{:S(2)}) copy-start(f32[48,768]{1,0:T(8,128)} %get-tuple-element.127) | copy-start | bytes 442372
  335.2 5.9 %copy-start.3 = (f32[48,768]{1,0:T(8,128)S(1)}, f32[48,768]{1,0:T(8,128)}, u32[]{:S(2)}) copy-start(f32[48,768]{1,0:T(8,128)} %get-tuple-element.129) | copy-start | bytes 442372
  335.2 6.6 %copy-start.2 = (f32[48,768]{1,0:T(8,128)S(1)}, f32[48,768]{1,0:T(8,128)}, u32[]{:S(2)}) copy-start(f32[48,768]{1,0:T(8,128)} %get-tuple-element.130) | copy-start | bytes 442372
  335.2 7.2 %copy-start.1 = (f32[48,768]{1,0:T(8,128)S(1)}, f32[48,768]{1,0:T(8,128)}, u32[]{:S(2)}) copy-start(f32[48,768]{1,0:T(8,128)} %get-tuple-element.132) | copy-start | bytes 442372

commit v5 on v1

--- a/solution.py
+++ b/solution.py
@@ -305,44 +305,963 @@
     return pl.pallas_call(back_kernel,out_shape=[s((rows,D),f32),s((D,D),bf16),s((D,D),bf16),s((D,D),bf16),s((8,D),f32)],
         compiler_params=pltpu.CompilerParams(vmem_limit_bytes=60*2**20),name="project_back")(tokens,vec,gres,fi,dq,dk,dv,qw,kw,vw)
 
+
+MESH = pl.DeviceIdType.MESH
+
+
+class Place:
+    def __init__(self, dp_total, fsdp_total):
+        half = fsdp_total // 2
+        self.outer_total = 4
+        self.inner_total = half // 4
+        assert half % 4 == 0
+        self.pairs = dp_total // 2
+        self.d = lax.axis_index("dp")
+        self.f = lax.axis_index("fsdp")
+        self.core = self.f % 2
+        self.inner = (self.f // 2) % self.inner_total
+        self.outer = self.f // (2 * self.inner_total)
+        self.side = self.d % 2
+        self.twin = self.d + 1 - 2 * self.side
+        self.flip = self.outer // 2
+        self.mirror = self.unmirror(self.outer)
+
+    def unmirror(self, at):
+        return at + self.flip * (3 - 2 * at)
+
+    def arrival(self, step):
+        return self.unmirror(step - self.mirror if step == 1 else step)
+
+    def device(self, outer, inner, core):
+        return (self.d, (outer * self.inner_total + inner) * 2 + core)
+
+    def at_outer(self, outer):
+        return self.device(outer, self.inner, self.core)
+
+    def at_inner(self, t):
+        return self.device(self.outer, (self.inner + t) % self.inner_total, self.core)
+
+    def other_core(self):
+        return self.device(self.outer, self.inner, 1 - self.core)
+
+    def at_twin(self):
+        return (self.twin, self.f)
+
+    def me(self):
+        return (self.d, self.f)
+
+    def at_pair(self, k):
+        return (self.side + 2 * ((self.d // 2 + k) % self.pairs), self.f)
+
+    def neighbours(self, pairs=False):
+        out = [self.at_outer((self.outer + s) % 4) for s in range(1, 4)]
+        out += [self.at_inner(t) for t in range(1, self.inner_total)]
+        out += [self.at_twin(), self.other_core()]
+        if pairs:
+            out += [self.at_pair(k) for k in range(1, self.pairs)]
+        return out
+
+
+def greet(others):
+    barrier = pltpu.get_barrier_semaphore()
+    for other in others:
+        pl.semaphore_signal(barrier, inc=1, device_id=other, device_id_type=MESH)
+    pl.semaphore_wait(barrier, len(others))
+
+
+class Gather:
+    def __init__(self, place, ref, edge, sems, base):
+        self.place, self.ref, self.edge = place, ref, edge
+        self.rows = ref.shape[-2]
+        self.send_sem, self.recv_sem = sems
+        self.base = base
+        A, B = place.outer_total, place.inner_total
+        keys = [("z", s) for s in range(1, A)] + [("Z", s) for s in range(1, A)]
+        keys += [("x", s, t) for s in range(A) for t in range(1, B)]
+        keys += [("y", t) for t in range(B)]
+        keys += [("c",)]
+        self.keys = {key: i for i, key in enumerate(keys)}
+        self.sent = []
+        self.sent_inside = []
+
+    @staticmethod
+    def count(B):
+        return 6 + 4 * (B - 1) + B + 1
+
+    def rows_of(self, kind):
+        e, r, p = self.edge, self.rows, self.place.side
+        if not e or kind == "all":
+            return pl.ds(0, r)
+        start, size = {"plane": (p * e, r - e), "mine": (p * (r - e), e), "theirs": ((1 - p) * (r - e), e)}[kind]
+        return pl.ds(pl.multiple_of(start, 8), size)
+
+    def part(self, outer, inner, core, kind):
+        return self.ref.at[outer, inner, core, self.rows_of(kind)]
+
+    def copy(self, key, ref, to):
+        i = self.base + self.keys[key]
+        into = i
+        if key[0] == "Z":
+            into = self.base + self.keys["z", 2 if key[1] == 2 else 3]
+        return pltpu.make_async_remote_copy(src_ref=ref, dst_ref=ref, send_sem=self.send_sem.at[i],
+                                            recv_sem=self.recv_sem.at[into], device_id=to, device_id_type=MESH)
+
+    def send(self, key, make):
+        self.copy(key, *make()).start()
+        self.sent.append((key, make))
+
+    def send_inside(self, key, make):
+        @pl.when(self.place.mirror == 1)
+        def _():
+            self.copy(key, *make()).start()
+
+        self.sent_inside.append((key, make))
+
+    def got(self, key, ref):
+        self.copy(key, ref, self.place.me()).wait_recv()
+
+    def outer_of(self, step):
+        return self.place.outer if step == 0 else self.place.arrival(step)
+
+    def own_line(self, step):
+        p = self.place
+        return self.part(self.outer_of(step), p.inner, p.core, "plane")
+
+    def start(self):
+        p = self.place
+        self.send(("z", 1), lambda: (self.own_line(0), p.at_outer(p.unmirror(1 - p.mirror))))
+        self.send_inside(("z", 2), lambda: (self.own_line(0), p.at_outer(p.unmirror(2))))
+        self.pass_inner(0)
+
+    def pass_inner(self, step):
+        p = self.place
+        for t in range(1, p.inner_total):
+            self.send(("x", step, t), lambda t=t: (self.own_line(step), p.at_inner(-t)))
+
+    def from_outer_step(self, step):
+        p = self.place
+        self.got(("z", step), self.own_line(step))
+        self.send_inside(("Z", step), lambda: (self.own_line(step), p.at_outer(p.unmirror(2 if step == 1 else 0))))
+        self.pass_inner(step)
+        if step == 3:
+            self.pass_twin(0)
+
+    def from_outer(self):
+        for step in range(1, 4):
+            self.from_outer_step(step)
+
+    def line(self, t, kind):
+        p = self.place
+        return self.part(slice(None), (p.inner + t) % p.inner_total, p.core, kind)
+
+    def pass_twin(self, t):
+        if self.edge:
+            self.send(("y", t), lambda: (self.line(t, "mine"), self.place.at_twin()))
+
+    def from_inner(self):
+        p = self.place
+        for t in range(1, p.inner_total):
+            for step in range(4):
+                self.got(("x", step, t), self.part(self.outer_of(step), (p.inner + t) % p.inner_total, p.core, "plane"))
+            self.pass_twin(t)
+
+    def half(self, core):
+        return self.part(slice(None), slice(None), core, "all")
+
+    def from_twin(self):
+        p = self.place
+        if self.edge:
+            for t in range(p.inner_total):
+                self.got(("y", t), self.line(t, "theirs"))
+        self.send(("c",), lambda: (self.half(p.core), p.other_core()))
+
+    def from_core(self):
+        self.got(("c",), self.half(1 - self.place.core))
+
+    def finish(self):
+        for key, make in self.sent:
+            self.copy(key, *make()).wait_send()
+
+        @pl.when(self.place.mirror == 1)
+        def _():
+            for key, make in self.sent_inside:
+                self.copy(key, *make()).wait_send()
+
+
+class Scatter:
+    def __init__(self, place, terms, bufs, edge, emit, sems, base):
+        self.place, self.terms, self.edge, self.emit = place, terms, edge, emit
+        self.sums, self.twin_buf, self.inner_buf, self.outer_buf, self.last_buf = bufs[:5]
+        self.pair_bufs = bufs[5:]
+        self.send_sem, self.recv_sem = sems
+        self.base = base
+        p, e, w = place.side, edge, terms.shape[-1]
+        at = lambda start, size: pl.ds(pl.multiple_of(start, 128), size)
+        self.plane = at(p * e, w - e)
+        self.mine = at(p * (w - e), e)
+        self.theirs = at((1 - p) * (w - e), e)
+        self.twin_plane = at((1 - p) * e, w - e)
+        self.middle = pl.ds(e, w - 2 * e)
+
+    @staticmethod
+    def count(B, pairs):
+        return 1 + 1 + (B - 1) + 3 + 1 + (pairs - 1)
+
+    @staticmethod
+    def shapes(B, pairs, rows, width, edge, lead=()):
+        out = [(4, B, rows, width), (4, B, rows, edge), (B - 1, 4, rows, width), (3, rows, width), (rows, width)]
+        if pairs > 1:
+            out += [(rows, width), (pairs - 1, rows, width)]
+        return [pltpu.VMEM(tuple(lead) + s, bf16) for s in out]
+
+    def copy(self, i, src, dst, to):
+        return pltpu.make_async_remote_copy(src_ref=src, dst_ref=dst, send_sem=self.send_sem.at[self.base + i],
+                                            recv_sem=self.recv_sem.at[self.base + i], device_id=to, device_id_type=MESH)
+
+    def copies(self, stage):
+        p = self.place
+        A, B = 4, p.inner_total
+        if stage == "core":
+            return [self.copy(0, self.terms.at[:, :, 1 - p.core], self.sums, p.other_core())]
+        if stage == "twin":
+            return [self.copy(1, self.sums.at[:, :, :, self.theirs], self.twin_buf, p.at_twin())]
+        if stage == "inner":
+            return [self.copy(1 + t, self.sums.at[:, (p.inner + B - t) % B, :, self.plane],
+                              self.inner_buf.at[t - 1, :, :, self.plane], p.at_inner(-t)) for t in range(1, B)]
+        if stage == "outer":
+            return [self.copy(B + s, self.sums.at[(p.outer + A - s) % A, p.inner, :, self.plane],
+                              self.outer_buf.at[s - 1, :, self.plane], p.at_outer((p.outer + A - s) % A))
+                    for s in range(1, A)]
+        if stage == "last":
+            return [self.copy(A + B, self.sums.at[p.outer, p.inner, :, self.plane], self.last_buf.at[:, self.plane],
+                              p.at_twin())]
+        half, others = self.pair_bufs
+        return [self.copy(A + B + k, half, others.at[k - 1], p.at_pair(p.pairs - k)) for k in range(1, p.pairs)]
+
+    def go(self, stage):
+        for c in self.copies(stage):
+            c.start()
+
+    def got(self, i, dst):
+        self.copy(i, dst, dst, self.place.me()).wait_recv()
+
+    def start(self):
+        self.go("core")
+
+    def from_core(self):
+        p = self.place
+        B = p.inner_total
+        self.got(0, self.sums)
+
+        def add(i, _):
+            a, b = i // B, i % B
+            self.sums[a, b] = (self.sums[a, b].astype(f32) + self.terms[a, b, p.core].astype(f32)).astype(bf16)
+            return 0
+
+        lax.fori_loop(0, 4 * B, add, 0)
+        self.go("twin")
+
+    def from_twin(self):
+        p = self.place
+        B = p.inner_total
+        self.got(1, self.twin_buf)
+
+        def add(i, _):
+            a, b = i // B, i % B
+            self.sums[a, b, :, self.mine] = (self.sums[a, b, :, self.mine].astype(f32)
+                                             + self.twin_buf[a, b].astype(f32)).astype(bf16)
+            return 0
+
+        lax.fori_loop(0, 4 * B, add, 0)
+        self.go("inner")
+
+    def from_inner(self):
+        p = self.place
+        B = p.inner_total
+        for t in range(1, B):
+            self.got(1 + t, self.inner_buf.at[t - 1, :, :, self.plane])
+
+        def add(a, _):
+            total = self.sums[a, p.inner, :, self.plane].astype(f32)
+            for t in range(1, B):
+                total = total + self.inner_buf[t - 1, a, :, self.plane].astype(f32)
+            self.sums[a, p.inner, :, self.plane] = total.astype(bf16)
+            return 0
+
+        lax.fori_loop(0, 4, add, 0)
+        self.go("outer")
+
+    def from_outer(self):
+        p = self.place
+        B = p.inner_total
+        for s in range(1, 4):
+            self.got(B + s, self.outer_buf.at[s - 1, :, self.plane])
+        total = self.sums[p.outer, p.inner, :, self.plane].astype(f32)
+        for s in range(1, 4):
+            total = total + self.outer_buf[s - 1, :, self.plane].astype(f32)
+        self.sums[p.outer, p.inner, :, self.plane] = total.astype(bf16)
+        self.go("last")
+
+    def from_last(self):
+        p = self.place
+        self.got(4 + p.inner_total, self.last_buf.at[:, self.twin_plane])
+        own = lambda cols: self.sums[p.outer, p.inner, :, cols].astype(f32)
+        last = lambda cols: self.last_buf[:, cols].astype(f32)
+        if p.pairs == 1:
+            self.emit(self.mine, own(self.mine))
+            self.emit(self.middle, own(self.middle) + last(self.middle))
+            self.emit(self.theirs, last(self.theirs))
+            return
+        half, others = self.pair_bufs
+        half[:, self.mine] = own(self.mine).astype(bf16)
+        half[:, self.middle] = (own(self.middle) + last(self.middle)).astype(bf16)
+        half[:, self.theirs] = last(self.theirs).astype(bf16)
+        self.go("pairs")
+
+    def from_pairs(self):
+        p = self.place
+        if p.pairs == 1:
+            return
+        half, others = self.pair_bufs
+        total = half[...].astype(f32)
+        for k in range(1, p.pairs):
+            self.got(4 + p.inner_total + k, others.at[k - 1])
+            total = total + others[k - 1].astype(f32)
+        self.emit(pl.ds(0, self.terms.shape[-1]), total)
+
+    def finish(self):
+        for stage in ("core", "twin", "inner", "outer", "last") + (("pairs",) if self.place.pairs > 1 else ()):
+            for c in self.copies(stage):
+                c.wait_send()
+
+
+class Total:
+    def __init__(self, place, value, bufs, out, sems, base):
+        self.place, self.value, self.bufs, self.out = place, value, bufs, out
+        self.send_sem, self.recv_sem = sems
+        p = place
+        rounds = [[p.other_core()], [p.at_inner(t) for t in range(1, p.inner_total)],
+                  [p.at_outer((p.outer + s) % 4) for s in range(1, 4)], [p.at_twin()],
+                  [p.at_pair(k) for k in range(1, p.pairs)]]
+        self.rounds = [r for r in rounds if r]
+        self.base = base
+
+    @staticmethod
+    def count(B, pairs):
+        return 1 + (B - 1) + 3 + 1 + (pairs - 1)
+
+    @staticmethod
+    def shapes(B, pairs, shape):
+        return [pltpu.VMEM((Total.count(B, pairs),) + shape, f32), pltpu.VMEM((5,) + shape, f32)]
+
+    def copies(self, r):
+        landing, held = self.bufs
+        i = sum(len(x) for x in self.rounds[:r])
+        return [(pltpu.make_async_remote_copy(src_ref=held.at[r], dst_ref=landing.at[i + k],
+                                              send_sem=self.send_sem.at[self.base + i + k],
+                                              recv_sem=self.recv_sem.at[self.base + i + k], device_id=to,
+                                              device_id_type=MESH), i + k) for k, to in enumerate(self.rounds[r])]
+
+    def start(self):
+        self.bufs[1][0] = self.value[...]
+        for c, _ in self.copies(0):
+            c.start()
+
+    def step(self, r):
+        landing, held = self.bufs
+        total = held[r]
+        for c, i in self.copies(r):
+            c.wait_recv()
+            total = total + landing[i]
+        if r + 1 < len(self.rounds):
+            held[r + 1] = total
+            for c, _ in self.copies(r + 1):
+                c.start()
+        else:
+            self.out[...] = total
+
+    def steps(self):
+        return [functools.partial(self.step, r) for r in range(len(self.rounds))]
+
+    def finish(self):
+        for r in range(len(self.rounds)):
+            for c, _ in self.copies(r):
+                c.wait_send()
+
+
+def local(src, dst, sem):
+    c = pltpu.make_async_copy(src, dst, sem)
+    c.start()
+    return c
+
+
+BLOCKS = 3
+
+
+def lane_tile(source, moves):
+    lane = None
+    out = None
+    for col, to, size in moves:
+        tile = source[:, col // 128 * 128:col // 128 * 128 + 128]
+        shift = (to - col) % 128
+        if shift:
+            tile = pltpu.roll(tile, shift, 1)
+        if out is None:
+            out = tile
+            lane = lax.broadcasted_iota(jnp.int32, tile.shape, 1)
+        else:
+            out = jnp.where((lane >= to) & (lane < to + size), tile, out)
+    return out
+
+
+def split_columns(source, owners):
+    piece = source.shape[1] // owners // BLOCKS
+    per = 128 // piece
+    out = []
+    for j in range(BLOCKS):
+        tiles = [lane_tile(source, [(((t * per + q) * BLOCKS + j) * piece, q * piece, piece) for q in range(per)])
+                 for t in range(owners // per)]
+        out.append(jnp.concatenate(tiles, axis=1))
+    return out
+
+
+def join_columns(parts, owners):
+    source = jnp.concatenate(parts, axis=1)
+    width = parts[0].shape[1]
+    piece = width // owners
+    per = 128 // piece
+    tiles = []
+    for t in range(source.shape[1] // 128):
+        moves = []
+        for q in range(per):
+            unit = t * per + q
+            moves.append(((unit % BLOCKS) * width + unit // BLOCKS * piece, q * piece, piece))
+        tiles.append(lane_tile(source, moves))
+    return jnp.concatenate(tiles, axis=1)
+
+
+CFG = {}
+
+
+def attend_block(counts_ref, q_ref, k_ref, v_ref, mixed_ref, lse_ref, pair, block):
+    rows = q_ref.shape[0]
+    lane = lax.broadcasted_iota(jnp.int32, (QB, 128), 1)
+    first = pl.multiple_of(block * QB, QB)
+    cols = pl.ds(pl.multiple_of(pair * 128, 128), 128)
+    q = q_ref[pl.ds(first, QB), cols]
+    k = k_ref[:, cols]
+    v = v_ref[:, cols]
+    ends = image_ends(counts_ref[0], counts_ref[1], rows)
+    rid = image_of(first + lax.broadcasted_iota(jnp.int32, (QB, 1), 0), ends)
+    cid = image_of(lax.broadcasted_iota(jnp.int32, (1, rows), 1), ends)
+    bias = jnp.where(rid == cid, 0.0, NEG)
+    outs = []
+    lses = []
+    for e in range(2):
+        qm = jnp.where((lane < 64) == (e == 0), q, jnp.zeros_like(q))
+        s = dot_nt(qm, k) + bias
+        m = jnp.max(s, axis=1, keepdims=True)
+        p = jnp.exp(s - m)
+        l = jnp.sum(p, axis=1, keepdims=True)
+        o = dot(p.astype(bf16), v)
+        outs.append(o * (1.0 / l))
+        lses.append(m + jnp.log(l))
+    mixed_ref[pl.ds(first, QB), cols] = jnp.where(lane < 64, outs[0], outs[1]).astype(bf16)
+    both = jnp.where(lane < 64, jnp.broadcast_to(lses[0], (QB, 128)), jnp.broadcast_to(lses[1], (QB, 128)))
+    t = both.T
+    lse_ref[pair, 0:1, pl.ds(first, QB)] = t[0:1, :]
+    lse_ref[pair, 1:2, pl.ds(first, QB)] = t[64:65, :]
+
+
+def gather_edge(rows, last=False):
+    return rows // 3 if rows % 24 == 0 else rows // 4 if last or rows < 64 else rows * 3 // 8
+
+
+def gather_plan(sm, u, vectors):
+    step = lambda unit, s: functools.partial(unit.from_outer_step, s)
+    head = [sm.start, u[0].start, sm.from_outer, u[1].start, u[0].from_outer, sm.from_inner, u[2].start,
+            u[1].from_outer, u[0].from_inner, sm.from_twin, u[3].start, u[2].from_outer, u[1].from_inner,
+            u[0].from_twin, sm.from_core, vectors, u[4].start, step(u[3], 1), u[0].from_core]
+    middle = [[step(u[3], 2)], [step(u[3], 3), u[5].start], [u[2].from_inner], [u[1].from_twin]]
+    rest = []
+    for t in range(4, len(u)):
+        rest += [[step(u[t], 1)] + ([u[t + 2].start] if t + 2 < len(u) else []), [step(u[t], 2)], [step(u[t], 3)],
+                 [u[t - 1].from_inner], [u[t - 2].from_twin, u[t - 3].from_core]]
+    n = len(u)
+    rest += [[u[n - 1].from_inner], [u[n - 2].from_twin, u[n - 3].from_core], [u[n - 1].from_twin, u[n - 2].from_core],
+             [u[n - 1].from_core]]
+    return head, middle, rest
+
+
+def gather_kernel(dp_total, n, counts_ref, tokens_hbm, small_ref, qo_ref, ko_ref, vo_ref, oo_ref, uo_ref, do_ref,
+                  q_hbm, k_hbm, v_hbm, vec_ref, mixed_hbm, lse_ref, qkv_all, o_all, up_all, down_all, small_all,
+                  tokens_s, q_s, k_s, v_s, mixed_s, w_s, small_s, up_own, send_sem, recv_sem, loc_sem):
+    place = Place(dp_total, n)
+    B = place.inner_total
+    own = qo_ref.shape[0]
+    piece = do_ref.shape[0] // BLOCKS
+    take_tokens = local(tokens_hbm, tokens_s, loc_sem.at[0])
+    for j, part in enumerate(split_columns(uo_ref[...].astype(f32), n)):
+        up_own[j] = part.astype(bf16)
+    sems = (send_sem, recv_sem)
+    refs = [(small_all, 0), (qkv_all, own), (o_all, gather_edge(own))]
+    for j in range(BLOCKS):
+        refs += [(up_all.at[j], gather_edge(own)), (down_all.at[j], gather_edge(piece, j == BLOCKS - 1))]
+    units = [Gather(place, ref, edge, sems, i * Gather.count(B)) for i, (ref, edge) in enumerate(refs)]
+    mine = lambda unit: unit.part(place.outer, place.inner, place.core, "plane")
+    fill = [local(small_ref, mine(units[0]), loc_sem.at[1])]
+    own_qkv = lambda i: qkv_all.at[place.outer, place.inner, place.core, pl.ds(i * own, own)]
+    fill.append(local(ko_ref, own_qkv(1), loc_sem.at[2]))
+
+    @pl.when(place.side == 0)
+    def _():
+        local(qo_ref, own_qkv(0), loc_sem.at[3]).wait()
+
+    @pl.when(place.side == 1)
+    def _():
+        local(vo_ref, own_qkv(2), loc_sem.at[3]).wait()
+
+    fill.append(local(oo_ref.at[units[2].rows_of("plane")], mine(units[2]), loc_sem.at[5]))
+    for j in range(BLOCKS):
+        a, b = units[3 + 2 * j], units[4 + 2 * j]
+        fill.append(local(up_own.at[j, a.rows_of("plane")], mine(a), loc_sem.at[6 + 2 * j]))
+        rows = b.rows_of("plane")
+        fill.append(local(do_ref.at[pl.ds(pl.multiple_of(j * piece + rows.start, 8), rows.size)], mine(b),
+                          loc_sem.at[7 + 2 * j]))
+    greet(place.neighbours())
+    for c in fill:
+        c.wait()
+
+    def vectors():
+        local(small_all, small_s, loc_sem.at[1]).wait()
+        total = jnp.zeros(vec_ref.shape, f32)
+        for i in range(n):
+            total = total + small_s[i // (2 * B), i // 2 % B, i % 2].astype(f32)
+        vec_ref[...] = total
+
+    head, middle, rest = CFG.get("plan", gather_plan)(units[0], units[1:], vectors)
+    for one in head:
+        one()
+    take = local(qkv_all, w_s, loc_sem.at[1])
+    take_tokens.wait()
+    take.wait()
+    rows, feat = tokens_s.shape
+
+    def project_rows(i):
+        sl = slice(i * RB, (i + 1) * RB)
+        xhat, _q = norm_parts(tokens_s[sl, :].astype(f32))
+        fi = (xhat * vec_ref[0:1, :] + vec_ref[1:2, :]).astype(bf16)
+        weight = lambda i: w_s[:, :, :, i * own:(i + 1) * own, :].reshape(feat, feat)
+        q_s[sl, :] = ((dot(fi, weight(0)) + vec_ref[2:3, :]).astype(bf16).astype(f32) * 0.125).astype(bf16)
+        k_s[sl, :] = dot(fi, weight(1)).astype(bf16)
+        v_s[sl, :] = (dot(fi, weight(2)) + vec_ref[3:4, :]).astype(bf16)
+
+    for i in range(rows // RB):
+        if CFG.get("proj", True):
+            project_rows(i)
+        for one in middle[i]:
+            one()
+    keep = [local(a, b, loc_sem.at[2 + i]) for i, (a, b) in enumerate(((q_s, q_hbm), (k_s, k_hbm), (v_s, v_hbm)))]
+    blocks = rows // QB
+    pieces = feat // 128 * blocks
+
+    def attend_piece(i, _):
+        if CFG.get("att", True):
+            attend_block(counts_ref, q_s, k_s, v_s, mixed_s, lse_ref, i // blocks, i % blocks)
+        for at in range(pieces):
+            todo = [one for k, batch in enumerate(rest) if k * pieces // len(rest) == at for one in batch]
+            if todo:
+                @pl.when(i == at)
+                def _(todo=todo):
+                    for one in todo:
+                        one()
+        return 0
+
+    lax.fori_loop(0, pieces, attend_piece, 0)
+    keep.append(local(mixed_s, mixed_hbm, loc_sem.at[0]))
+    for c in keep:
+        c.wait()
+    for x in units:
+        x.finish()
+
+
+def gather_attend(sizes, counts, tokens, small, qw, kw, vw, ow, up, down):
+    dp_total, n = sizes
+    rows, feat = tokens.shape
+    own = qw.shape[0]
+    B = n // 8
+    pairs = feat // 128
+    s = jax.ShapeDtypeStruct
+    vm = pl.BlockSpec(memory_space=pltpu.VMEM)
+    anyspec = pl.BlockSpec(memory_space=pl.ANY)
+    full = lambda *dims: (4, B, 2) + dims
+    width = up.shape[1] // BLOCKS
+    piece = down.shape[0] // BLOCKS
+    act = s((rows, feat), bf16)
+    copies = (3 + 2 * BLOCKS) * Gather.count(B)
+    return pl.pallas_call(
+        functools.partial(gather_kernel, dp_total, n),
+        in_specs=[pl.BlockSpec(memory_space=pltpu.SMEM), anyspec] + [vm] * 7,
+        out_specs=[anyspec] * 3 + [vm, anyspec, vm] + [anyspec] * 5,
+        out_shape=[act, act, act, s(small.shape, f32), act, s((pairs, 2, rows), f32), s(full(3 * own, feat), bf16),
+                   s(full(own, feat), bf16), s((BLOCKS,) + full(own, width), bf16),
+                   s((BLOCKS,) + full(piece, feat), bf16), s(full(*small.shape), bf16)],
+        scratch_shapes=[pltpu.VMEM((rows, feat), bf16)] * 5 + [
+            pltpu.VMEM(full(3 * own, feat), bf16), pltpu.VMEM(full(*small.shape), bf16),
+            pltpu.VMEM((BLOCKS, own, width), bf16), pltpu.SemaphoreType.DMA((copies,)),
+            pltpu.SemaphoreType.DMA((copies,)), pltpu.SemaphoreType.DMA((6 + 2 * BLOCKS,))],
+        compiler_params=pltpu.CompilerParams(collective_id=1, has_side_effects=True, vmem_limit_bytes=60 * 2**20),
+        name="gather_attend",
+    )(counts, tokens, small, qw, kw, vw, ow, up, down)
+
+
+def scatter_edge(width):
+    return 128 if width == 768 else width // 4
+
+
+def feed_kernel(dp_total, n, counts_ref, mixed_ref, tokens_ref, cot_ref, outw_ref, vec_ref, up_hbm, down_hbm,
+                layer_ref, gres_ref, gmix_ref, gout_ref, gup_ref, gdown_ref, gvec_ref,
+                res_s, si_s, gb_s, hid_s, gi_s, up_s, down_s, ub_s, gub_s, gup_s, *rest):
+    rows, feat = tokens_ref.shape
+    width = gi_s.shape[1]
+    piece = gdown_ref.shape[0] // BLOCKS
+    place = Place(dp_total, n)
+    B, pairs = place.inner_total, place.pairs
+    per = 5 if pairs == 1 else 7
+    uterm_s, dterm_s = rest[:2]
+    ubufs, dbufs = rest[2:2 + per], rest[2 + per:2 + 2 * per]
+    send_sem, recv_sem, loc_sem = rest[2 + 2 * per:]
+    load = lambda j: (pltpu.make_async_copy(up_hbm.at[j], up_s.at[j], loc_sem.at[2 * j]),
+                      pltpu.make_async_copy(down_hbm.at[j], down_s.at[j], loc_sem.at[2 * j + 1]))
+    for j in range(BLOCKS):
+        for c in load(j):
+            c.start()
+    count = Scatter.count(B, pairs)
+
+    def unit_u(j):
+        def emit(cols, value):
+            gup_s[j, :, cols] = value
+        return Scatter(place, uterm_s.at[j % 2], [b.at[j] for b in ubufs], scatter_edge(width), emit,
+                       (send_sem, recv_sem), 2 * j * count)
+
+    def unit_d(j):
+        def emit(cols, value):
+            gdown_ref[pl.ds(pl.multiple_of(j * piece, 8), piece), cols] = value
+        return Scatter(place, dterm_s.at[j % 2], [b.at[j] for b in dbufs], scatter_edge(feat), emit,
+                       (send_sem, recv_sem), (2 * j + 1) * count)
+
+    def last(unit):
+        unit.from_last()
+        unit.from_pairs()
+
+    obias, gain, shift, dbias = (vec_ref[i:i + 1, :] for i in range(4, 8))
+    ub = jnp.concatenate([vec_ref[8 + i:9 + i, :] for i in range(BLOCKS * width // feat)], axis=1)
+    for j, part in enumerate(split_columns(jnp.broadcast_to(ub, (8, ub.shape[1])), n)):
+        ub_s[j] = part
+
+    def begin(i, _):
+        first = pl.multiple_of(i * RB, RB)
+        sl = pl.ds(first, RB)
+        res = tokens_ref[sl, :].astype(f32) + (dot(mixed_ref[sl, :], outw_ref[...]) + obias)
+        res_s[sl, :] = res
+        xhat, _q = norm_parts(res)
+        si_s[sl, :] = (xhat * gain + shift).astype(bf16)
+        gb_s[sl, :] = jnp.where(live_mask(counts_ref, first, RB), cot_ref[sl, :], jnp.zeros((), bf16))
+        gres_ref[sl, :] = jnp.zeros((RB, feat), f32)
+        return 0
+
+    lax.fori_loop(0, rows // RB, begin, 0)
+    greet(place.neighbours(pairs=True))
+
+    def block(j, _):
+        for c in load(j):
+            c.wait()
+        upw = lambda: up_s[j].reshape(feat, width)
+        downw = lambda: down_s[j].reshape(width, feat)
+        cols = pl.ds(pl.multiple_of(j * width, 128), width)
+        gub_s[j] = jnp.zeros(gub_s.shape[1:], f32)
+
+        def after(back, when, todo):
+            @pl.when(when & (j >= back))
+            def _():
+                todo(j - back)
+
+        def rows_piece(i, _):
+            sl = pl.ds(pl.multiple_of(i * RB, RB), RB)
+            pre = dot(si_s[sl, :], upw()) + ub_s[j, 0:1, :]
+            cdf = 0.5 + 0.5 * lax.erf(pre * INV_SQRT2)
+            pdf = jnp.exp(-0.5 * pre * pre) * INV_SQRT2PI
+            hid_s[sl, cols] = (pre * cdf).astype(bf16)
+            gi = (dot_nt(gb_s[sl, :], downw()) * (cdf + pre * pdf)).astype(bf16)
+            gi_s[sl, :] = gi
+            gub_s[j, 0:1, :] += jnp.sum(gi.astype(f32), axis=0, keepdims=True)
+            after(1, i == 0, lambda k: unit_u(k).from_twin())
+            after(2, i == 0, lambda k: unit_u(k).from_outer())
+            after(2, i == 1, lambda k: last(unit_d(k)))
+            after(2, i == 2, lambda k: last(unit_u(k)))
+            after(1, i == 3, lambda k: unit_d(k).from_inner())
+            return 0
+
+        lax.fori_loop(0, rows // RB, rows_piece, 0)
+        always = j >= 0
+
+        @pl.when(j >= 2)
+        def _():
+            for c in unit_u(j - 2).copies("core") + unit_d(j - 2).copies("core"):
+                c.wait_send()
+
+        dterm_s[j % 2] = dot_tn(hid_s[:, cols], gb_s[...]).astype(bf16).reshape(dterm_s.shape[1:])
+        unit_d(j).start()
+        after(1, always, lambda k: unit_u(k).from_inner())
+        uterm_s[j % 2] = dot_tn(si_s[...], gi_s[...]).astype(bf16).reshape(uterm_s.shape[1:])
+        unit_u(j).start()
+        unit_d(j).from_core()
+        gres_ref[...] += dot_nt(gi_s[...], upw())
+        unit_u(j).from_core()
+        unit_d(j).from_twin()
+        after(1, always, lambda k: unit_d(k).from_outer())
+        return 0
+
+    lax.fori_loop(0, BLOCKS, block, 0)
+    end, before = BLOCKS - 1, BLOCKS - 2
+    gvec_ref[...] = jnp.zeros_like(gvec_ref)
+
+    def finish_rows(i, _):
+        first = pl.multiple_of(i * RB, RB)
+        sl = pl.ds(first, RB)
+        res = res_s[sl, :]
+        layer = res + (dot(hid_s[sl, :], down_s[...].reshape(BLOCKS * width, feat)) + dbias)
+        layer_ref[sl, :] = jnp.where(live_mask(counts_ref, first, RB), layer, 0.0).astype(bf16)
+        xhat, q = norm_parts(res)
+        gs = gres_ref[sl, :]
+        t = gs * gain
+        gb = gb_s[sl, :].astype(f32)
+        gres = gb + q * (t - jnp.mean(t, axis=-1, keepdims=True) - xhat * jnp.mean(t * xhat, axis=-1, keepdims=True))
+        gres_ref[sl, :] = gres
+        ga = gres.astype(bf16)
+        si_s[sl, :] = ga
+        gvec_ref[7:8, :] += jnp.sum(gb, axis=0, keepdims=True)
+        gvec_ref[5:6, :] += jnp.sum(gs * xhat, axis=0, keepdims=True)
+        gvec_ref[6:7, :] += jnp.sum(gs, axis=0, keepdims=True)
+        gvec_ref[4:5, :] += jnp.sum(ga.astype(f32), axis=0, keepdims=True)
+        gmix_ref[sl, :] = dot_nt(ga, outw_ref[...]).astype(bf16)
+
+        def at(k, *todo):
+            @pl.when(i == k)
+            def _():
+                for one in todo:
+                    one()
+
+        at(0, unit_u(end).from_twin, unit_u(before).from_outer)
+        at(1, lambda: last(unit_d(before)))
+        at(2, lambda: last(unit_u(before)), unit_d(end).from_inner)
+        return 0
+
+    lax.fori_loop(0, rows // RB, finish_rows, 0)
+    unit_u(end).from_inner()
+    gout_ref[...] = dot_tn(mixed_ref[...], si_s[...]).astype(bf16)
+    total = join_columns([gub_s[j] for j in range(BLOCKS)], n)
+    for i in range(total.shape[1] // feat):
+        gvec_ref[8 + i:9 + i, :] = total[0:1, i * feat:(i + 1) * feat]
+    unit_d(end).from_outer()
+    unit_u(end).from_outer()
+    last(unit_d(end))
+    last(unit_u(end))
+    gup_ref[...] = join_columns([gup_s[j] for j in range(BLOCKS)], n)
+
+    def drain(j, _):
+        for unit in (unit_u(j), unit_d(j)):
+            for stage in ("twin", "inner", "outer", "last") + (("pairs",) if pairs > 1 else ()):
+                for c in unit.copies(stage):
+                    c.wait_send()
+
+            @pl.when(j >= BLOCKS - 2)
+            def _(unit=unit):
+                for c in unit.copies("core"):
+                    c.wait_send()
+        return 0
+
+    lax.fori_loop(0, BLOCKS, drain, 0)
+
+
+def feed_forward(sizes, counts, mixed, tokens, cot, outw, vec, up_all, down_all):
+    dp_total, n = sizes
+    rows, feat = tokens.shape
+    B, pairs = n // 8, dp_total // 2
+    own, width = up_all.shape[-2:]
+    piece = down_all.shape[-2]
+    s = jax.ShapeDtypeStruct
+    vm = pl.BlockSpec(memory_space=pltpu.VMEM)
+    anyspec = pl.BlockSpec(memory_space=pl.ANY)
+    act = lambda dt: pltpu.VMEM((rows, feat), dt)
+    copies = 2 * BLOCKS * Scatter.count(B, pairs)
+    return pl.pallas_call(
+        functools.partial(feed_kernel, dp_total, n),
+        in_specs=[pl.BlockSpec(memory_space=pltpu.SMEM)] + [vm] * 5 + [anyspec] * 2,
+        out_specs=[vm] * 7,
+        out_shape=[s((rows, feat), bf16), s((rows, feat), f32), s((rows, feat), bf16), s((feat, feat), bf16),
+                   s((own, BLOCKS * width), f32), s((BLOCKS * piece, feat), f32), s(vec.shape, f32)],
+        scratch_shapes=[act(f32), act(bf16), act(bf16), pltpu.VMEM((rows, BLOCKS * width), bf16),
+                        pltpu.VMEM((rows, width), bf16), pltpu.VMEM(up_all.shape, bf16),
+                        pltpu.VMEM(down_all.shape, bf16), pltpu.VMEM((BLOCKS, 8, width), f32),
+                        pltpu.VMEM((BLOCKS, 8, width), f32), pltpu.VMEM((BLOCKS, own, width), f32),
+                        pltpu.VMEM((2,) + up_all.shape[1:], bf16), pltpu.VMEM((2,) + down_all.shape[1:], bf16)]
+        + Scatter.shapes(B, pairs, own, width, scatter_edge(width), (BLOCKS,))
+        + Scatter.shapes(B, pairs, piece, feat, scatter_edge(feat), (BLOCKS,))
+        + [pltpu.SemaphoreType.DMA((copies,)), pltpu.SemaphoreType.DMA((copies,)),
+           pltpu.SemaphoreType.DMA((2 * BLOCKS,))],
+        compiler_params=pltpu.CompilerParams(collective_id=2, has_side_effects=True, vmem_limit_bytes=67043328),
+        name="feed_forward",
+    )(counts, mixed, tokens, cot, outw, vec, up_all, down_all)
+
+
+def back_kernel(dp_total, n, edges, tokens_ref, vec_ref, gres_ref, dq_ref, dk_ref, dv_ref, w_ref, oterm_ref, small_ref,
+                gtok_ref, gq_ref, gk_ref, gv_ref, go_ref, total_ref,
+                fi_s, small_s, qterm_s, kterm_s, vterm_s, *rest):
+    place = Place(dp_total, n)
+    B, pairs = place.inner_total, place.pairs
+    rows, feat = tokens_ref.shape
+    own = gq_ref.shape[0]
+    per = 5 if pairs == 1 else 7
+    send_sem, recv_sem = rest[-2:]
+    sems = (send_sem, recv_sem)
+
+    def into(ref):
+        def emit(cols, value):
+            ref[:, cols] = value
+        return emit
+
+    pieces = [(oterm_ref, go_ref), (qterm_s, gq_ref), (kterm_s, gk_ref), (vterm_s, gv_ref)]
+    o, q, k, v = [Scatter(place, term, rest[i * per:(i + 1) * per], edges[i], into(out), sems,
+                          i * Scatter.count(B, pairs)) for i, (term, out) in enumerate(pieces)]
+    small = Total(place, small_s, rest[4 * per:4 * per + 2], total_ref, sems, 4 * Scatter.count(B, pairs))
+    gain, shift = vec_ref[0:1, :], vec_ref[1:2, :]
+    greet(place.neighbours(pairs=True))
+    o.start()
+
+    def norm_rows(i, _):
+        sl = pl.ds(pl.multiple_of(i * RB, RB), RB)
+        xhat, _q = norm_parts(tokens_ref[sl, :].astype(f32))
+        fi_s[sl, :] = (xhat * gain + shift).astype(bf16)
+        return 0
+
+    lax.fori_loop(0, rows // RB, norm_rows, 0)
+    grad = lambda d: dot_tn(fi_s[...], d[...]).astype(bf16).reshape(qterm_s.shape)
+    o.from_core()
+    qterm_s[...] = grad(dq_ref)
+    q.start()
+    o.from_twin()
+    kterm_s[...] = grad(dk_ref)
+    k.start()
+    q.from_core()
+    vterm_s[...] = grad(dv_ref)
+    v.start()
+    k.from_core()
+    q.from_twin()
+    small_s[...] = small_ref[...]
+
+    def back_rows(i, _):
+        sl = pl.ds(pl.multiple_of(i * RB, RB), RB)
+        dq, dk, dv = dq_ref[sl, :], dk_ref[sl, :], dv_ref[sl, :]
+        weight = lambda i: w_ref[:, :, :, i * own:(i + 1) * own, :].reshape(feat, feat)
+        gs = dot_nt(dq, weight(0)) + dot_nt(dk, weight(1)) + dot_nt(dv, weight(2))
+        xhat, q_ = norm_parts(tokens_ref[sl, :].astype(f32))
+        t = gs * gain
+        gtok_ref[sl, :] = gres_ref[sl, :] + q_ * (t - jnp.mean(t, axis=-1, keepdims=True)
+                                                  - xhat * jnp.mean(t * xhat, axis=-1, keepdims=True))
+        for r, a in enumerate((gs * xhat, gs, dq.astype(f32), dv.astype(f32))):
+            small_s[r:r + 1, :] += jnp.sum(a, axis=0, keepdims=True)
+
+        def at(j, *todo):
+            @pl.when(i == j)
+            def _():
+                for one in todo:
+                    one()
+
+        at(0, v.from_core, k.from_twin, o.from_inner)
+        at(1, v.from_twin, q.from_inner)
+        at(2, o.from_outer)
+        at(3, k.from_inner)
+        return 0
+
+    lax.fori_loop(0, rows // RB, back_rows, 0)
+
+    def last(unit):
+        unit.from_last()
+        unit.from_pairs()
+
+    small.start()
+    steps = small.steps()
+    steps[0]()
+    v.from_inner()
+    q.from_outer()
+    steps[1]()
+    last(o)
+    k.from_outer()
+    steps[2]()
+    last(q)
+    v.from_outer()
+    for one in steps[3:]:
+        one()
+    last(k)
+    last(v)
+    for unit in (o, q, k, v, small):
+        unit.finish()
+
+
+def project_back(sizes, tokens, vec, gres, dq, dk, dv, qkv_all, gout, small):
+    dp_total, n = sizes
+    rows, feat = tokens.shape
+    B, pairs = n // 8, dp_total // 2
+    own = feat // n
+    edges = (128, 256, 128, 256)
+    s = jax.ShapeDtypeStruct
+    vm = pl.BlockSpec(memory_space=pltpu.VMEM)
+    term = (4, B, 2, own, feat)
+    scratch = [pltpu.VMEM((rows, feat), bf16), pltpu.VMEM(small.shape, f32)] + [pltpu.VMEM(term, bf16)] * 3
+    for e in edges:
+        scratch += Scatter.shapes(B, pairs, own, feat, e)
+    scratch += Total.shapes(B, pairs, small.shape)
+    copies = 4 * Scatter.count(B, pairs) + Total.count(B, pairs)
+    scratch += [pltpu.SemaphoreType.DMA((copies,))] * 2
+    return pl.pallas_call(
+        functools.partial(back_kernel, dp_total, n, edges),
+        in_specs=[vm] * 9, out_specs=[vm] * 6,
+        out_shape=[s((rows, feat), f32)] + [s((own, feat), f32)] * 4 + [s(small.shape, f32)],
+        scratch_shapes=scratch,
+        compiler_params=pltpu.CompilerParams(collective_id=3, has_side_effects=True, vmem_limit_bytes=60 * 2**20),
+        name="project_back",
+    )(tokens, vec, gres, dq, dk, dv, qkv_all, gout.reshape(term), small)
+
 FSDP="fsdp"
 
-def on_device(tokens, image_counts, cotangent, first_gain, first_shift, query_weight, query_bias, key_weight,
+def spread(vectors, index, total):
+    own = vectors.shape[-1]
+    at = lax.broadcasted_iota(jnp.int32, (1, total, own), 1)
+    wide = jnp.where(at == index, vectors[:, None, :], jnp.zeros((), vectors.dtype))
+    return wide.reshape(vectors.shape[0], total * own)
+
+def on_device(sizes, tokens, image_counts, cotangent, first_gain, first_shift, query_weight, query_bias, key_weight,
               value_weight, value_bias, out_weight, out_bias, second_gain, second_shift, up_weight, up_bias,
               down_weight, down_bias):
     rows, feat = tokens.shape
     own = query_weight.shape[0]
     n = feat // own
     counts = image_counts[0]
-    gather = lambda a: lax.all_gather(a, FSDP, axis=0, tiled=False)
-    small = jnp.concatenate([jnp.stack([first_gain, first_shift, query_bias, value_bias, out_bias, second_gain, second_shift, down_bias]),
-        up_bias.reshape(-1, own)])
-    small_all = gather(small)
-    attn_all = gather(jnp.stack([query_weight, key_weight, value_weight, out_weight]))
-    full = lambda i: attn_all[:, i].reshape(feat, feat)
-    qw, kw, vw, ow = full(0), full(1), full(2), full(3)
-    up = gather(up_weight).reshape(feat, -1)
-    down = gather(down_weight).reshape(-1, feat)
-    wide = jnp.transpose(small_all[:, :8], (1, 0, 2)).reshape(8, feat).astype(f32)
-    ub = small_all[:, 8:].reshape(1, -1).astype(f32)
-    vec1 = wide[0:4]
-    vec2 = wide[4:8]
-    fi, q, k, v = project(tokens, vec1, qw, kw, vw)
-    mixed, lse = attn_fwd(counts, q, k, v)
-    layer_out, gres, gmix, gup, gub, gdown, gout, gv2 = middle(counts, mixed, tokens, cotangent, ow, vec2, up, ub, down)
+    me = lax.axis_index(FSDP)
+    eight = jnp.stack([first_gain, first_shift, query_bias, value_bias, out_bias, second_gain, second_shift, down_bias])
+    small = jnp.concatenate([spread(eight, me, n), spread(up_bias[None], me, n).reshape(-1, feat)])
+    small = jnp.concatenate([small, jnp.zeros((16 - small.shape[0], feat), bf16)])
+    q, k, v, vec, mixed, lse, qkv_all, o_all, up_all, down_all, _ = gather_attend(
+        sizes, counts, tokens, small, query_weight, key_weight, value_weight, out_weight, up_weight, down_weight)
+    layer_out, gres, gmix, gout, gup, gdown, gvec = feed_forward(
+        sizes, counts, mixed, tokens, cotangent, o_all.reshape(feat, feat), vec, up_all, down_all)
     dq, dk, dv = attn_bwd(counts, q, k, v, gmix, lse)
-    gtok, gq, gk, gv, gv1 = project_back(tokens, vec1, gres, fi, dq, dk, dv, qw, kw, vw)
-    scatter = lambda a: lax.psum_scatter(a, FSDP, scatter_dimension=0, tiled=False)
-    pair = lambda a: lax.psum(a, "dp").astype(f32)
-    su = scatter(gup.reshape(n, own, -1))
-    sd = scatter(gdown.reshape(n, -1, feat))
-    sa = scatter(jnp.stack([g.reshape(n, own, feat) for g in (gq, gk, gv, gout)], axis=1))
-    smalls = jnp.concatenate([gv1[0:4], gv2[0:4]]).reshape(8, n, own)
-    smalls = jnp.concatenate([jnp.transpose(smalls, (1, 0, 2)), gub.reshape(n, -1, own)], axis=1).astype(bf16)
-    ss = scatter(smalls)
-    su, sd, sa, ss = (pair(a) for a in (su, sd, sa, ss))
-    return (layer_out, gtok, ss[0], ss[1], sa[0], ss[2], sa[1], sa[2], ss[3], sa[3], ss[7], ss[5], ss[6], su,
-            ss[8:].reshape(-1), sd, ss[4])
+    gtok, gq, gk, gv, go, total = project_back(sizes, tokens, vec, gres, dq, dk, dv, qkv_all, gout, gvec)
+    mine = lax.dynamic_index_in_dim(total[:8].reshape(8, n, own), me, 1, keepdims=False)
+    ub_mine = lax.dynamic_index_in_dim(total[8:12].reshape(n, -1), me, 0, keepdims=False)
+    return (layer_out, gtok, mine[0], mine[1], gq, mine[2], gk, gv, mine[3], go, mine[4], mine[5], mine[6],
+            gup, ub_mine, gdown, mine[7])
 
 
 def solution(mesh):
@@ -350,7 +1269,7 @@
     mat = P("fsdp", None)
     vec = P("fsdp")
     return jax.shard_map(
-        on_device,
+        functools.partial(on_device, (mesh.shape["dp"], mesh.shape["fsdp"])),
         mesh=mesh,
         in_specs=(rows, rows, rows, vec, vec, mat, vec, mat, mat, vec, mat, vec, vec, vec, mat, vec, mat, vec),
         out_specs=(rows, rows, vec, vec, mat, vec, mat, mat, vec, mat, vec, vec, vec, mat, vec, mat, vec),

time: 559 us -> 301 us (0.54)
  waiting for transfers between devices: 363 us -> 0 us
  Pallas kernels: 131 us -> 286 us
  blocking collectives: 28.5 us -> 0 us
  between operations: 14.2 us -> 0.73 us
  other arithmetic: 9.21 us -> 0.65 us
    reduce_scatter x4 -> x0, waiting for transfers between devices: 228 us -> none  [on_device(): lax.psum_scatter(a, FSDP, scatter_dimension=0, tiled=False)]
    pallas_call x4 -> x3, Pallas kernels: 94 us -> 249 us  [the longest x1 97.9 us: gather_attend(): pl.pallas_call(functools.partial(gather_kernel, dp_total, n), in_specs=[p...]
    all_gather x3 -> x0, waiting for transfers between devices: 101 us -> none  [on_device(): gather = lambda a: lax.all_gather(a, FSDP, axis=0, tiled=False)]
    psum x1 -> x0, waiting for transfers between devices: 32.2 us -> none  [on_device(): pair = lambda a: lax.psum(a, 'dp').astype(f32)]
    all_gather x1 -> x0, blocking collectives: 23.5 us -> none  [on_device(): gather = lambda a: lax.all_gather(a, FSDP, axis=0, tiled=False)]
    unnamed x8 -> x24, local copies, waits for them, and re-layouts: 0.01 us -> 8.42 us
    slice x9 -> x2, local copies, waits for them, and re-layouts: 7.47 us -> 1.48 us  [the longest x1 0.74 us: on_device(): total[:8].reshape(8, n, own)]
    another operation x3 -> x0, other arithmetic: 5.76 us -> none  [the longest x1 3.98 us: on_device(): jnp.stack([g.reshape(n, own, feat) for g in (gq, gk, gv, gout)], axis=1)]
  transfers between devices with their start and end apart: 8 -> 0, of which waited for: 8 -> 0; matrix products, arithmetic and copies ran while one was open for 3% -> 0% of each run, Pallas kernels for 15% -> 0%
where the time goes in v5:
time: 301 us; the launch traced here: 300 us
  Pallas kernels  286 us (95%)
  local copies, waits for them, and re-layouts  13.2 us (4%)
    pallas_call x1, Pallas kernels, gather_attend(): pl.pallas_call(functools.partial(gather_kernel, dp_total, n), in_specs=[p...  97.9 us
    pallas_call x1, Pallas kernels, feed_forward(): pl.pallas_call(functools.partial(feed_kernel, dp_total, n), in_specs=[pl....  93.5 us
    pallas_call x1, Pallas kernels, project_back(): pl.pallas_call(functools.partial(back_kernel, dp_total, n, edges), in_spe...  57.6 us
    pallas_call x1, Pallas kernels, attn_bwd(): pl.pallas_call(bwd_kernel, grid_spec=pltpu.PrefetchScalarGridSpec(num_sca...  36.6 us
    unnamed x24, local copies, waits for them, and re-layouts  8.42 us

profile of v5, /device:TPU:0, one launch (start us, length us, event | category | flops | bytes accessed | tf_op | source)
XLA Modules:
  0.0 300.2 jit_solution(2078243669279147041)
XLA Ops:
  0.7 0.1 broadcast_in_dim.44
  0.7 0.1 broadcast_in_dim.45
  0.8 0.8 stack.35
  1.6 0.1 broadcast_in_dim.48
  1.8 0.1 iota.11
  1.8 0.1 iota.12
  1.9 0.7 broadcast_in_dim.50
  2.6 0.1 broadcast_in_dim.51
  2.7 0.6 pad_maximum_fusion.small_ref
  3.3 97.9 %gather_attend.1 = (bf16[1024,768]{1,0:T(8,128)(2,1)}, bf16[1024,768]{1,0:T(8,128)(2,1)}, bf16[1024,768]{1,0:T(8,128)(2,1)}, f32[16,768]{1,0:T(8,128)}, bf16[102...) custom-call(s32[2]{0:T(128)} %bitcast.32, ...), custom_call_target="tpu_custom_call" | custom-call | tf_op jit(solution)/shard_map/gather_attend/pallas_call | solution.py:902
  101.2 93.5 %feed_forward.1 = (bf16[1024,768]{1,0:T(8,128)(2,1)}, f32[1024,768]{1,0:T(8,128)}, bf16[1024,768]{1,0:T(8,128)(2,1)}, bf16[768,768]{1,0:T(8,128)(2,1)}, f32[48,3...) custom-call(s32[2]{0:T(128)} %bitcast.33, bf16[1024,768]{1,0:T(8,128)(2,1)} %get-tuple-element.43.mixed_ref, ...), custom_call_target="tpu_custom_call" | custom-call | tf_op jit(solution)/shard_map/feed_forward/pallas_call | solution.py:1098
  194.8 36.6 %attend_back.1 = (bf16[1024,768]{1,0:T(8,128)(2,1)}, bf16[1024,768]{1,0:T(8,128)(2,1)}, bf16[1024,768]{1,0:T(8,128)(2,1)}) custom-call(s32[2]{0:T(128)} %bitcast.34, bf16[1024,768]{1,0:T(8,128)(2,1)} %get-tuple-element.50.q_ref, bf16[1024,768]{1,0:T(8,128)(2,1)} %get-tuple-element.51.k_ref, bf16[1024,768]{1,0:T(8,128)(2,1)} %get-tuple-element.52.v_ref, ...), custom_call_target="tpu_custom_call" | custom-call | tf_op jit(solution)/shard_map/attend_back/pallas_call | solution.py:151
  231.3 57.6 %project_back.1 = (f32[1024,768]{1,0:T(8,128)}, f32[48,768]{1,0:T(8,128)}, f32[48,768]{1,0:T(8,128)}, f32[48,768]{1,0:T(8,128)}, f32[48,768]{1,0:T(8,128)}, /*index=5*/f32[16,768]{1,0:T(8,128)}) custom-call(bf16[1024,768]{1,0:T(8,128)(2,1)} %tokens_ref.3, f32[16,768]{1,0:T(8,128)} %get-tuple-element.45.vec_ref, f32[1024,768]{1,0:T(8,128)} %get-tuple-element.49.gres_ref, ...), custom_call_target="tpu_custom_call" | custom-call | tf_op jit(solution)/shard_map/project_back/pallas_call | solution.py:1227
  289.0 0.7 slice.38
  289.7 0.1 reshape.83
  289.8 0.6 fusion
  290.4 0.7 slice.46
  291.1 0.1 reshape.84
  291.2 0.6 constant_dynamic-slice_fusion.7
  291.8 0.0 copy-done.1
  291.8 1.1 copy.43
  292.9 1.3 copy-done
  294.2 1.7 copy.44
  295.9 0.0 copy-done.7
  295.9 0.7 copy.45
  296.6 0.0 copy-done.6
  296.6 0.7 copy.46
  297.2 0.7 copy.47
  297.9 0.0 copy-done.4
  297.9 0.7 copy.48
  298.6 0.8 copy.49
  299.4 0.8 copy.50
  (16 shorter events, 0.1 us)
Async XLA Ops:
  231.3 60.4 %copy-start.1 = (bf16[1024,768]{1,0:T(8,128)(2,1)S(1)}, bf16[1024,768]{1,0:T(8,128)(2,1)}, u32[]{:S(2)}) copy-start(bf16[1024,768]{1,0:T(8,128)(2,1)} %get-tuple-element.94) | copy-start | bytes 4718596
  291.8 2.5 copy-start
  294.2 1.7 copy-start.7
  294.2 2.3 copy-start.6
  294.2 3.0 %copy-start.5 = (f32[48,768]{1,0:T(8,128)S(1)}, f32[48,768]{1,0:T(8,128)}, u32[]{:S(2)}) copy-start(f32[48,768]{1,0:T(8,128)} %get-tuple-element.101) | copy-start | bytes 442372
  294.2 3.7 %copy-start.4 = (f32[48,768]{1,0:T(8,128)S(1)}, f32[48,768]{1,0:T(8,128)}, u32[]{:S(2)}) copy-start(f32[48,768]{1,0:T(8,128)} %get-tuple-element.103) | copy-start | bytes 442372
  295.9 2.7 copy-start.3
  295.9 3.5 %copy-start.2 = (f32[192,768]{1,0:T(8,128)S(1)}, f32[192,768]{1,0:T(8,128)}, u32[]{:S(2)}) copy-start(f32[192,768]{1,0:T(8,128)} %get-tuple-element.109) | copy-start | bytes 1769476

commit v6 on v5

--- a/solution.py
+++ b/solution.py
@@ -916,58 +916,106 @@
 
 
 def scatter_edge(width):
-    return 128 if width == 768 else width // 4
-
-
-def feed_kernel(dp_total, n, counts_ref, mixed_ref, tokens_ref, cot_ref, outw_ref, vec_ref, up_hbm, down_hbm,
-                layer_ref, gres_ref, gmix_ref, gout_ref, gup_ref, gdown_ref, gvec_ref,
-                res_s, si_s, gb_s, hid_s, gi_s, up_s, down_s, ub_s, gub_s, gup_s, *rest):
+    return 128 if width == 768 else width // 4 if width % 512 == 0 else width // 3
+
+
+def key_lanes(keys, ends):
+    lane = lax.broadcasted_iota(jnp.int32, keys.shape, 1)
+    image = image_of(lax.broadcasted_iota(jnp.int32, keys.shape, 0), ends)
+    return [jnp.where((lane < 64) == (e == 0), keys, jnp.where(image == lane - 64 * (1 - e), 0.0, NEG).astype(bf16))
+            for e in range(2)]
+
+
+def query_lanes(queries, first, ends, e):
+    lane = lax.broadcasted_iota(jnp.int32, queries.shape, 1)
+    image = image_of(first + lax.broadcasted_iota(jnp.int32, queries.shape, 0), ends)
+    return jnp.where((lane < 64) == (e == 0), queries, jnp.where(image == lane - 64 * (1 - e), 1.0, 0.0).astype(bf16))
+
+
+def layer_kernel(dp_total, n, counts_ref, mixed_hbm, tokens_ref, cot_hbm, outw_ref, vec_ref, lse_ref, up_hbm, down_hbm,
+                 q_hbm, k_hbm, v_hbm, qkv_all,
+                 layer_ref, gtok_ref, gup_ref, gdown_ref, gq_ref, gk_ref, gv_ref, go_ref, total_ref,
+                 res_s, si_s, gb_s, mixed_s, hid_s, gi_s, up_s, down_s, kt_s, ub_s, gub_s, gqkv_s, small_s, *rest):
     rows, feat = tokens_ref.shape
     width = gi_s.shape[1]
+    own = gq_ref.shape[0]
     piece = gdown_ref.shape[0] // BLOCKS
+    heads = feat // 128
     place = Place(dp_total, n)
     B, pairs = place.inner_total, place.pairs
     per = 5 if pairs == 1 else 7
     uterm_s, dterm_s = rest[:2]
-    ubufs, dbufs = rest[2:2 + per], rest[2 + per:2 + 2 * per]
-    send_sem, recv_sem, loc_sem = rest[2 + 2 * per:]
+    ubufs, dbufs, obufs, abufs = (rest[2 + i * per:2 + (i + 1) * per] for i in range(4))
+    total_bufs = rest[2 + 4 * per:4 + 4 * per]
+    send_sem, recv_sem, loc_sem = rest[4 + 4 * per:]
+    sems = (send_sem, recv_sem)
+    count = Scatter.count(B, pairs)
+    wide = lambda start: pl.ds(start, feat)
     load = lambda j: (pltpu.make_async_copy(up_hbm.at[j], up_s.at[j], loc_sem.at[2 * j]),
                       pltpu.make_async_copy(down_hbm.at[j], down_s.at[j], loc_sem.at[2 * j + 1]))
+    at_end = 3 * feat
+    first_loads = [local(mixed_hbm, mixed_s, loc_sem.at[2 * BLOCKS]),
+                   local(cot_hbm, hid_s.at[:, wide(at_end)], loc_sem.at[2 * BLOCKS + 1])]
     for j in range(BLOCKS):
         for c in load(j):
             c.start()
-    count = Scatter.count(B, pairs)
 
     def unit_u(j):
         def emit(cols, value):
-            gup_s[j, :, cols] = value
-        return Scatter(place, uterm_s.at[j % 2], [b.at[j] for b in ubufs], scatter_edge(width), emit,
-                       (send_sem, recv_sem), 2 * j * count)
+            gup_ref[:, pl.ds(pl.multiple_of(j * width + cols.start, 128), cols.size)] = value
+        return Scatter(place, uterm_s.at[j % 2], [b.at[j] for b in ubufs], scatter_edge(width), emit, sems,
+                       2 * j * count)
 
     def unit_d(j):
         def emit(cols, value):
             gdown_ref[pl.ds(pl.multiple_of(j * piece, 8), piece), cols] = value
-        return Scatter(place, dterm_s.at[j % 2], [b.at[j] for b in dbufs], scatter_edge(feat), emit,
-                       (send_sem, recv_sem), (2 * j + 1) * count)
+        return Scatter(place, dterm_s.at[j % 2], [b.at[j] for b in dbufs], scatter_edge(feat), emit, sems,
+                       (2 * j + 1) * count)
+
+    def emit_out(cols, value):
+        go_ref[:, cols] = value
+
+    unit_o = Scatter(place, uterm_s.at[1, :, :, :, :, wide(0)], obufs, 256, emit_out, sems, 2 * BLOCKS * count)
+
+    def pair_term(p):
+        return dterm_s.at[1, :, :, :, pl.ds(0, own), pl.ds(pl.multiple_of(p % 2 * 384, 128), 384)]
+
+    def unit_a(p):
+        def emit(cols, value):
+            gqkv_s[p, :, cols] = value
+        return Scatter(place, pair_term(p), [b.at[p] for b in abufs], 128, emit, sems,
+                       (2 * BLOCKS + 1 + p) * count)
+
+    small = Total(place, small_s, total_bufs, total_ref, sems, (2 * BLOCKS + 1 + heads) * count)
 
     def last(unit):
         unit.from_last()
         unit.from_pairs()
 
+    def sent(unit, *stages):
+        for stage in stages:
+            for c in unit.copies(stage):
+                c.wait_send()
+
+    rest_stages = ("twin", "inner", "outer", "last") + (("pairs",) if pairs > 1 else ())
+    gain_one, shift_one = vec_ref[0:1, :], vec_ref[1:2, :]
     obias, gain, shift, dbias = (vec_ref[i:i + 1, :] for i in range(4, 8))
     ub = jnp.concatenate([vec_ref[8 + i:9 + i, :] for i in range(BLOCKS * width // feat)], axis=1)
     for j, part in enumerate(split_columns(jnp.broadcast_to(ub, (8, ub.shape[1])), n)):
         ub_s[j] = part
+    small_s[...] = jnp.zeros_like(small_s)
+    for c in first_loads:
+        c.wait()
 
     def begin(i, _):
         first = pl.multiple_of(i * RB, RB)
         sl = pl.ds(first, RB)
-        res = tokens_ref[sl, :].astype(f32) + (dot(mixed_ref[sl, :], outw_ref[...]) + obias)
+        res = tokens_ref[sl, :].astype(f32) + (dot(mixed_s[sl, :], outw_ref[...]) + obias)
         res_s[sl, :] = res
         xhat, _q = norm_parts(res)
         si_s[sl, :] = (xhat * gain + shift).astype(bf16)
-        gb_s[sl, :] = jnp.where(live_mask(counts_ref, first, RB), cot_ref[sl, :], jnp.zeros((), bf16))
-        gres_ref[sl, :] = jnp.zeros((RB, feat), f32)
+        gb_s[sl, :] = jnp.where(live_mask(counts_ref, first, RB), hid_s[sl, wide(at_end)], jnp.zeros((), bf16))
+        gtok_ref[sl, :] = jnp.zeros((RB, feat), f32)
         return 0
 
     lax.fori_loop(0, rows // RB, begin, 0)
@@ -1004,19 +1052,14 @@
 
         lax.fori_loop(0, rows // RB, rows_piece, 0)
         always = j >= 0
-
-        @pl.when(j >= 2)
-        def _():
-            for c in unit_u(j - 2).copies("core") + unit_d(j - 2).copies("core"):
-                c.wait_send()
-
+        after(2, always, lambda k: (sent(unit_u(k), "core"), sent(unit_d(k), "core")))
         dterm_s[j % 2] = dot_tn(hid_s[:, cols], gb_s[...]).astype(bf16).reshape(dterm_s.shape[1:])
         unit_d(j).start()
         after(1, always, lambda k: unit_u(k).from_inner())
         uterm_s[j % 2] = dot_tn(si_s[...], gi_s[...]).astype(bf16).reshape(uterm_s.shape[1:])
         unit_u(j).start()
         unit_d(j).from_core()
-        gres_ref[...] += dot_nt(gi_s[...], upw())
+        gtok_ref[...] += dot_nt(gi_s[...], upw())
         unit_u(j).from_core()
         unit_d(j).from_twin()
         after(1, always, lambda k: unit_d(k).from_outer())
@@ -1024,7 +1067,8 @@
 
     lax.fori_loop(0, BLOCKS, block, 0)
     end, before = BLOCKS - 1, BLOCKS - 2
-    gvec_ref[...] = jnp.zeros_like(gvec_ref)
+    weights = [local(qkv_all.at[:, :, :, pl.ds(i * own, own)], up_s.at[i, :, :, :, :, wide(0)], loc_sem.at[i])
+               for i in range(3)]
 
     def finish_rows(i, _):
         first = pl.multiple_of(i * RB, RB)
@@ -1033,18 +1077,18 @@
         layer = res + (dot(hid_s[sl, :], down_s[...].reshape(BLOCKS * width, feat)) + dbias)
         layer_ref[sl, :] = jnp.where(live_mask(counts_ref, first, RB), layer, 0.0).astype(bf16)
         xhat, q = norm_parts(res)
-        gs = gres_ref[sl, :]
+        gs = gtok_ref[sl, :]
         t = gs * gain
         gb = gb_s[sl, :].astype(f32)
         gres = gb + q * (t - jnp.mean(t, axis=-1, keepdims=True) - xhat * jnp.mean(t * xhat, axis=-1, keepdims=True))
-        gres_ref[sl, :] = gres
+        gtok_ref[sl, :] = gres
         ga = gres.astype(bf16)
         si_s[sl, :] = ga
-        gvec_ref[7:8, :] += jnp.sum(gb, axis=0, keepdims=True)
-        gvec_ref[5:6, :] += jnp.sum(gs * xhat, axis=0, keepdims=True)
-        gvec_ref[6:7, :] += jnp.sum(gs, axis=0, keepdims=True)
-        gvec_ref[4:5, :] += jnp.sum(ga.astype(f32), axis=0, keepdims=True)
-        gmix_ref[sl, :] = dot_nt(ga, outw_ref[...]).astype(bf16)
+        small_s[7:8, :] += jnp.sum(gb, axis=0, keepdims=True)
+        small_s[5:6, :] += jnp.sum(gs * xhat, axis=0, keepdims=True)
+        small_s[6:7, :] += jnp.sum(gs, axis=0, keepdims=True)
+        small_s[4:5, :] += jnp.sum(ga.astype(f32), axis=0, keepdims=True)
+        hid_s[sl, wide(at_end)] = dot_nt(ga, outw_ref[...]).astype(bf16)
 
         def at(k, *todo):
             @pl.when(i == k)
@@ -1058,180 +1102,200 @@
         return 0
 
     lax.fori_loop(0, rows // RB, finish_rows, 0)
+    take = [local(x, hid_s.at[:, wide(i * feat)], loc_sem.at[3 + i]) for i, x in enumerate((q_hbm, k_hbm, v_hbm))]
+    sent(unit_u(before), "core")
+    sent(unit_d(before), "core")
+    unit_o.terms[...] = dot_tn(mixed_s[...], si_s[...]).astype(bf16).reshape(unit_o.terms.shape)
+    unit_o.start()
     unit_u(end).from_inner()
-    gout_ref[...] = dot_tn(mixed_ref[...], si_s[...]).astype(bf16)
-    total = join_columns([gub_s[j] for j in range(BLOCKS)], n)
-    for i in range(total.shape[1] // feat):
-        gvec_ref[8 + i:9 + i, :] = total[0:1, i * feat:(i + 1) * feat]
-    unit_d(end).from_outer()
-    unit_u(end).from_outer()
-    last(unit_d(end))
-    last(unit_u(end))
-    gup_ref[...] = join_columns([gup_s[j] for j in range(BLOCKS)], n)
+    gub = join_columns([gub_s[j] for j in range(BLOCKS)], n)
+    for i in range(gub.shape[1] // feat):
+        small_s[8 + i:9 + i, :] = gub[0:1, i * feat:(i + 1) * feat]
+
+    def norm_rows(i, _):
+        sl = pl.ds(pl.multiple_of(i * RB, RB), RB)
+        xhat, _q = norm_parts(tokens_ref[sl, :].astype(f32))
+        gi_s[sl, wide(0)] = (xhat * gain_one + shift_one).astype(bf16)
+        return 0
+
+    lax.fori_loop(0, rows // RB, norm_rows, 0)
+    for c in take:
+        c.wait()
+    ends = image_ends(counts_ref[0], counts_ref[1], rows)
+    key_at = lambda e: pl.ds(feat + e * 128, 128)
+    dk_at, dv_at = pl.ds(0, 128), pl.ds(128, 128)
+
+    def pair(p, _):
+        part = lambda which: pl.ds(pl.multiple_of(which * feat + p * 128, 128), 128)
+        cols = part(0)
+        keys = hid_s[:, part(1)]
+        for e, x in enumerate(key_lanes(keys, ends)):
+            gi_s[:, key_at(e)] = x
+        kt_s[...] = keys.T
+        res_s[:, pl.ds(0, 256)] = jnp.zeros((rows, 256), f32)
+
+        def attend_back(b, _):
+            first = pl.multiple_of(b * QB, QB)
+            sl = pl.ds(first, QB)
+            q, do = hid_s[sl, part(0)], hid_s[sl, part(3)]
+            v = hid_s[:, part(2)]
+            lane = lax.broadcasted_iota(jnp.int32, q.shape, 1)
+            zero = jnp.zeros_like(q)
+            dqs = []
+            dks = dvs = None
+            for e in range(2):
+                mask = (lane < 64) == (e == 0)
+                qm, dom = jnp.where(mask, q, zero), jnp.where(mask, do, zero)
+                s = dot_nt(gi_s[:, key_at(e)], query_lanes(q, first, ends, e))
+                probs = jnp.exp(s - lse_ref[p, e:e + 1, sl])
+                dp = dot_nt(v, dom)
+                centre = jnp.sum(probs * dp, axis=0, keepdims=True)
+                ds = (probs * (dp - centre)).astype(bf16)
+                dv_e = dot(probs.astype(bf16), dom)
+                dk_e = dot(ds, qm)
+                dqs.append(dot(kt_s[e * 64:(e + 1) * 64, :], ds))
+                dvs = dv_e if dvs is None else dvs + dv_e
+                dks = dk_e if dks is None else dks + dk_e
+            res_s[:, dk_at] += dks
+            res_s[:, dv_at] += dvs
+            gb_s[sl, cols] = (jnp.concatenate(dqs, axis=0).T * 0.125).astype(bf16)
+
+            def at(k, when, todo):
+                @pl.when((b == k) & when)
+                def _():
+                    todo()
+
+            at(0, p == 0, unit_o.from_core)
+            at(1, p == 0, lambda: unit_d(end).from_outer())
+            at(2, p == 0, unit_o.from_twin)
+            at(3, p == 0, lambda: unit_u(end).from_outer())
+            at(0, p == 1, lambda: last(unit_d(end)))
+            at(1, p == 1, lambda: (last(unit_u(end)), unit_o.from_inner()))
+            at(3, p == 1, unit_o.from_outer)
+            at(0, p == 2, lambda: last(unit_o))
+            at(0, p >= 3, lambda: last(unit_a(p - 3)))
+            at(0, p >= 1, lambda: unit_a(p - 1).from_core())
+            at(1, p >= 2, lambda: unit_a(p - 2).from_inner())
+            at(2, p >= 1, lambda: unit_a(p - 1).from_twin())
+            at(3, p >= 2, lambda: unit_a(p - 2).from_outer())
+            return 0
+
+        lax.fori_loop(0, rows // QB, attend_back, 0)
+        dk, dv = res_s[:, dk_at].astype(bf16), res_s[:, dv_at].astype(bf16)
+        mixed_s[:, cols] = dk
+        si_s[:, cols] = dv
+        both = jnp.concatenate([gb_s[:, cols], dk, dv], axis=1)
+
+        @pl.when(p >= 2)
+        def _():
+            sent(unit_a(p - 2), "core")
+
+        term = pair_term(p)
+        term[...] = dot_tn(gi_s[:, wide(0)], both).astype(bf16).reshape(term.shape)
+        unit_a(p).start()
+        return 0
+
+    lax.fori_loop(0, heads, pair, 0)
+    for c in weights:
+        c.wait()
+
+    def back_rows(i, _):
+        sl = pl.ds(pl.multiple_of(i * RB, RB), RB)
+        dq, dk, dv = gb_s[sl, :], mixed_s[sl, :], si_s[sl, :]
+        weight = lambda i: up_s[i, :, :, :, :, wide(0)].reshape(feat, feat)
+        gs = dot_nt(dq, weight(0)) + dot_nt(dk, weight(1)) + dot_nt(dv, weight(2))
+        xhat, q = norm_parts(tokens_ref[sl, :].astype(f32))
+        t = gs * gain_one
+        gtok_ref[sl, :] += q * (t - jnp.mean(t, axis=-1, keepdims=True)
+                                - xhat * jnp.mean(t * xhat, axis=-1, keepdims=True))
+        for r, a in enumerate((gs * xhat, gs, dq.astype(f32), dv.astype(f32))):
+            small_s[r:r + 1, :] += jnp.sum(a, axis=0, keepdims=True)
+
+        def at(k, *todo):
+            @pl.when(i == k)
+            def _():
+                for one in todo:
+                    one()
+
+        at(0, lambda: last(unit_a(heads - 3)), lambda: unit_a(heads - 1).from_core())
+        at(1, lambda: unit_a(heads - 2).from_inner())
+        at(2, lambda: unit_a(heads - 1).from_twin())
+        at(3, lambda: unit_a(heads - 2).from_outer())
+        return 0
+
+    lax.fori_loop(0, rows // RB, back_rows, 0)
+    steps = small.steps()
+    small.start()
+    unit_a(heads - 1).from_inner()
+    steps[0]()
+    last(unit_a(heads - 2))
+    steps[1]()
+    unit_a(heads - 1).from_outer()
+    gup_ref[...] = join_columns([gup_ref[:, j * width:(j + 1) * width] for j in range(BLOCKS)], n)
+    steps[2]()
+    last(unit_a(heads - 1))
+    for one in steps[3:]:
+        one()
+    for p in range(heads):
+        for i, ref in enumerate((gq_ref, gk_ref, gv_ref)):
+            ref[:, p * 128:(p + 1) * 128] = gqkv_s[p, :, i * 128:(i + 1) * 128]
 
     def drain(j, _):
-        for unit in (unit_u(j), unit_d(j)):
-            for stage in ("twin", "inner", "outer", "last") + (("pairs",) if pairs > 1 else ()):
-                for c in unit.copies(stage):
-                    c.wait_send()
-
-            @pl.when(j >= BLOCKS - 2)
-            def _(unit=unit):
-                for c in unit.copies("core"):
-                    c.wait_send()
+        sent(unit_u(j), *rest_stages)
+        sent(unit_d(j), *rest_stages)
         return 0
 
     lax.fori_loop(0, BLOCKS, drain, 0)
-
-
-def feed_forward(sizes, counts, mixed, tokens, cot, outw, vec, up_all, down_all):
+    sent(unit_u(end), "core")
+    sent(unit_d(end), "core")
+    sent(unit_o, "core", *rest_stages)
+
+    def drain_pairs(p, _):
+        sent(unit_a(p), *rest_stages)
+
+        @pl.when(p >= heads - 2)
+        def _():
+            sent(unit_a(p), "core")
+        return 0
+
+    lax.fori_loop(0, heads, drain_pairs, 0)
+    small.finish()
+
+
+def layer_back(sizes, counts, mixed, tokens, cot, outw, vec, lse, up_all, down_all, q, k, v, qkv_all):
     dp_total, n = sizes
     rows, feat = tokens.shape
     B, pairs = n // 8, dp_total // 2
     own, width = up_all.shape[-2:]
     piece = down_all.shape[-2]
+    heads = feat // 128
     s = jax.ShapeDtypeStruct
     vm = pl.BlockSpec(memory_space=pltpu.VMEM)
     anyspec = pl.BlockSpec(memory_space=pl.ANY)
-    act = lambda dt: pltpu.VMEM((rows, feat), dt)
-    copies = 2 * BLOCKS * Scatter.count(B, pairs)
+    act = lambda dt, cols=feat: pltpu.VMEM((rows, cols), dt)
+    copies = (2 * BLOCKS + 1 + heads) * Scatter.count(B, pairs) + Total.count(B, pairs)
     return pl.pallas_call(
-        functools.partial(feed_kernel, dp_total, n),
-        in_specs=[pl.BlockSpec(memory_space=pltpu.SMEM)] + [vm] * 5 + [anyspec] * 2,
-        out_specs=[vm] * 7,
-        out_shape=[s((rows, feat), bf16), s((rows, feat), f32), s((rows, feat), bf16), s((feat, feat), bf16),
-                   s((own, BLOCKS * width), f32), s((BLOCKS * piece, feat), f32), s(vec.shape, f32)],
-        scratch_shapes=[act(f32), act(bf16), act(bf16), pltpu.VMEM((rows, BLOCKS * width), bf16),
-                        pltpu.VMEM((rows, width), bf16), pltpu.VMEM(up_all.shape, bf16),
-                        pltpu.VMEM(down_all.shape, bf16), pltpu.VMEM((BLOCKS, 8, width), f32),
-                        pltpu.VMEM((BLOCKS, 8, width), f32), pltpu.VMEM((BLOCKS, own, width), f32),
+        functools.partial(layer_kernel, dp_total, n),
+        in_specs=[pl.BlockSpec(memory_space=pltpu.SMEM), anyspec, vm, anyspec, vm, vm, vm] + [anyspec] * 6,
+        out_specs=[vm] * 9,
+        out_shape=[s((rows, feat), bf16), s((rows, feat), f32), s((own, BLOCKS * width), f32),
+                   s((BLOCKS * piece, feat), f32)] + [s((own, feat), f32)] * 4 + [s(vec.shape, f32)],
+        scratch_shapes=[act(f32), act(bf16), act(bf16), act(bf16), act(bf16, BLOCKS * width), act(bf16, width),
+                        pltpu.VMEM(up_all.shape, bf16), pltpu.VMEM(down_all.shape, bf16),
+                        pltpu.VMEM((128, rows), bf16), pltpu.VMEM((BLOCKS, 8, width), f32),
+                        pltpu.VMEM((BLOCKS, 8, width), f32), pltpu.VMEM((heads, own, 384), f32),
+                        pltpu.VMEM(vec.shape, f32),
                         pltpu.VMEM((2,) + up_all.shape[1:], bf16), pltpu.VMEM((2,) + down_all.shape[1:], bf16)]
         + Scatter.shapes(B, pairs, own, width, scatter_edge(width), (BLOCKS,))
         + Scatter.shapes(B, pairs, piece, feat, scatter_edge(feat), (BLOCKS,))
+        + Scatter.shapes(B, pairs, own, feat, 256)
+        + Scatter.shapes(B, pairs, own, 384, 128, (heads,))
+        + Total.shapes(B, pairs, vec.shape)
         + [pltpu.SemaphoreType.DMA((copies,)), pltpu.SemaphoreType.DMA((copies,)),
-           pltpu.SemaphoreType.DMA((2 * BLOCKS,))],
+           pltpu.SemaphoreType.DMA((2 * BLOCKS + 2,))],
         compiler_params=pltpu.CompilerParams(collective_id=2, has_side_effects=True, vmem_limit_bytes=67043328),
-        name="feed_forward",
-    )(counts, mixed, tokens, cot, outw, vec, up_all, down_all)
-
-
-def back_kernel(dp_total, n, edges, tokens_ref, vec_ref, gres_ref, dq_ref, dk_ref, dv_ref, w_ref, oterm_ref, small_ref,
-                gtok_ref, gq_ref, gk_ref, gv_ref, go_ref, total_ref,
-                fi_s, small_s, qterm_s, kterm_s, vterm_s, *rest):
-    place = Place(dp_total, n)
-    B, pairs = place.inner_total, place.pairs
-    rows, feat = tokens_ref.shape
-    own = gq_ref.shape[0]
-    per = 5 if pairs == 1 else 7
-    send_sem, recv_sem = rest[-2:]
-    sems = (send_sem, recv_sem)
-
-    def into(ref):
-        def emit(cols, value):
-            ref[:, cols] = value
-        return emit
-
-    pieces = [(oterm_ref, go_ref), (qterm_s, gq_ref), (kterm_s, gk_ref), (vterm_s, gv_ref)]
-    o, q, k, v = [Scatter(place, term, rest[i * per:(i + 1) * per], edges[i], into(out), sems,
-                          i * Scatter.count(B, pairs)) for i, (term, out) in enumerate(pieces)]
-    small = Total(place, small_s, rest[4 * per:4 * per + 2], total_ref, sems, 4 * Scatter.count(B, pairs))
-    gain, shift = vec_ref[0:1, :], vec_ref[1:2, :]
-    greet(place.neighbours(pairs=True))
-    o.start()
-
-    def norm_rows(i, _):
-        sl = pl.ds(pl.multiple_of(i * RB, RB), RB)
-        xhat, _q = norm_parts(tokens_ref[sl, :].astype(f32))
-        fi_s[sl, :] = (xhat * gain + shift).astype(bf16)
-        return 0
-
-    lax.fori_loop(0, rows // RB, norm_rows, 0)
-    grad = lambda d: dot_tn(fi_s[...], d[...]).astype(bf16).reshape(qterm_s.shape)
-    o.from_core()
-    qterm_s[...] = grad(dq_ref)
-    q.start()
-    o.from_twin()
-    kterm_s[...] = grad(dk_ref)
-    k.start()
-    q.from_core()
-    vterm_s[...] = grad(dv_ref)
-    v.start()
-    k.from_core()
-    q.from_twin()
-    small_s[...] = small_ref[...]
-
-    def back_rows(i, _):
-        sl = pl.ds(pl.multiple_of(i * RB, RB), RB)
-        dq, dk, dv = dq_ref[sl, :], dk_ref[sl, :], dv_ref[sl, :]
-        weight = lambda i: w_ref[:, :, :, i * own:(i + 1) * own, :].reshape(feat, feat)
-        gs = dot_nt(dq, weight(0)) + dot_nt(dk, weight(1)) + dot_nt(dv, weight(2))
-        xhat, q_ = norm_parts(tokens_ref[sl, :].astype(f32))
-        t = gs * gain
-        gtok_ref[sl, :] = gres_ref[sl, :] + q_ * (t - jnp.mean(t, axis=-1, keepdims=True)
-                                                  - xhat * jnp.mean(t * xhat, axis=-1, keepdims=True))
-        for r, a in enumerate((gs * xhat, gs, dq.astype(f32), dv.astype(f32))):
-            small_s[r:r + 1, :] += jnp.sum(a, axis=0, keepdims=True)
-
-        def at(j, *todo):
-            @pl.when(i == j)
-            def _():
-                for one in todo:
-                    one()
-
-        at(0, v.from_core, k.from_twin, o.from_inner)
-        at(1, v.from_twin, q.from_inner)
-        at(2, o.from_outer)
-        at(3, k.from_inner)
-        return 0
-
-    lax.fori_loop(0, rows // RB, back_rows, 0)
-
-    def last(unit):
-        unit.from_last()
-        unit.from_pairs()
-
-    small.start()
-    steps = small.steps()
-    steps[0]()
-    v.from_inner()
-    q.from_outer()
-    steps[1]()
-    last(o)
-    k.from_outer()
-    steps[2]()
-    last(q)
-    v.from_outer()
-    for one in steps[3:]:
-        one()
-    last(k)
-    last(v)
-    for unit in (o, q, k, v, small):
-        unit.finish()
-
-
-def project_back(sizes, tokens, vec, gres, dq, dk, dv, qkv_all, gout, small):
-    dp_total, n = sizes
-    rows, feat = tokens.shape
-    B, pairs = n // 8, dp_total // 2
-    own = feat // n
-    edges = (128, 256, 128, 256)
-    s = jax.ShapeDtypeStruct
-    vm = pl.BlockSpec(memory_space=pltpu.VMEM)
-    term = (4, B, 2, own, feat)
-    scratch = [pltpu.VMEM((rows, feat), bf16), pltpu.VMEM(small.shape, f32)] + [pltpu.VMEM(term, bf16)] * 3
-    for e in edges:
-        scratch += Scatter.shapes(B, pairs, own, feat, e)
-    scratch += Total.shapes(B, pairs, small.shape)
-    copies = 4 * Scatter.count(B, pairs) + Total.count(B, pairs)
-    scratch += [pltpu.SemaphoreType.DMA((copies,))] * 2
-    return pl.pallas_call(
-        functools.partial(back_kernel, dp_total, n, edges),
-        in_specs=[vm] * 9, out_specs=[vm] * 6,
-        out_shape=[s((rows, feat), f32)] + [s((own, feat), f32)] * 4 + [s(small.shape, f32)],
-        scratch_shapes=scratch,
-        compiler_params=pltpu.CompilerParams(collective_id=3, has_side_effects=True, vmem_limit_bytes=60 * 2**20),
-        name="project_back",
-    )(tokens, vec, gres, dq, dk, dv, qkv_all, gout.reshape(term), small)
+        name="layer_back",
+    )(counts, mixed, tokens, cot, outw, vec, lse, up_all, down_all, q, k, v, qkv_all)
 
 FSDP="fsdp"
 
@@ -1254,10 +1318,8 @@
     small = jnp.concatenate([small, jnp.zeros((16 - small.shape[0], feat), bf16)])
     q, k, v, vec, mixed, lse, qkv_all, o_all, up_all, down_all, _ = gather_attend(
         sizes, counts, tokens, small, query_weight, key_weight, value_weight, out_weight, up_weight, down_weight)
-    layer_out, gres, gmix, gout, gup, gdown, gvec = feed_forward(
-        sizes, counts, mixed, tokens, cotangent, o_all.reshape(feat, feat), vec, up_all, down_all)
-    dq, dk, dv = attn_bwd(counts, q, k, v, gmix, lse)
-    gtok, gq, gk, gv, go, total = project_back(sizes, tokens, vec, gres, dq, dk, dv, qkv_all, gout, gvec)
+    layer_out, gtok, gup, gdown, gq, gk, gv, go, total = layer_back(
+        sizes, counts, mixed, tokens, cotangent, o_all.reshape(feat, feat), vec, lse, up_all, down_all, q, k, v, qkv_all)
     mine = lax.dynamic_index_in_dim(total[:8].reshape(8, n, own), me, 1, keepdims=False)
     ub_mine = lax.dynamic_index_in_dim(total[8:12].reshape(n, -1), me, 0, keepdims=False)
     return (layer_out, gtok, mine[0], mine[1], gq, mine[2], gk, gv, mine[3], go, mine[4], mine[5], mine[6],

time: 301 us -> 281 us (0.934)
  Pallas kernels: 286 us -> 266 us
    pallas_call x3 -> x1, Pallas kernels: 188 us -> 168 us  [layer_back(): pl.pallas_call(functools.partial(layer_kernel, dp_total, n), in_specs=[pl...]
    unnamed x24 -> x22, local copies, waits for them, and re-layouts: 8.42 us -> 8.77 us
where the time goes in v6:
time: 281 us
  Pallas kernels  266 us (95%)
  local copies, waits for them, and re-layouts  13.5 us (5%)
    pallas_call x1, Pallas kernels, layer_back(): pl.pallas_call(functools.partial(layer_kernel, dp_total, n), in_specs=[pl...  168 us
    pallas_call x1, Pallas kernels, gather_attend(): pl.pallas_call(functools.partial(gather_kernel, dp_total, n), in_specs=[p...  97.9 us
    unnamed x22, local copies, waits for them, and re-layouts  8.77 us

profile of v6, /device:TPU:0, one launch (start us, length us, event | category | flops | bytes accessed | tf_op | source)
XLA Modules:
  0.0 280.5 jit_solution(8763221885476132149)
XLA Ops:
  0.7 0.1 broadcast_in_dim.44
  0.7 0.1 broadcast_in_dim.45
  0.8 0.8 stack.35
  1.6 0.1 broadcast_in_dim.48
  1.8 0.1 iota.11
  1.8 0.1 iota.12
  1.9 0.7 broadcast_in_dim.50
  2.6 0.1 broadcast_in_dim.51
  2.7 0.6 pad_maximum_fusion.small_ref
  3.3 97.9 %gather_attend.1 = (bf16[1024,768]{1,0:T(8,128)(2,1)}, bf16[1024,768]{1,0:T(8,128)(2,1)}, bf16[1024,768]{1,0:T(8,128)(2,1)}, f32[16,768]{1,0:T(8,128)}, bf16[102...) custom-call(s32[2]{0:T(128)} %bitcast.30, ...), custom_call_target="tpu_custom_call" | custom-call | tf_op jit(solution)/shard_map/gather_attend/pallas_call | solution.py:902
  101.2 167.7 %layer_back.1 = (bf16[1024,768]{1,0:T(8,128)(2,1)}, f32[1024,768]{1,0:T(8,128)}, f32[48,3072]{1,0:T(8,128)}, f32[192,768]{1,0:T(8,128)}, f32[48,768]{1,0:T(8,128...) custom-call(s32[2]{0:T(128)} %bitcast.31, ...), custom_call_target="tpu_custom_call" | custom-call | tf_op jit(solution)/shard_map/layer_back/pallas_call | solution.py:1277
  269.0 0.7 slice.38
  269.7 0.1 reshape.79
  269.8 0.6 fusion
  270.4 0.7 slice.46
  271.1 0.1 reshape.80
  271.2 0.6 constant_dynamic-slice_fusion.7
  271.7 2.8 copy.43
  274.5 0.0 copy-done
  274.6 0.0 copy-start.3
  274.6 1.7 copy.44
  276.2 0.0 copy-done.6
  276.2 0.7 copy.45
  276.9 0.0 copy-done.5
  276.9 0.7 copy.46
  277.6 0.0 copy-done.4
  277.6 0.7 copy.47
  278.2 0.0 copy-done.3
  278.2 0.7 copy.48
  278.9 0.0 copy-done.2
  278.9 0.8 copy.49
  279.7 0.8 copy.50
  (12 shorter events, 0.1 us)
Async XLA Ops:
  271.7 2.8 copy-start
  274.6 1.7 copy-start.6
  274.6 2.4 copy-start.5
  274.6 3.0 %copy-start.4 = (f32[48,768]{1,0:T(8,128)S(1)}, f32[48,768]{1,0:T(8,128)}, u32[]{:S(2)}) copy-start(f32[48,768]{1,0:T(8,128)} %get-tuple-element.87) | copy-start | bytes 442372
  274.6 3.7 %copy-start.3 = (f32[48,768]{1,0:T(8,128)S(1)}, f32[48,768]{1,0:T(8,128)}, u32[]{:S(2)}) copy-start(f32[48,768]{1,0:T(8,128)} %get-tuple-element.89) | copy-start | bytes 442372
  276.2 2.7 copy-start.2
  276.2 3.5 %copy-start.1 = (f32[192,768]{1,0:T(8,128)S(1)}, f32[192,768]{1,0:T(8,128)}, u32[]{:S(2)}) copy-start(f32[192,768]{1,0:T(8,128)} %get-tuple-element.95) | copy-start | bytes 1769476

commit v7 on v6

v7 whole, which is shorter than its diff:
```python
import functools
import math

import jax
import jax.numpy as jnp
from jax import lax
from jax.experimental import pallas as pl
from jax.experimental.pallas import tpu as pltpu
from jax.sharding import PartitionSpec as P

EPS = 1e-06
NT = (((1,), (1,)), ((), ()))
TN = (((0,), (0,)), ((), ()))


SMALL_ROWS=197; LARGE_ROWS=325
QB=256
NEG=-1e30

def image_ends(small, large, rows):
    ends=[]
    for i in range(1, rows//SMALL_ROWS+1):
        e = jnp.minimum(i, small)*SMALL_ROWS + jnp.maximum(i-small,0)*LARGE_ROWS
        ends.append(jnp.where(i<=small+large, e, 2*rows))
    return ends

def image_of(places, ends):
    idx = jnp.zeros(places.shape, jnp.int32)
    for e in ends:
        idx = idx + (places>=e).astype(jnp.int32)
    return idx


f32=jnp.float32; bf16=jnp.bfloat16
RB=256
INV_SQRT2=1/math.sqrt(2.0); INV_SQRT2PI=1/math.sqrt(2*math.pi)

def dot(a,b): return jnp.dot(a,b,preferred_element_type=f32)
def dot_nt(a,b): return lax.dot_general(a,b,NT,preferred_element_type=f32)
def dot_tn(a,b): return lax.dot_general(a,b,TN,preferred_element_type=f32)

def norm_parts(x):
    mean=jnp.mean(x,axis=-1,keepdims=True)
    cen=x-mean
    var=jnp.mean(cen*cen,axis=-1,keepdims=True)
    q=lax.rsqrt(var+EPS)
    return cen*q, q

def live_mask(counts_ref, first, n):
    end=counts_ref[0]*197+counts_ref[1]*325
    r=first+lax.broadcasted_iota(jnp.int32,(n,1),0)
    return r<end


MESH = pl.DeviceIdType.MESH


class Place:
    def __init__(self, dp_total, fsdp_total):
        half = fsdp_total // 2
        self.outer_total = 4
        self.inner_total = half // 4
        assert half % 4 == 0
        self.pairs = dp_total // 2
        self.d = lax.axis_index("dp")
        self.f = lax.axis_index("fsdp")
        self.core = self.f % 2
        self.inner = (self.f // 2) % self.inner_total
        self.outer = self.f // (2 * self.inner_total)
        self.side = self.d % 2
        self.twin = self.d + 1 - 2 * self.side
        self.flip = self.outer // 2
        self.mirror = self.unmirror(self.outer)

        B = self.inner_total
        self.outers = [self.outer] + [(self.outer + s) % 4 for s in range(1, 4)]
        self.inners = [self.inner] + [(self.inner + t) % B for t in range(1, B)]
        self.cores = [self.core, 1 - self.core]
        self.ends = [self.unmirror(0), self.unmirror(1), self.unmirror(2)]
        self.next_outer = self.unmirror(1 - self.mirror)
        self.arrivals = [self.outer, self.next_outer, self.ends[2], self.unmirror(3)]
        self.outer_devices = [self.device(o, self.inner, self.core) for o in self.outers]
        self.inner_devices = [self.device(self.outer, i, self.core) for i in self.inners]
        self.core_device = self.device(self.outer, self.inner, self.cores[1])
        self.twin_device = (self.twin, self.f)
        self.pair_devices = [(self.d, self.f)] + [(self.side + 2 * ((self.d // 2 + k) % self.pairs), self.f)
                                                  for k in range(1, self.pairs)]

    def unmirror(self, at):
        return at + self.flip * (3 - 2 * at)

    def device(self, outer, inner, core):
        return (self.d, (outer * self.inner_total + inner) * 2 + core)

    def at_outer(self, outer):
        return self.device(outer, self.inner, self.core)

    def at_inner(self, t):
        return self.inner_devices[t % self.inner_total]

    def other_core(self):
        return self.core_device

    def at_twin(self):
        return self.twin_device

    def me(self):
        return (self.d, self.f)

    def at_pair(self, k):
        return self.pair_devices[k % self.pairs]

    def neighbours(self, pairs=False):
        out = self.outer_devices[1:]
        out += [self.at_inner(t) for t in range(1, self.inner_total)]
        out += [self.at_twin(), self.other_core()]
        if pairs:
            out = self.outer_devices[1:] + Total.near_devices(self)
            out += [self.at_pair(k) for k in range(1, self.pairs)]
        return out


def greet(others):
    barrier = pltpu.get_barrier_semaphore()
    for other in others:
        pl.semaphore_signal(barrier, inc=1, device_id=other, device_id_type=MESH)
    pl.semaphore_wait(barrier, len(others))


class Gather:
    def __init__(self, place, ref, edge, sems, base):
        self.place, self.ref, self.edge = place, ref, edge
        self.rows = ref.shape[-2]
        self.send_sem, self.recv_sem = sems
        self.base = base
        A, B = place.outer_total, place.inner_total
        keys = [("z", s) for s in range(1, A)] + [("Z", s) for s in range(1, A)]
        keys += [("x", s, t) for s in range(A) for t in range(1, B)]
        keys += [("y", t) for t in range(B)]
        keys += [("c",)]
        self.keys = {key: i for i, key in enumerate(keys)}
        self.sent = []
        self.sent_inside = []

    @staticmethod
    def count(B):
        return 6 + 4 * (B - 1) + B + 1

    def rows_of(self, kind):
        e, r, p = self.edge, self.rows, self.place.side
        if not e or kind == "all":
            return pl.ds(0, r)
        start, size = {"plane": (p * e, r - e), "mine": (p * (r - e), e), "theirs": ((1 - p) * (r - e), e)}[kind]
        return pl.ds(pl.multiple_of(start, 8), size)

    def part(self, outer, inner, core, kind):
        return self.ref.at[outer, inner, core, self.rows_of(kind)]

    def copy(self, key, ref, to):
        i = self.base + self.keys[key]
        into = i
        if key[0] == "Z":
            into = self.base + self.keys["z", 2 if key[1] == 2 else 3]
        return pltpu.make_async_remote_copy(src_ref=ref, dst_ref=ref, send_sem=self.send_sem.at[i],
                                            recv_sem=self.recv_sem.at[into], device_id=to, device_id_type=MESH)

    def send(self, key, make):
        self.copy(key, *make()).start()
        self.sent.append((key, make))

    def send_inside(self, key, make):
        @pl.when(self.place.mirror == 1)
        def _():
            self.copy(key, *make()).start()

        self.sent_inside.append((key, make))

    def got(self, key, ref):
        self.copy(key, ref, self.place.me()).wait_recv()

    def outer_of(self, step):
        return self.place.arrivals[step]

    def own_line(self, step):
        p = self.place
        return self.part(self.outer_of(step), p.inner, p.core, "plane")

    def start(self):
        p = self.place
        self.send(("z", 1), lambda: (self.own_line(0), p.at_outer(p.next_outer)))
        self.send_inside(("z", 2), lambda: (self.own_line(0), p.at_outer(p.ends[2])))
        self.pass_inner(0)

    def pass_inner(self, step):
        p = self.place
        for t in range(1, p.inner_total):
            self.send(("x", step, t), lambda t=t: (self.own_line(step), p.at_inner(-t)))

    def onward(self, step):
        p = self.place
        return self.own_line(step), p.at_outer(p.ends[2 if step == 1 else 0])

    def arrived(self, step, record):
        self.got(("z", step), self.own_line(step))
        kept = list(self.sent)
        self.pass_inner(step)
        if step == 3:
            self.pass_twin(0)
        if not record:
            self.sent = kept

    def from_next(self):
        self.arrived(1, True)
        self.send_inside(("Z", 1), functools.partial(self.onward, 1))

    def relay(self, step):
        @pl.when(self.place.mirror == 1)
        def _():
            self.got(("z", step), self.own_line(step))
            self.copy(("Z", step), *self.onward(step)).start()
            kept = list(self.sent)
            self.pass_inner(step)
            if step == 3:
                self.pass_twin(0)
            self.sent = kept

        self.sent_inside.append((("Z", step), functools.partial(self.onward, step)))

    def take(self, step):
        @pl.when(self.place.mirror == 0)
        def _():
            self.arrived(step, False)

        for t in range(1, self.place.inner_total):
            self.sent.append((("x", step, t), lambda t=t: (self.own_line(step), self.place.at_inner(-t))))
        if step == 3 and self.edge:
            self.sent.append((("y", 0), lambda: (self.line(0, "mine"), self.place.at_twin())))

    def relay_2(self):
        self.relay(2)

    def relay_3(self):
        self.relay(3)

    def take_2(self):
        self.take(2)

    def take_3(self):
        self.take(3)

    def line(self, t, kind):
        p = self.place
        return self.part(slice(None), p.inners[t], p.core, kind)

    def pass_twin(self, t):
        if self.edge:
            self.send(("y", t), lambda: (self.line(t, "mine"), self.place.at_twin()))

    def from_inner(self):
        p = self.place
        for t in range(1, p.inner_total):
            for step in range(4):
                self.got(("x", step, t), self.part(self.outer_of(step), p.inners[t], p.core, "plane"))
            self.pass_twin(t)

    def half(self, core):
        return self.part(slice(None), slice(None), core, "all")

    def from_twin(self):
        p = self.place
        if self.edge:
            for t in range(p.inner_total):
                self.got(("y", t), self.line(t, "theirs"))
        self.send(("c",), lambda: (self.half(p.core), p.other_core()))

    def from_core(self):
        self.got(("c",), self.half(self.place.cores[1]))

    def finish(self):
        for key, make in self.sent:
            self.copy(key, *make()).wait_send()

        @pl.when(self.place.mirror == 1)
        def _():
            for key, make in self.sent_inside:
                self.copy(key, *make()).wait_send()


class Scatter:
    def __init__(self, place, terms, bufs, edge, emit, sems, base):
        self.place, self.terms, self.edge, self.emit = place, terms, edge, emit
        self.sums, self.twin_buf, self.inner_buf, self.outer_buf, self.last_buf = bufs[:5]
        self.pair_bufs = bufs[5:]
        self.send_sem, self.recv_sem = sems
        self.base = base
        p, e, w = place.side, edge, terms.shape[-1]
        at = lambda start, size: pl.ds(pl.multiple_of(start, 128), size)
        self.plane = at(p * e, w - e)
        self.mine = at(p * (w - e), e)
        self.theirs = at((1 - p) * (w - e), e)
        self.twin_plane = at((1 - p) * e, w - e)
        self.middle = pl.ds(e, w - 2 * e)

    @staticmethod
    def count(B, pairs):
        return 1 + 1 + (B - 1) + 3 + 1 + (pairs - 1)

    @staticmethod
    def shapes(B, pairs, rows, width, edge, lead=()):
        out = [(4, B, rows, width), (4, B, rows, edge), (B - 1, 4, rows, width), (3, rows, width), (rows, width)]
        if pairs > 1:
            out += [(rows, width), (pairs - 1, rows, width)]
        return [pltpu.VMEM(tuple(lead) + s, bf16) for s in out]

    def copy(self, i, src, dst, to):
        return pltpu.make_async_remote_copy(src_ref=src, dst_ref=dst, send_sem=self.send_sem.at[self.base + i],
                                            recv_sem=self.recv_sem.at[self.base + i], device_id=to, device_id_type=MESH)

    def copies(self, stage):
        p = self.place
        A, B = 4, p.inner_total
        if stage == "core":
            return [self.copy(0, self.terms.at[:, :, p.cores[1]], self.sums, p.other_core())]
        if stage == "twin":
            return [self.copy(1, self.sums.at[:, :, :, self.theirs], self.twin_buf, p.at_twin())]
        if stage == "inner":
            return [self.copy(1 + t, self.sums.at[:, p.inners[(B - t) % B], :, self.plane],
                              self.inner_buf.at[t - 1, :, :, self.plane], p.at_inner(-t)) for t in range(1, B)]
        if stage == "outer":
            return [self.copy(B + s, self.sums.at[p.outers[A - s], p.inner, :, self.plane],
                              self.outer_buf.at[s - 1, :, self.plane], p.outer_devices[A - s])
                    for s in range(1, A)]
        if stage == "last":
            return [self.copy(A + B, self.sums.at[p.outer, p.inner, :, self.plane], self.last_buf.at[:, self.plane],
                              p.at_twin())]
        half, others = self.pair_bufs
        return [self.copy(A + B + k, half, others.at[k - 1], p.at_pair(p.pairs - k)) for k in range(1, p.pairs)]

    def go(self, stage):
        for c in self.copies(stage):
            c.start()

    def got(self, i, dst):
        self.copy(i, dst, dst, self.place.me()).wait_recv()

    def start(self):
        self.go("core")

    def from_core(self):
        p = self.place
        B = p.inner_total
        self.got(0, self.sums)

        def add(i, _):
            a, b = i // B, i % B
            self.sums[a, b] = self.sums[a, b] + self.terms[a, b, p.core]
            return 0

        lax.fori_loop(0, 4 * B, add, 0)
        self.go("twin")

    def from_twin(self):
        p = self.place
        B = p.inner_total
        self.got(1, self.twin_buf)

        def add(i, _):
            a, b = i // B, i % B
            self.sums[a, b, :, self.mine] = self.sums[a, b, :, self.mine] + self.twin_buf[a, b]
            return 0

        lax.fori_loop(0, 4 * B, add, 0)
        self.go("inner")

    def from_inner(self):
        p = self.place
        B = p.inner_total
        for t in range(1, B):
            self.got(1 + t, self.inner_buf.at[t - 1, :, :, self.plane])

        def add(a, _):
            if B == 2:
                self.sums[a, p.inner, :, self.plane] = (self.sums[a, p.inner, :, self.plane]
                                                        + self.inner_buf[0, a, :, self.plane])
                return 0
            total = self.sums[a, p.inner, :, self.plane].astype(f32)
            for t in range(1, B):
                total = total + self.inner_buf[t - 1, a, :, self.plane].astype(f32)
            self.sums[a, p.inner, :, self.plane] = total.astype(bf16)
            return 0

        lax.fori_loop(0, 4, add, 0)
        self.go("outer")

    def from_outer(self):
        p = self.place
        B = p.inner_total
        for s in range(1, 4):
            self.got(B + s, self.outer_buf.at[s - 1, :, self.plane])
        total = self.sums[p.outer, p.inner, :, self.plane].astype(f32)
        for s in range(1, 4):
            total = total + self.outer_buf[s - 1, :, self.plane].astype(f32)
        self.sums[p.outer, p.inner, :, self.plane] = total.astype(bf16)
        self.go("last")

    def from_last(self):
        p = self.place
        self.got(4 + p.inner_total, self.last_buf.at[:, self.twin_plane])
        own = lambda cols: self.sums[p.outer, p.inner, :, cols].astype(f32)
        last = lambda cols: self.last_buf[:, cols].astype(f32)
        if p.pairs == 1:
            self.emit(self.mine, own(self.mine))
            self.emit(self.middle, own(self.middle) + last(self.middle))
            self.emit(self.theirs, last(self.theirs))
            return
        half, others = self.pair_bufs
        half[:, self.mine] = own(self.mine).astype(bf16)
        half[:, self.middle] = (own(self.middle) + last(self.middle)).astype(bf16)
        half[:, self.theirs] = last(self.theirs).astype(bf16)
        self.go("pairs")

    def from_pairs(self):
        p = self.place
        if p.pairs == 1:
            return
        half, others = self.pair_bufs
        total = half[...].astype(f32)
        for k in range(1, p.pairs):
            self.got(4 + p.inner_total + k, others.at[k - 1])
            total = total + others[k - 1].astype(f32)
        self.emit(pl.ds(0, self.terms.shape[-1]), total)

    def finish(self):
        for stage in ("core", "twin", "inner", "outer", "last") + (("pairs",) if self.place.pairs > 1 else ()):
            for c in self.copies(stage):
                c.wait_send()


class Total:
    def __init__(self, place, bufs, out, sems, base):
        self.place, self.landing, self.out = place, bufs[0], out
        self.send_sem, self.recv_sem = sems
        p, B = place, place.inner_total
        near = []
        for side in range(2):
            for t in range(B):
                for core in range(2):
                    if side or t or core:
                        dev = p.device(p.outer, p.inners[t], p.cores[core])[1]
                        near.append((p.d if not side else p.twin, dev))
        self.rounds = [(near, (p.side * B + p.inner) * 2 + p.core, 4 * B),
                       (p.outer_devices[1:], p.outer, 4)]
        if p.pairs > 1:
            self.rounds.append(([p.at_pair(k) for k in range(1, p.pairs)], p.d // 2, p.pairs))
        self.base = base

    @staticmethod
    def near_devices(place):
        return Total(place, [None], None, (None, None), 0).rounds[0][0]

    @staticmethod
    def count(B, pairs):
        return 4 * B + 4 + pairs

    @staticmethod
    def shapes(B, pairs, shape):
        return [pltpu.VMEM((Total.count(B, pairs),) + shape, f32)]

    def first(self, r):
        return sum(x[2] for x in self.rounds[:r])

    def send_copy(self, r, k):
        others, mine, _ = self.rounds[r]
        at = self.landing.at[self.first(r) + mine]
        return pltpu.make_async_remote_copy(src_ref=at, dst_ref=at, send_sem=self.send_sem.at[self.base + self.first(r) + k],
                                            recv_sem=self.recv_sem.at[self.base + self.first(r) + mine],
                                            device_id=others[k], device_id_type=MESH)

    def begin(self, r, value):
        others, mine, _ = self.rounds[r]
        self.landing[self.first(r) + mine] = value
        for k in range(len(others)):
            self.send_copy(r, k).start()

    def start(self, value):
        self.begin(0, value)

    def step(self, r):
        others, mine, members = self.rounds[r]
        for k in range(1, members):
            slot = self.first(r) + (mine + k) % members
            at = self.landing.at[slot]
            pltpu.make_async_remote_copy(src_ref=at, dst_ref=at, send_sem=self.send_sem.at[self.base],
                                         recv_sem=self.recv_sem.at[self.base + slot], device_id=self.place.me(),
                                         device_id_type=MESH).wait_recv()
        total = self.landing[self.first(r)]
        for k in range(1, members):
            total = total + self.landing[self.first(r) + k]
        if r + 1 < len(self.rounds):
            self.begin(r + 1, total)
        else:
            self.out[...] = total

    def steps(self):
        return [functools.partial(self.step, r) for r in range(len(self.rounds))]

    def finish(self):
        for r in range(len(self.rounds)):
            for k in range(len(self.rounds[r][0])):
                self.send_copy(r, k).wait_send()


def local(src, dst, sem):
    c = pltpu.make_async_copy(src, dst, sem)
    c.start()
    return c


BLOCKS = 3


def lane_tile(source, moves):
    lane = None
    out = None
    for col, to, size in moves:
        tile = source[:, col // 128 * 128:col // 128 * 128 + 128]
        shift = (to - col) % 128
        if shift:
            tile = pltpu.roll(tile, shift, 1)
        if out is None:
            out = tile
            lane = lax.broadcasted_iota(jnp.int32, tile.shape, 1)
        else:
            out = jnp.where((lane >= to) & (lane < to + size), tile, out)
    return out


def split_columns(source, owners):
    piece = source.shape[1] // owners // BLOCKS
    per = 128 // piece
    out = []
    for j in range(BLOCKS):
        tiles = [lane_tile(source, [(((t * per + q) * BLOCKS + j) * piece, q * piece, piece) for q in range(per)])
                 for t in range(owners // per)]
        out.append(jnp.concatenate(tiles, axis=1))
    return out


def join_columns(parts, owners):
    source = jnp.concatenate(parts, axis=1)
    width = parts[0].shape[1]
    piece = width // owners
    per = 128 // piece
    tiles = []
    for t in range(source.shape[1] // 128):
        moves = []
        for q in range(per):
            unit = t * per + q
            moves.append(((unit % BLOCKS) * width + unit // BLOCKS * piece, q * piece, piece))
        tiles.append(lane_tile(source, moves))
    return jnp.concatenate(tiles, axis=1)


EARLY = 2
PARTS = 3


def attend_block(counts_ref, q_ref, k_ref, v_ref, mixed_ref, lse_ref, pair, block):
    rows = q_ref.shape[0]
    lane = lax.broadcasted_iota(jnp.int32, (QB, 128), 1)
    first = pl.multiple_of(block * QB, QB)
    cols = pl.ds(pl.multiple_of(pair * 128, 128), 128)
    q = q_ref[pl.ds(first, QB), cols]
    k = k_ref[:, cols]
    v = v_ref[:, cols]
    ends = image_ends(counts_ref[0], counts_ref[1], rows)
    rid = image_of(first + lax.broadcasted_iota(jnp.int32, (QB, 1), 0), ends)
    cid = image_of(lax.broadcasted_iota(jnp.int32, (1, rows), 1), ends)
    bias = jnp.where(rid == cid, 0.0, NEG)
    outs = []
    lses = []
    for e in range(2):
        qm = jnp.where((lane < 64) == (e == 0), q, jnp.zeros_like(q))
        s = dot_nt(qm, k) + bias
        m = jnp.max(s, axis=1, keepdims=True)
        p = jnp.exp(s - m)
        l = jnp.sum(p, axis=1, keepdims=True)
        o = dot(p.astype(bf16), v)
        outs.append(o * (1.0 / l))
        lses.append(m + jnp.log(l))
    mixed_ref[pl.ds(first, QB), cols] = jnp.where(lane < 64, outs[0], outs[1]).astype(bf16)
    both = jnp.where(lane < 64, jnp.broadcast_to(lses[0], (QB, 128)), jnp.broadcast_to(lses[1], (QB, 128)))
    t = both.T
    lse_ref[pair, 0:1, pl.ds(first, QB)] = t[0:1, :]
    lse_ref[pair, 1:2, pl.ds(first, QB)] = t[64:65, :]


def gather_edge(rows, last=False):
    return rows // 3 if rows % 24 == 0 else rows // 4 if last or rows < 64 else rows * 3 // 8


def gather_plan(units, early, pieces):
    n = len(units)
    slots = [[] for _ in range(n + 12)]
    for t, u in enumerate(units):
        if t >= 3:
            slots[t - 2].append(u.start)
    for t, u in enumerate(units):
        inner, twin, core = (4, 5, 6) if t <= early else (5, 7, 9) if t <= PARTS else (6, 9, 11)
        stages = [(0, u.from_next), (1, u.relay_2), (2, u.relay_3), (2, u.take_2), (3, u.take_3),
                  (inner, u.from_inner), (twin, u.from_twin), (core, u.from_core)]
        for at, one in stages:
            slots[t + at].append(one)
    cut = early + 7
    rest = slots[cut:]
    while not rest[-1]:
        rest.pop()
    places = [[] for _ in range(pieces)]
    for k, slot in enumerate(rest):
        places[k * pieces // len(rest)] += slot
    for t in range(2, PARTS + 1):
        assert any(units[t].from_core in place for place in places[:(t - 1) * pieces // PARTS])
    return [one for slot in slots[:cut] for one in slot], places


def gather_kernel(dp_total, n, counts_ref, tokens_hbm, small_ref, qo_ref, ko_ref, vo_ref, oo_ref, uo_ref, do_ref,
                  q_hbm, k_hbm, v_hbm, vec_ref, mixed_hbm, lse_ref, up_last, qkv_all, o_all, up_all, down_all, small_all,
                  tokens_s, fi_s, q_s, k_s, v_s, mixed_s, w_s, small_s, up_own, send_sem, recv_sem, loc_sem):
    place = Place(dp_total, n)
    B = place.inner_total
    own = qo_ref.shape[0]
    piece = do_ref.shape[0] // BLOCKS
    greet(place.neighbours())
    take_tokens = local(tokens_hbm, tokens_s, loc_sem.at[0])
    sems = (send_sem, recv_sem)
    refs = [(small_all, 0)] + [(qkv_all.at[j], own) for j in range(PARTS)] + [(o_all, gather_edge(own))]
    for j in range(EARLY):
        refs += [(up_all.at[j], gather_edge(own)), (down_all.at[j], gather_edge(piece, j == EARLY - 1))]
    units = [Gather(place, ref, edge, sems, i * Gather.count(B))
             for i, (ref, edge) in enumerate(refs)]
    mine = lambda unit: unit.part(place.outer, place.inner, place.core, "plane")
    block = qkv_all.shape[-1]

    def own_part(source, j, i):
        return local(source.at[:, pl.ds(j * block, block)],
                     qkv_all.at[j, place.outer, place.inner, place.core, pl.ds(i * own, own)], loc_sem.at[2 + 2 * j + i % 2])

    fill = [local(small_ref, mine(units[0]), loc_sem.at[1])] + [own_part(ko_ref, j, 1) for j in range(PARTS)]

    @pl.when(place.side == 0)
    def _():
        for c in [own_part(qo_ref, j, 0) for j in range(PARTS)]:
            c.wait()

    @pl.when(place.side == 1)
    def _():
        for c in [own_part(vo_ref, j, 2) for j in range(PARTS)]:
            c.wait()

    for c in fill:
        c.wait()
    units[0].start()
    units[1].start()
    for j, part in enumerate(split_columns(uo_ref[...].astype(f32), n)):
        up_own[j] = part.astype(bf16)
    base = 1 + PARTS
    fill = [local(oo_ref.at[units[base].rows_of("plane")], mine(units[base]), loc_sem.at[1])]
    for j in range(EARLY):
        a, b = units[base + 1 + 2 * j], units[base + 2 + 2 * j]
        fill.append(local(up_own.at[j, a.rows_of("plane")], mine(a), loc_sem.at[2 + 2 * j]))
        rows = b.rows_of("plane")
        fill.append(local(do_ref.at[pl.ds(pl.multiple_of(j * piece + rows.start, 8), rows.size)], mine(b),
                          loc_sem.at[3 + 2 * j]))
    for j in range(EARLY, BLOCKS):
        fill.append(local(up_own.at[j], up_last.at[j - EARLY], loc_sem.at[2 + 2 * j]))
    for c in fill:
        c.wait()
    units[2].start()

    def vectors():
        local(small_all, small_s, loc_sem.at[1]).wait()
        total = jnp.zeros(vec_ref.shape, f32)
        for i in range(n):
            total = total + small_s[i // (2 * B), i // 2 % B, i % 2].astype(f32)
        vec_ref[...] = total

    rows, feat = tokens_s.shape
    blocks = rows // QB
    per = qkv_all.shape[-1] // 128 * blocks
    pieces = PARTS * per
    head, rest = gather_plan(units, 1, pieces)
    for one in head:
        one()
    weight_load = lambda j: pltpu.make_async_copy(qkv_all.at[j], w_s.at[j], loc_sem.at[2 + j])
    weight_load(0).start()
    vectors()
    take_tokens.wait()

    def norm_rows(i, _):
        sl = pl.ds(pl.multiple_of(i * RB, RB), RB)
        xhat, _q = norm_parts(tokens_s[sl, :].astype(f32))
        fi_s[sl, :] = (xhat * vec_ref[0:1, :] + vec_ref[1:2, :]).astype(bf16)
        return 0

    lax.fori_loop(0, rows // RB, norm_rows, 0)
    def project(j):
        cols = pl.ds(pl.multiple_of(j * block, 128), block)
        weight_load(j).wait()

        def project_rows(i, _):
            sl = pl.ds(pl.multiple_of(i * RB, RB), RB)
            fi = fi_s[sl, :]
            weight = lambda i: w_s[j, :, :, :, i * own:(i + 1) * own, :].reshape(feat, block)
            q_s[sl, cols] = ((dot(fi, weight(0)) + vec_ref[2:3, cols]).astype(bf16).astype(f32) * 0.125).astype(bf16)
            k_s[sl, cols] = dot(fi, weight(1)).astype(bf16)
            v_s[sl, cols] = (dot(fi, weight(2)) + vec_ref[3:4, cols]).astype(bf16)
            return 0

        lax.fori_loop(0, rows // RB, project_rows, 0)

    def attend_piece(i, _):
        @pl.when(i % per == 0)
        def _():
            project(i // per)

        attend_block(counts_ref, q_s, k_s, v_s, mixed_s, lse_ref, i // blocks, i % blocks)
        for at, todo in enumerate(rest):
            if todo:
                @pl.when(i == at)
                def _(todo=todo):
                    for one in todo:
                        one()

        @pl.when((i % per == per - 1) & (i < pieces - 1))
        def _():
            weight_load(i // per + 1).start()

        return 0

    lax.fori_loop(0, pieces, attend_piece, 0)
    keep = [local(a, b, loc_sem.at[2 + i]) for i, (a, b) in enumerate(((q_s, q_hbm), (k_s, k_hbm), (v_s, v_hbm)))]
    keep.append(local(mixed_s, mixed_hbm, loc_sem.at[0]))
    for c in keep:
        c.wait()
    for x in units:
        x.finish()


def gather_attend(sizes, counts, tokens, small, qw, kw, vw, ow, up, down):
    dp_total, n = sizes
    rows, feat = tokens.shape
    own = qw.shape[0]
    B = n // 8
    pairs = feat // 128
    s = jax.ShapeDtypeStruct
    vm = pl.BlockSpec(memory_space=pltpu.VMEM)
    anyspec = pl.BlockSpec(memory_space=pl.ANY)
    full = lambda *dims: (4, B, 2) + dims
    width = up.shape[1] // BLOCKS
    piece = down.shape[0] // BLOCKS
    act = s((rows, feat), bf16)
    copies = (2 + PARTS + 2 * EARLY) * Gather.count(B)
    return pl.pallas_call(
        functools.partial(gather_kernel, dp_total, n),
        in_specs=[pl.BlockSpec(memory_space=pltpu.SMEM), anyspec] + [vm] * 7,
        out_specs=[anyspec] * 3 + [vm, anyspec, vm] + [anyspec] * 6,
        out_shape=[act, act, act, s(small.shape, f32), act, s((pairs, 2, rows), f32),
                   s((max(1, BLOCKS - EARLY), own, width), bf16), s((PARTS,) + full(3 * own, feat // PARTS), bf16),
                   s(full(own, feat), bf16), s((EARLY,) + full(own, width), bf16),
                   s((EARLY,) + full(piece, feat), bf16), s(full(*small.shape), bf16)],
        scratch_shapes=[pltpu.VMEM((rows, feat), bf16)] * 6 + [
            pltpu.VMEM((PARTS,) + full(3 * own, feat // PARTS), bf16), pltpu.VMEM(full(*small.shape), bf16),
            pltpu.VMEM((BLOCKS, own, width), bf16), pltpu.SemaphoreType.DMA((copies,)),
            pltpu.SemaphoreType.DMA((copies,)), pltpu.SemaphoreType.DMA((6 + 2 * BLOCKS,))],
        compiler_params=pltpu.CompilerParams(collective_id=1, has_side_effects=True, vmem_limit_bytes=60 * 2**20),
        name="gather_attend",
    )(counts, tokens, small, qw, kw, vw, ow, up, down)


def scatter_edge(width):
    return 128 if width == 768 else width // 4 if width % 512 == 0 else width // 3


def late_edge(rows):
    return 16 if rows % 48 == 0 or rows == 64 else 0


def key_lanes(keys, ends):
    lane = lax.broadcasted_iota(jnp.int32, keys.shape, 1)
    image = image_of(lax.broadcasted_iota(jnp.int32, keys.shape, 0), ends)
    return [jnp.where((lane < 64) == (e == 0), keys, jnp.where(image == lane - 64 * (1 - e), 0.0, NEG).astype(bf16))
            for e in range(2)]


def query_lanes(queries, first, ends, e):
    lane = lax.broadcasted_iota(jnp.int32, queries.shape, 1)
    image = image_of(first + lax.broadcasted_iota(jnp.int32, queries.shape, 0), ends)
    return jnp.where((lane < 64) == (e == 0), queries, jnp.where(image == lane - 64 * (1 - e), 1.0, 0.0).astype(bf16))


def layer_kernel(dp_total, n, counts_ref, mixed_hbm, tokens_ref, cot_hbm, outw_ref, vec_ref, lse_ref, up_hbm, down_hbm,
                 up_last, down_own, q_hbm, k_hbm, v_hbm, qkv_all,
                 layer_ref, gtok_ref, gup_ref, gdown_ref, gq_ref, gk_ref, gv_ref, go_ref, total_ref,
                 res_s, si_s, gb_s, mixed_s, hid_s, gi_s, up_s, down_s, kt_s, ub_s, gub_s, gqkv_s, small_s, *rest):
    rows, feat = tokens_ref.shape
    width = gi_s.shape[1]
    own = gq_ref.shape[0]
    piece = gdown_ref.shape[0] // BLOCKS
    heads = feat // 128
    place = Place(dp_total, n)
    B, pairs = place.inner_total, place.pairs
    per = 5 if pairs == 1 else 7
    uterm_s, dterm_s = rest[:2]
    ubufs, dbufs, obufs, abufs = (rest[2 + i * per:2 + (i + 1) * per] for i in range(4))
    total_bufs = rest[2 + 4 * per:3 + 4 * per]
    send_sem, recv_sem, loc_sem, gather_send, gather_recv, weight_sem = rest[3 + 4 * per:]
    sems = (send_sem, recv_sem)
    count = Scatter.count(B, pairs)
    wide = lambda start: pl.ds(start, feat)
    load = lambda j: (pltpu.make_async_copy(up_hbm.at[j], up_s.at[j], loc_sem.at[2 * j]),
                      pltpu.make_async_copy(down_hbm.at[j], down_s.at[j], loc_sem.at[2 * j + 1]))
    at_end = 3 * feat
    first_loads = [local(mixed_hbm, mixed_s, loc_sem.at[2 * BLOCKS]),
                   local(cot_hbm, hid_s.at[:, wide(at_end)], loc_sem.at[2 * BLOCKS + 1])]
    for j in range(EARLY):
        for c in load(j):
            c.start()
    late = []
    for j in range(EARLY, BLOCKS):
        late += [(up_s.at[j], late_edge(own), up_last.at[j - EARLY], 0), (down_s.at[j], late_edge(piece), down_own, j * piece)]
    gathers = []
    for i, (ref, edge, source, start) in enumerate(late):
        unit = Gather(place, ref, edge, (gather_send, gather_recv), i * Gather.count(B))
        gathers.append(unit)
        part = unit.rows_of("plane")
        first_loads.append(local(source.at[pl.ds(pl.multiple_of(start + part.start, 8), part.size)],
                                 unit.part(place.outer, place.inner, place.core, "plane"),
                                 loc_sem.at[2 * EARLY + i]))
    gu, gd = gathers

    def unit_u(j):
        def emit(cols, value):
            gup_ref[:, pl.ds(pl.multiple_of(j * width + cols.start, 128), cols.size)] = value
        return Scatter(place, uterm_s.at[j % 2], [b.at[j] for b in ubufs], scatter_edge(width), emit, sems,
                       2 * j * count)

    def unit_d(j):
        def emit(cols, value):
            gdown_ref[pl.ds(pl.multiple_of(j * piece, 8), piece), cols] = value
        return Scatter(place, dterm_s.at[j % 2], [b.at[j] for b in dbufs], scatter_edge(feat), emit, sems,
                       (2 * j + 1) * count)

    def emit_out(cols, value):
        go_ref[:, cols] = value

    unit_o = Scatter(place, uterm_s.at[1, :, :, :, :, wide(0)], obufs, 256, emit_out, sems, 2 * BLOCKS * count)

    def pair_term(p):
        return dterm_s.at[1, :, :, :, pl.ds(0, own), pl.ds(pl.multiple_of(p % 2 * 384, 128), 384)]

    def unit_a(p):
        def emit(cols, value):
            gqkv_s[p, :, cols] = value
        return Scatter(place, pair_term(p), [b.at[p] for b in abufs], 128, emit, sems,
                       (2 * BLOCKS + 1 + p) * count)

    small = Total(place, total_bufs, total_ref, sems, (2 * BLOCKS + 1 + heads) * count)

    def last(unit):
        unit.from_last()
        unit.from_pairs()

    def sent(unit, *stages):
        for stage in stages:
            for c in unit.copies(stage):
                c.wait_send()

    rest_stages = ("twin", "inner", "outer", "last") + (("pairs",) if pairs > 1 else ())
    gain_one, shift_one = vec_ref[0:1, :], vec_ref[1:2, :]
    obias, gain, shift, dbias = (vec_ref[i:i + 1, :] for i in range(4, 8))
    ub = jnp.concatenate([vec_ref[8 + i:9 + i, :] for i in range(BLOCKS * width // feat)], axis=1)
    for j, part in enumerate(split_columns(jnp.broadcast_to(ub, (8, ub.shape[1])), n)):
        ub_s[j] = part
    small_s[...] = jnp.zeros_like(small_s)
    for c in first_loads:
        c.wait()

    def begin(i, _):
        first = pl.multiple_of(i * RB, RB)
        sl = pl.ds(first, RB)
        res = tokens_ref[sl, :].astype(f32) + (dot(mixed_s[sl, :], outw_ref[...]) + obias)
        res_s[sl, :] = res
        xhat, _q = norm_parts(res)
        si_s[sl, :] = (xhat * gain + shift).astype(bf16)
        gb_s[sl, :] = jnp.where(live_mask(counts_ref, first, RB), hid_s[sl, wide(at_end)], jnp.zeros((), bf16))
        gtok_ref[sl, :] = jnp.zeros((RB, feat), f32)
        return 0

    lax.fori_loop(0, rows // RB, begin, 0)
    greet(place.neighbours(pairs=True))
    gu.start()
    gd.start()

    def block(j, _):
        @pl.when(j < EARLY)
        def _():
            for c in load(j):
                c.wait()

        upw = lambda: up_s[j].reshape(feat, width)
        downw = lambda: down_s[j].reshape(width, feat)
        cols = pl.ds(pl.multiple_of(j * width, 128), width)
        gub_s[j] = jnp.zeros(gub_s.shape[1:], f32)

        def after(back, when, todo):
            @pl.when(when & (j >= back))
            def _():
                todo(j - back)

        def rows_piece(i, _):
            sl = pl.ds(pl.multiple_of(i * RB, RB), RB)
            pre = dot(si_s[sl, :], upw()) + ub_s[j, 0:1, :]
            cdf = 0.5 + 0.5 * lax.erf(pre * INV_SQRT2)
            pdf = jnp.exp(-0.5 * pre * pre) * INV_SQRT2PI
            hid_s[sl, cols] = (pre * cdf).astype(bf16)
            gi = (dot_nt(gb_s[sl, :], downw()) * (cdf + pre * pdf)).astype(bf16)
            gi_s[sl, :] = gi
            gub_s[j, 0:1, :] += jnp.sum(gi.astype(f32), axis=0, keepdims=True)
            for at, row, todo in ((0, 0, (gu.from_next,)), (0, 1, (gu.relay_2, gd.from_next)),
                                  (0, 2, (gu.relay_3, gu.take_2, gd.relay_2)),
                                  (0, 3, (gu.take_3, gd.relay_3, gd.take_2)), (1, 0, (gd.from_inner,)),
                                  (1, 1, (gu.from_twin,)), (1, 2, (gd.from_twin,)), (1, 3, (gu.from_core,))):
                @pl.when((j == at) & (i == row))
                def _(todo=todo):
                    for one in todo:
                        one()
            after(1, i == 0, lambda k: unit_d(k).from_core())
            after(1, i == 1, lambda k: unit_u(k).from_core())
            after(2, i == 1, lambda k: unit_d(k).from_inner())
            after(1, i == 3, lambda k: unit_d(k).from_twin())
            return 0

        lax.fori_loop(0, rows // RB, rows_piece, 0)
        always = j >= 0
        after(2, always, lambda k: (sent(unit_u(k), "core"), sent(unit_d(k), "core")))
        dterm_s[j % 2] = dot_tn(hid_s[:, cols], gb_s[...]).astype(bf16).reshape(dterm_s.shape[1:])
        unit_d(j).start()

        @pl.when(j == 0)
        def _():
            gd.take_3()

        after(1, always, lambda k: unit_u(k).from_twin())
        after(2, always, lambda k: unit_u(k).from_inner())
        uterm_s[j % 2] = dot_tn(si_s[...], gi_s[...]).astype(bf16).reshape(uterm_s.shape[1:])
        unit_u(j).start()
        gtok_ref[...] += dot_nt(gi_s[...], upw())

        @pl.when(j == 0)
        def _():
            gu.from_inner()

        @pl.when(j == 1)
        def _():
            gd.from_core()

        return 0

    lax.fori_loop(0, BLOCKS, block, 0)
    end, before = BLOCKS - 1, BLOCKS - 2
    gu.finish()
    gd.finish()
    third = qkv_all.shape[-1]
    weights = [local(qkv_all.at[j, :, :, :, pl.ds(i * own, own)], up_s.at[i, :, :, :, :, pl.ds(j * third, third)],
                     weight_sem.at[i * PARTS + j]) for i in range(3) for j in range(PARTS)]

    def finish_rows(i, _):
        first = pl.multiple_of(i * RB, RB)
        sl = pl.ds(first, RB)
        res = res_s[sl, :]
        layer = res + (dot(hid_s[sl, :], down_s[...].reshape(BLOCKS * width, feat)) + dbias)
        layer_ref[sl, :] = jnp.where(live_mask(counts_ref, first, RB), layer, 0.0).astype(bf16)
        xhat, q = norm_parts(res)
        gs = gtok_ref[sl, :]
        t = gs * gain
        gb = gb_s[sl, :].astype(f32)
        gres = gb + q * (t - jnp.mean(t, axis=-1, keepdims=True) - xhat * jnp.mean(t * xhat, axis=-1, keepdims=True))
        gtok_ref[sl, :] = gres
        ga = gres.astype(bf16)
        si_s[sl, :] = ga
        small_s[7:8, :] += jnp.sum(gb, axis=0, keepdims=True)
        small_s[5:6, :] += jnp.sum(gs * xhat, axis=0, keepdims=True)
        small_s[6:7, :] += jnp.sum(gs, axis=0, keepdims=True)
        small_s[4:5, :] += jnp.sum(ga.astype(f32), axis=0, keepdims=True)
        hid_s[sl, wide(at_end)] = dot_nt(ga, outw_ref[...]).astype(bf16)

        def at(k, *todo):
            @pl.when(i == k)
            def _():
                for one in todo:
                    one()

        at(0, lambda: unit_d(end).from_core(), lambda: unit_d(0).from_outer())
        at(1, lambda: unit_u(end).from_core(), lambda: unit_d(before).from_inner())
        at(2, lambda: unit_u(0).from_outer())
        at(3, lambda: unit_d(end).from_twin())
        return 0

    lax.fori_loop(0, rows // RB, finish_rows, 0)
    take = [local(x, hid_s.at[:, wide(i * feat)], loc_sem.at[3 + i]) for i, x in enumerate((q_hbm, k_hbm, v_hbm))]
    sent(unit_u(before), "core")
    sent(unit_d(before), "core")
    unit_o.terms[...] = dot_tn(mixed_s[...], si_s[...]).astype(bf16).reshape(unit_o.terms.shape)
    unit_o.start()
    unit_u(end).from_twin()
    unit_u(before).from_inner()
    gub = join_columns([gub_s[j] for j in range(BLOCKS)], n)
    for i in range(gub.shape[1] // feat):
        small_s[8 + i:9 + i, :] = gub[0:1, i * feat:(i + 1) * feat]

    def norm_rows(i, _):
        sl = pl.ds(pl.multiple_of(i * RB, RB), RB)
        xhat, _q = norm_parts(tokens_ref[sl, :].astype(f32))
        gi_s[sl, wide(0)] = (xhat * gain_one + shift_one).astype(bf16)
        return 0

    lax.fori_loop(0, rows // RB, norm_rows, 0)
    for c in take:
        c.wait()
    ends = image_ends(counts_ref[0], counts_ref[1], rows)
    key_at = lambda e: pl.ds(feat + e * 128, 128)
    dk_at, dv_at = pl.ds(0, 128), pl.ds(128, 128)

    def pair(p, _):
        part = lambda which: pl.ds(pl.multiple_of(which * feat + p * 128, 128), 128)
        cols = part(0)
        keys = hid_s[:, part(1)]
        for e, x in enumerate(key_lanes(keys, ends)):
            gi_s[:, key_at(e)] = x
        kt_s[...] = keys.T
        res_s[:, pl.ds(0, 256)] = jnp.zeros((rows, 256), f32)

        def attend_back(b, _):
            first = pl.multiple_of(b * QB, QB)
            sl = pl.ds(first, QB)
            q, do = hid_s[sl, part(0)], hid_s[sl, part(3)]
            v = hid_s[:, part(2)]
            lane = lax.broadcasted_iota(jnp.int32, q.shape, 1)
            zero = jnp.zeros_like(q)
            dqs = []
            dks = dvs = None
            for e in range(2):
                mask = (lane < 64) == (e == 0)
                qm, dom = jnp.where(mask, q, zero), jnp.where(mask, do, zero)
                s = dot_nt(gi_s[:, key_at(e)], query_lanes(q, first, ends, e))
                probs = jnp.exp(s - lse_ref[p, e:e + 1, sl])
                dp = dot_nt(v, dom)
                centre = jnp.sum(probs * dp, axis=0, keepdims=True)
                ds = (probs * (dp - centre)).astype(bf16)
                dv_e = dot(probs.astype(bf16), dom)
                dk_e = dot(ds, qm)
                dqs.append(dot(kt_s[e * 64:(e + 1) * 64, :], ds))
                dvs = dv_e if dvs is None else dvs + dv_e
                dks = dk_e if dks is None else dks + dk_e
            res_s[:, dk_at] += dks
            res_s[:, dv_at] += dvs
            gb_s[sl, cols] = (jnp.concatenate(dqs, axis=0).T * 0.125).astype(bf16)

            def at(k, when, todo):
                @pl.when((b == k) & when)
                def _():
                    todo()

            at(0, p == 0, lambda: last(unit_d(0)))
            at(1, p == 0, lambda: (unit_o.from_core(), last(unit_u(0))))
            at(2, p == 0, lambda: unit_d(before).from_outer())
            at(3, p == 0, lambda: (unit_u(before).from_outer(), unit_d(end).from_inner()))
            at(0, p == 1, lambda: unit_o.from_twin())
            at(1, p == 1, lambda: (last(unit_d(before)), unit_u(end).from_inner()))
            at(2, p == 1, lambda: last(unit_u(before)))
            at(3, p == 1, lambda: unit_o.from_inner())
            at(0, p == 2, lambda: unit_d(end).from_outer())
            at(2, p == 2, lambda: unit_u(end).from_outer())
            at(3, p == 2, lambda: (last(unit_d(end)), unit_o.from_outer()))
            at(0, p == 3, lambda: last(unit_u(end)))
            at(2, p == 3, lambda: last(unit_o))
            at(1, p >= 1, lambda: unit_a(p - 1).from_core())
            at(3, p >= 1, lambda: unit_a(p - 1).from_twin())
            at(1, p >= 2, lambda: unit_a(p - 2).from_inner())
            at(0, p >= 3, lambda: unit_a(p - 3).from_outer())
            at(2, p >= 3, lambda: last(unit_a(p - 3)))
            return 0

        lax.fori_loop(0, rows // QB, attend_back, 0)
        dk, dv = res_s[:, dk_at].astype(bf16), res_s[:, dv_at].astype(bf16)
        mixed_s[:, cols] = dk
        si_s[:, cols] = dv
        both = jnp.concatenate([gb_s[:, cols], dk, dv], axis=1)

        @pl.when(p >= 2)
        def _():
            sent(unit_a(p - 2), "core")

        term = pair_term(p)
        term[...] = dot_tn(gi_s[:, wide(0)], both).astype(bf16).reshape(term.shape)
        unit_a(p).start()
        return 0

    lax.fori_loop(0, heads, pair, 0)
    for c in weights:
        c.wait()

    def back_rows(i, _):
        sl = pl.ds(pl.multiple_of(i * RB, RB), RB)
        dq, dk, dv = gb_s[sl, :], mixed_s[sl, :], si_s[sl, :]
        weight = lambda i: up_s[i, :, :, :, :, wide(0)].reshape(feat, feat)
        gs = dot_nt(dq, weight(0)) + dot_nt(dk, weight(1)) + dot_nt(dv, weight(2))
        xhat, q = norm_parts(tokens_ref[sl, :].astype(f32))
        t = gs * gain_one
        gtok_ref[sl, :] += q * (t - jnp.mean(t, axis=-1, keepdims=True)
                                - xhat * jnp.mean(t * xhat, axis=-1, keepdims=True))
        for r, a in enumerate((gs * xhat, gs, dq.astype(f32), dv.astype(f32))):
            small_s[r:r + 1, :] += jnp.sum(a, axis=0, keepdims=True)

        def at(k, *todo):
            @pl.when(i == k)
            def _():
                for one in todo:
                    one()

        at(0, lambda: unit_a(heads - 3).from_outer(), lambda: unit_a(heads - 1).from_core())
        at(1, lambda: unit_a(heads - 2).from_inner(), lambda: unit_a(heads - 1).from_twin())
        at(2, lambda: last(unit_a(heads - 3)))
        at(3, lambda: unit_a(heads - 2).from_outer(), lambda: unit_a(heads - 1).from_inner())
        return 0

    lax.fori_loop(0, rows // RB, back_rows, 0)
    small.start(small_s[...])
    steps = small.steps()
    last(unit_a(heads - 2))
    gup_ref[...] = join_columns([gup_ref[:, j * width:(j + 1) * width] for j in range(BLOCKS)], n)
    steps[0]()
    unit_a(heads - 1).from_outer()
    steps[1]()
    last(unit_a(heads - 1))
    for one in steps[2:]:
        one()
    for p in range(heads):
        for i, ref in enumerate((gq_ref, gk_ref, gv_ref)):
            ref[:, p * 128:(p + 1) * 128] = gqkv_s[p, :, i * 128:(i + 1) * 128]

    def drain(j, _):
        sent(unit_u(j), *rest_stages)
        sent(unit_d(j), *rest_stages)
        return 0

    lax.fori_loop(0, BLOCKS, drain, 0)
    sent(unit_u(end), "core")
    sent(unit_d(end), "core")
    sent(unit_o, "core", *rest_stages)

    def drain_pairs(p, _):
        sent(unit_a(p), *rest_stages)

        @pl.when(p >= heads - 2)
        def _():
            sent(unit_a(p), "core")
        return 0

    lax.fori_loop(0, heads, drain_pairs, 0)
    small.finish()


def layer_back(sizes, counts, mixed, tokens, cot, outw, vec, lse, up_all, down_all, up_last, down_own, q, k, v, qkv_all):
    dp_total, n = sizes
    rows, feat = tokens.shape
    B, pairs = n // 8, dp_total // 2
    own, width = up_all.shape[-2:]
    piece = down_all.shape[-2]
    heads = feat // 128
    s = jax.ShapeDtypeStruct
    vm = pl.BlockSpec(memory_space=pltpu.VMEM)
    anyspec = pl.BlockSpec(memory_space=pl.ANY)
    act = lambda dt, cols=feat: pltpu.VMEM((rows, cols), dt)
    copies = (2 * BLOCKS + 1 + heads) * Scatter.count(B, pairs) + Total.count(B, pairs)
    return pl.pallas_call(
        functools.partial(layer_kernel, dp_total, n),
        in_specs=[pl.BlockSpec(memory_space=pltpu.SMEM), anyspec, vm, anyspec, vm, vm, vm] + [anyspec] * 8,
        out_specs=[vm] * 9,
        out_shape=[s((rows, feat), bf16), s((rows, feat), f32), s((own, BLOCKS * width), f32),
                   s((BLOCKS * piece, feat), f32)] + [s((own, feat), f32)] * 4 + [s(vec.shape, f32)],
        scratch_shapes=[act(f32), act(bf16), act(bf16), act(bf16), act(bf16, BLOCKS * width), act(bf16, width),
                        pltpu.VMEM((BLOCKS,) + up_all.shape[1:], bf16), pltpu.VMEM((BLOCKS,) + down_all.shape[1:], bf16),
                        pltpu.VMEM((128, rows), bf16), pltpu.VMEM((BLOCKS, 8, width), f32),
                        pltpu.VMEM((BLOCKS, 8, width), f32), pltpu.VMEM((heads, own, 384), f32),
                        pltpu.VMEM(vec.shape, f32),
                        pltpu.VMEM((2,) + up_all.shape[1:], bf16), pltpu.VMEM((2,) + down_all.shape[1:], bf16)]
        + Scatter.shapes(B, pairs, own, width, scatter_edge(width), (BLOCKS,))
        + Scatter.shapes(B, pairs, piece, feat, scatter_edge(feat), (BLOCKS,))
        + Scatter.shapes(B, pairs, own, feat, 256)
        + Scatter.shapes(B, pairs, own, 384, 128, (heads,))
        + Total.shapes(B, pairs, vec.shape)
        + [pltpu.SemaphoreType.DMA((copies,)), pltpu.SemaphoreType.DMA((copies,)),
           pltpu.SemaphoreType.DMA((2 * BLOCKS + 2,))]
        + [pltpu.SemaphoreType.DMA((2 * (BLOCKS - EARLY) * Gather.count(B),))] * 2
        + [pltpu.SemaphoreType.DMA((3 * PARTS,))],
        compiler_params=pltpu.CompilerParams(collective_id=2, has_side_effects=True, vmem_limit_bytes=67043328),
        name="layer_back",
    )(counts, mixed, tokens, cot, outw, vec, lse, up_all, down_all, up_last, down_own, q, k, v, qkv_all)

FSDP="fsdp"

def hand_kernel(*refs):
    half = len(refs) // 2
    for a, b in zip(refs[:half], refs[half:]):
        b[...] = a[...]


def hand_over(by_rows, by_cols, whole):
    steps = 4
    arrays = list(by_rows) + list(by_cols) + list(whole)
    specs = [pl.BlockSpec((a.shape[0] // steps, a.shape[1]), lambda i: (i, 0)) for a in by_rows]
    specs += [pl.BlockSpec((a.shape[0], a.shape[1] // steps), lambda i: (0, i)) for a in by_cols]
    specs += [pl.BlockSpec(a.shape, lambda i: (0, 0)) for a in whole]
    return pl.pallas_call(hand_kernel, grid=(steps,), in_specs=specs, out_specs=specs,
                          out_shape=[jax.ShapeDtypeStruct(a.shape, a.dtype) for a in arrays], name="hand_over")(*arrays)


def spread(vectors, index, total):
    own = vectors.shape[-1]
    at = lax.broadcasted_iota(jnp.int32, (1, total, own), 1)
    wide = jnp.where(at == index, vectors[:, None, :], jnp.zeros((), vectors.dtype))
    return wide.reshape(vectors.shape[0], total * own)

def on_device(sizes, tokens, image_counts, cotangent, first_gain, first_shift, query_weight, query_bias, key_weight,
              value_weight, value_bias, out_weight, out_bias, second_gain, second_shift, up_weight, up_bias,
              down_weight, down_bias):
    rows, feat = tokens.shape
    own = query_weight.shape[0]
    n = feat // own
    counts = image_counts[0]
    me = lax.axis_index(FSDP)
    eight = jnp.stack([first_gain, first_shift, query_bias, value_bias, out_bias, second_gain, second_shift, down_bias])
    small = jnp.concatenate([spread(eight, me, n), spread(up_bias[None], me, n).reshape(-1, feat)])
    small = jnp.concatenate([small, jnp.zeros((16 - small.shape[0], feat), bf16)])
    q, k, v, vec, mixed, lse, up_last, qkv_all, o_all, up_all, down_all, _ = gather_attend(
        sizes, counts, tokens, small, query_weight, key_weight, value_weight, out_weight, up_weight, down_weight)
    layer_out, gtok, gup, gdown, gq, gk, gv, go, total = layer_back(
        sizes, counts, mixed, tokens, cotangent, o_all.reshape(feat, feat), vec, lse, up_all, down_all, up_last,
        down_weight, q, k, v, qkv_all)
    gtok, layer_out, gdown, gup, gq, gk, gv, go = hand_over((gtok, layer_out, gdown), (gup,), (gq, gk, gv, go))
    mine = lax.dynamic_index_in_dim(total[:8].reshape(8, n, own), me, 1, keepdims=False)
    ub_mine = lax.dynamic_index_in_dim(total[8:12].reshape(n, -1), me, 0, keepdims=False)
    return (layer_out, gtok, mine[0], mine[1], gq, mine[2], gk, gv, mine[3], go, mine[4], mine[5], mine[6],
            gup, ub_mine, gdown, mine[7])


def solution(mesh):
    rows = P(("dp", "fsdp"), None)
    mat = P("fsdp", None)
    vec = P("fsdp")
    return jax.shard_map(
        functools.partial(on_device, (mesh.shape["dp"], mesh.shape["fsdp"])),
        mesh=mesh,
        in_specs=(rows, rows, rows, vec, vec, mat, vec, mat, mat, vec, mat, vec, vec, vec, mat, vec, mat, vec),
        out_specs=(rows, rows, vec, vec, mat, vec, mat, mat, vec, mat, vec, vec, vec, mat, vec, mat, vec),
        check_vma=False,
    )
```

time: 281 us -> 255 us (0.907)
  Pallas kernels: 266 us -> 250 us
  local copies, waits for them, and re-layouts: 13.5 us -> 3.3 us
    pallas_call x1, Pallas kernels: 97.9 us -> 81.9 us  [gather_attend(): pl.pallas_call(functools.partial(gather_kernel, dp_total, n), in_specs=[p...]
    unnamed x22 -> x2, local copies, waits for them, and re-layouts: 8.77 us -> 0.01 us
    pallas_call x0 -> x1, Pallas kernels: none -> 5.94 us  [hand_over(): pl.pallas_call(hand_kernel, grid=(steps,), in_specs=specs, out_specs=spec...]
    pallas_call x1, Pallas kernels: 168 us -> 162 us  [layer_back(): pl.pallas_call(functools.partial(layer_kernel, dp_total, n), in_specs=[pl...]
where the time goes in v7:
time: 255 us
  Pallas kernels  250 us (98%)
  local copies, waits for them, and re-layouts  3.3 us (1%)
    pallas_call x1, Pallas kernels, layer_back(): pl.pallas_call(functools.partial(layer_kernel, dp_total, n), in_specs=[pl...  162 us
    pallas_call x1, Pallas kernels, gather_attend(): pl.pallas_call(functools.partial(gather_kernel, dp_total, n), in_specs=[p...  81.9 us
    pallas_call x1, Pallas kernels, hand_over(): pl.pallas_call(hand_kernel, grid=(steps,), in_specs=specs, out_specs=spec...  5.94 us

profile of v7, /device:TPU:0, one launch (start us, length us, event | category | flops | bytes accessed | tf_op | source)
XLA Modules:
  0.0 254.7 jit_solution(7015076484827241412)
XLA Ops:
  0.7 0.1 broadcast_in_dim.44
  0.7 0.1 broadcast_in_dim.45
  0.8 0.8 stack.35
  1.6 0.1 broadcast_in_dim.48
  1.8 0.1 iota.11
  1.8 0.1 iota.12
  1.9 0.7 broadcast_in_dim.50
  2.6 0.1 broadcast_in_dim.51
  2.7 0.6 pad_maximum_fusion.small_ref
  3.3 81.9 %gather_attend.1 = (bf16[1024,768]{1,0:T(8,128)(2,1)}, bf16[1024,768]{1,0:T(8,128)(2,1)}, bf16[1024,768]{1,0:T(8,128)(2,1)}, f32[16,768]{1,0:T(8,128)}, bf16[102...) custom-call(s32[2]{0:T(128)} %bitcast.30, ...), custom_call_target="tpu_custom_call" | custom-call | tf_op jit(solution)/shard_map/gather_attend/pallas_call | solution.py:763
  85.3 162.1 %layer_back.1 = (bf16[1024,768]{1,0:T(8,128)(2,1)}, f32[1024,768]{1,0:T(8,128)}, f32[48,3072]{1,0:T(8,128)}, f32[192,768]{1,0:T(8,128)}, f32[48,768]{1,0:T(8,128...) custom-call(s32[2]{0:T(128)} %bitcast.31, ...), custom_call_target="tpu_custom_call" | custom-call | tf_op jit(solution)/shard_map/layer_back/pallas_call | solution.py:1186
  247.4 0.0 copy-start
  247.4 5.9 %hand_over.1 = (f32[1024,768]{1,0:T(8,128)}, bf16[1024,768]{1,0:T(8,128)(2,1)}, f32[192,768]{1,0:T(8,128)}, f32[48,3072]{1,0:T(8,128)}, f32[48,768]{1,0:T(8,128)...) custom-call(f32[1024,768]{1,0:T(8,128)} %get-tuple-element.56.refs_0_, ...), custom_call_target="tpu_custom_call" | custom-call | tf_op jit(solution)/shard_map/hand_over/pallas_call | solution.py:1225
  253.4 0.0 copy-done
  253.4 0.1 reshape.79
  253.5 0.6 fusion
  254.1 0.1 reshape.80
  254.1 0.6 constant_dynamic-slice_fusion.7
  (7 shorter events, 0.0 us)
Async XLA Ops:
  247.4 6.0 %copy-start = (f32[16,768]{1,0:T(8,128)S(1)}, f32[16,768]{1,0:T(8,128)}, u32[]{:S(2)}) copy-start(f32[16,768]{1,0:T(8,128)} %get-tuple-element.66) | copy-start | bytes 147460

commit v8 on v7

--- a/solution.py
+++ b/solution.py
@@ -516,6 +516,17 @@
     return c
 
 
+def mask_lanes(shape, first, ends, hit, miss):
+    lane = lax.broadcasted_iota(jnp.int32, shape, 1)
+    image = image_of(first + lax.broadcasted_iota(jnp.int32, shape, 0), ends)
+    return jnp.where(image == jnp.where(lane < 64, lane, lane - 64), hit, miss).astype(bf16)
+
+
+def head_lanes(values, others, e):
+    lane = lax.broadcasted_iota(jnp.int32, values.shape, 1)
+    return jnp.where((lane < 64) == (e == 0), values, others)
+
+
 BLOCKS = 3
 
 
@@ -561,27 +572,20 @@
     return jnp.concatenate(tiles, axis=1)
 
 
-EARLY = 2
 PARTS = 3
 
 
-def attend_block(counts_ref, q_ref, k_ref, v_ref, mixed_ref, lse_ref, pair, block):
-    rows = q_ref.shape[0]
+def attend_block(q_ref, k_ref, v_ref, own_ref, far_ref, mixed_ref, lse_ref, pair, block):
     lane = lax.broadcasted_iota(jnp.int32, (QB, 128), 1)
     first = pl.multiple_of(block * QB, QB)
     cols = pl.ds(pl.multiple_of(pair * 128, 128), 128)
     q = q_ref[pl.ds(first, QB), cols]
     k = k_ref[:, cols]
     v = v_ref[:, cols]
-    ends = image_ends(counts_ref[0], counts_ref[1], rows)
-    rid = image_of(first + lax.broadcasted_iota(jnp.int32, (QB, 1), 0), ends)
-    cid = image_of(lax.broadcasted_iota(jnp.int32, (1, rows), 1), ends)
-    bias = jnp.where(rid == cid, 0.0, NEG)
     outs = []
     lses = []
     for e in range(2):
-        qm = jnp.where((lane < 64) == (e == 0), q, jnp.zeros_like(q))
-        s = dot_nt(qm, k) + bias
+        s = dot_nt(head_lanes(q, own_ref[pl.ds(first, QB), :], e), head_lanes(k, far_ref[...], e))
         m = jnp.max(s, axis=1, keepdims=True)
         p = jnp.exp(s - m)
         l = jnp.sum(p, axis=1, keepdims=True)
@@ -606,7 +610,7 @@
         if t >= 3:
             slots[t - 2].append(u.start)
     for t, u in enumerate(units):
-        inner, twin, core = (4, 5, 6) if t <= early else (5, 7, 9) if t <= PARTS else (6, 9, 11)
+        inner, twin, core = (4, 5, 6) if t <= early else (5, 7, 9) if t <= PARTS else (5, 7, 9)
         stages = [(0, u.from_next), (1, u.relay_2), (2, u.relay_3), (2, u.take_2), (3, u.take_3),
                   (inner, u.from_inner), (twin, u.from_twin), (core, u.from_core)]
         for at, one in stages:
@@ -624,8 +628,8 @@
 
 
 def gather_kernel(dp_total, n, counts_ref, tokens_hbm, small_ref, qo_ref, ko_ref, vo_ref, oo_ref, uo_ref, do_ref,
-                  q_hbm, k_hbm, v_hbm, vec_ref, mixed_hbm, lse_ref, up_last, qkv_all, o_all, up_all, down_all, small_all,
-                  tokens_s, fi_s, q_s, k_s, v_s, mixed_s, w_s, small_s, up_own, send_sem, recv_sem, loc_sem):
+                  q_hbm, k_hbm, v_hbm, vec_ref, mixed_hbm, lse_ref, qkv_all, o_all, up_all, down_all, small_all,
+                  tokens_s, fi_s, own_s, far_s, q_s, k_s, v_s, mixed_s, w_s, small_s, up_own, send_sem, recv_sem, loc_sem, out_sem):
     place = Place(dp_total, n)
     B = place.inner_total
     own = qo_ref.shape[0]
@@ -634,8 +638,8 @@
     take_tokens = local(tokens_hbm, tokens_s, loc_sem.at[0])
     sems = (send_sem, recv_sem)
     refs = [(small_all, 0)] + [(qkv_all.at[j], own) for j in range(PARTS)] + [(o_all, gather_edge(own))]
-    for j in range(EARLY):
-        refs += [(up_all.at[j], gather_edge(own)), (down_all.at[j], gather_edge(piece, j == EARLY - 1))]
+    for j in range(BLOCKS):
+        refs += [(up_all.at[j], gather_edge(own)), (down_all.at[j], gather_edge(piece, j == BLOCKS - 1))]
     units = [Gather(place, ref, edge, sems, i * Gather.count(B))
              for i, (ref, edge) in enumerate(refs)]
     mine = lambda unit: unit.part(place.outer, place.inner, place.core, "plane")
@@ -665,14 +669,12 @@
         up_own[j] = part.astype(bf16)
     base = 1 + PARTS
     fill = [local(oo_ref.at[units[base].rows_of("plane")], mine(units[base]), loc_sem.at[1])]
-    for j in range(EARLY):
+    for j in range(BLOCKS):
         a, b = units[base + 1 + 2 * j], units[base + 2 + 2 * j]
         fill.append(local(up_own.at[j, a.rows_of("plane")], mine(a), loc_sem.at[2 + 2 * j]))
         rows = b.rows_of("plane")
         fill.append(local(do_ref.at[pl.ds(pl.multiple_of(j * piece + rows.start, 8), rows.size)], mine(b),
                           loc_sem.at[3 + 2 * j]))
-    for j in range(EARLY, BLOCKS):
-        fill.append(local(up_own.at[j], up_last.at[j - EARLY], loc_sem.at[2 + 2 * j]))
     for c in fill:
         c.wait()
     units[2].start()
@@ -696,8 +698,13 @@
     vectors()
     take_tokens.wait()
 
+    ends = image_ends(counts_ref[0], counts_ref[1], rows)
+
     def norm_rows(i, _):
-        sl = pl.ds(pl.multiple_of(i * RB, RB), RB)
+        first = pl.multiple_of(i * RB, RB)
+        sl = pl.ds(first, RB)
+        own_s[sl, :] = mask_lanes((RB, 128), first, ends, 1.0, 0.0)
+        far_s[sl, :] = mask_lanes((RB, 128), first, ends, 0.0, NEG)
         xhat, _q = norm_parts(tokens_s[sl, :].astype(f32))
         fi_s[sl, :] = (xhat * vec_ref[0:1, :] + vec_ref[1:2, :]).astype(bf16)
         return 0
@@ -717,13 +724,20 @@
             return 0
 
         lax.fori_loop(0, rows // RB, project_rows, 0)
+        for c in out_copies(j)[:3]:
+            c.start()
+
+    def out_copies(j):
+        cols = pl.ds(pl.multiple_of(j * block, 128), block)
+        return [pltpu.make_async_copy(a.at[:, cols], b.at[:, cols], out_sem.at[4 * j + i])
+                for i, (a, b) in enumerate(((q_s, q_hbm), (k_s, k_hbm), (v_s, v_hbm), (mixed_s, mixed_hbm)))]
 
     def attend_piece(i, _):
         @pl.when(i % per == 0)
         def _():
             project(i // per)
 
-        attend_block(counts_ref, q_s, k_s, v_s, mixed_s, lse_ref, i // blocks, i % blocks)
+        attend_block(q_s, k_s, v_s, own_s, far_s, mixed_s, lse_ref, i // blocks, i % blocks)
         for at, todo in enumerate(rest):
             if todo:
                 @pl.when(i == at)
@@ -731,6 +745,10 @@
                     for one in todo:
                         one()
 
+        @pl.when(i % per == per - 1)
+        def _():
+            out_copies(i // per)[3].start()
+
         @pl.when((i % per == per - 1) & (i < pieces - 1))
         def _():
             weight_load(i // per + 1).start()
@@ -738,10 +756,9 @@
         return 0
 
     lax.fori_loop(0, pieces, attend_piece, 0)
-    keep = [local(a, b, loc_sem.at[2 + i]) for i, (a, b) in enumerate(((q_s, q_hbm), (k_s, k_hbm), (v_s, v_hbm)))]
-    keep.append(local(mixed_s, mixed_hbm, loc_sem.at[0]))
-    for c in keep:
-        c.wait()
+    for j in range(PARTS):
+        for c in out_copies(j):
+            c.wait()
     for x in units:
         x.finish()
 
@@ -759,19 +776,20 @@
     width = up.shape[1] // BLOCKS
     piece = down.shape[0] // BLOCKS
     act = s((rows, feat), bf16)
-    copies = (2 + PARTS + 2 * EARLY) * Gather.count(B)
+    copies = (2 + PARTS + 2 * BLOCKS) * Gather.count(B)
     return pl.pallas_call(
         functools.partial(gather_kernel, dp_total, n),
         in_specs=[pl.BlockSpec(memory_space=pltpu.SMEM), anyspec] + [vm] * 7,
-        out_specs=[anyspec] * 3 + [vm, anyspec, vm] + [anyspec] * 6,
-        out_shape=[act, act, act, s(small.shape, f32), act, s((pairs, 2, rows), f32),
-                   s((max(1, BLOCKS - EARLY), own, width), bf16), s((PARTS,) + full(3 * own, feat // PARTS), bf16),
-                   s(full(own, feat), bf16), s((EARLY,) + full(own, width), bf16),
-                   s((EARLY,) + full(piece, feat), bf16), s(full(*small.shape), bf16)],
-        scratch_shapes=[pltpu.VMEM((rows, feat), bf16)] * 6 + [
+        out_specs=[anyspec] * 3 + [vm, anyspec, vm] + [anyspec] * 5,
+        out_shape=[act, act, act, s(small.shape, f32), act, s((pairs, 2, rows), f32), s((PARTS,) + full(3 * own, feat // PARTS), bf16),
+                   s(full(own, feat), bf16), s((BLOCKS,) + full(own, width), bf16),
+                   s((BLOCKS,) + full(piece, feat), bf16), s(full(*small.shape), bf16)],
+        scratch_shapes=[pltpu.VMEM((rows, feat), bf16)] * 2 + [pltpu.VMEM((rows, 128), bf16)] * 2 + [
+            pltpu.VMEM((rows, feat), bf16)] * 4 + [
             pltpu.VMEM((PARTS,) + full(3 * own, feat // PARTS), bf16), pltpu.VMEM(full(*small.shape), bf16),
             pltpu.VMEM((BLOCKS, own, width), bf16), pltpu.SemaphoreType.DMA((copies,)),
-            pltpu.SemaphoreType.DMA((copies,)), pltpu.SemaphoreType.DMA((6 + 2 * BLOCKS,))],
+            pltpu.SemaphoreType.DMA((copies,)), pltpu.SemaphoreType.DMA((6 + 2 * BLOCKS,)),
+            pltpu.SemaphoreType.DMA((4 * PARTS,))],
         compiler_params=pltpu.CompilerParams(collective_id=1, has_side_effects=True, vmem_limit_bytes=60 * 2**20),
         name="gather_attend",
     )(counts, tokens, small, qw, kw, vw, ow, up, down)
@@ -781,27 +799,10 @@
     return 128 if width == 768 else width // 4 if width % 512 == 0 else width // 3
 
 
-def late_edge(rows):
-    return 16 if rows % 48 == 0 or rows == 64 else 0
-
-
-def key_lanes(keys, ends):
-    lane = lax.broadcasted_iota(jnp.int32, keys.shape, 1)
-    image = image_of(lax.broadcasted_iota(jnp.int32, keys.shape, 0), ends)
-    return [jnp.where((lane < 64) == (e == 0), keys, jnp.where(image == lane - 64 * (1 - e), 0.0, NEG).astype(bf16))
-            for e in range(2)]
-
-
-def query_lanes(queries, first, ends, e):
-    lane = lax.broadcasted_iota(jnp.int32, queries.shape, 1)
-    image = image_of(first + lax.broadcasted_iota(jnp.int32, queries.shape, 0), ends)
-    return jnp.where((lane < 64) == (e == 0), queries, jnp.where(image == lane - 64 * (1 - e), 1.0, 0.0).astype(bf16))
-
-
 def layer_kernel(dp_total, n, counts_ref, mixed_hbm, tokens_ref, cot_hbm, outw_ref, vec_ref, lse_ref, up_hbm, down_hbm,
-                 up_last, down_own, q_hbm, k_hbm, v_hbm, qkv_all,
+                 q_hbm, k_hbm, v_hbm, qkv_all,
                  layer_ref, gtok_ref, gup_ref, gdown_ref, gq_ref, gk_ref, gv_ref, go_ref, total_ref,
-                 res_s, si_s, gb_s, mixed_s, hid_s, gi_s, up_s, down_s, kt_s, ub_s, gub_s, gqkv_s, small_s, *rest):
+                 res_s, si_s, gb_s, mixed_s, hid_s, gi_s, up_s, down_s, kt_s, own_s, far_s, ub_s, gub_s, gqkv_s, small_s, *rest):
     rows, feat = tokens_ref.shape
     width = gi_s.shape[1]
     own = gq_ref.shape[0]
@@ -813,7 +814,7 @@
     uterm_s, dterm_s = rest[:2]
     ubufs, dbufs, obufs, abufs = (rest[2 + i * per:2 + (i + 1) * per] for i in range(4))
     total_bufs = rest[2 + 4 * per:3 + 4 * per]
-    send_sem, recv_sem, loc_sem, gather_send, gather_recv, weight_sem = rest[3 + 4 * per:]
+    send_sem, recv_sem, loc_sem, weight_sem = rest[3 + 4 * per:]
     sems = (send_sem, recv_sem)
     count = Scatter.count(B, pairs)
     wide = lambda start: pl.ds(start, feat)
@@ -822,22 +823,9 @@
     at_end = 3 * feat
     first_loads = [local(mixed_hbm, mixed_s, loc_sem.at[2 * BLOCKS]),
                    local(cot_hbm, hid_s.at[:, wide(at_end)], loc_sem.at[2 * BLOCKS + 1])]
-    for j in range(EARLY):
+    for j in range(BLOCKS):
         for c in load(j):
             c.start()
-    late = []
-    for j in range(EARLY, BLOCKS):
-        late += [(up_s.at[j], late_edge(own), up_last.at[j - EARLY], 0), (down_s.at[j], late_edge(piece), down_own, j * piece)]
-    gathers = []
-    for i, (ref, edge, source, start) in enumerate(late):
-        unit = Gather(place, ref, edge, (gather_send, gather_recv), i * Gather.count(B))
-        gathers.append(unit)
-        part = unit.rows_of("plane")
-        first_loads.append(local(source.at[pl.ds(pl.multiple_of(start + part.start, 8), part.size)],
-                                 unit.part(place.outer, place.inner, place.core, "plane"),
-                                 loc_sem.at[2 * EARLY + i]))
-    gu, gd = gathers
-
     def unit_u(j):
         def emit(cols, value):
             gup_ref[:, pl.ds(pl.multiple_of(j * width + cols.start, 128), cols.size)] = value
@@ -898,15 +886,10 @@
 
     lax.fori_loop(0, rows // RB, begin, 0)
     greet(place.neighbours(pairs=True))
-    gu.start()
-    gd.start()
 
     def block(j, _):
-        @pl.when(j < EARLY)
-        def _():
-            for c in load(j):
-                c.wait()
-
+        for c in load(j):
+            c.wait()
         upw = lambda: up_s[j].reshape(feat, width)
         downw = lambda: down_s[j].reshape(width, feat)
         cols = pl.ds(pl.multiple_of(j * width, 128), width)
@@ -926,14 +909,6 @@
             gi = (dot_nt(gb_s[sl, :], downw()) * (cdf + pre * pdf)).astype(bf16)
             gi_s[sl, :] = gi
             gub_s[j, 0:1, :] += jnp.sum(gi.astype(f32), axis=0, keepdims=True)
-            for at, row, todo in ((0, 0, (gu.from_next,)), (0, 1, (gu.relay_2, gd.from_next)),
-                                  (0, 2, (gu.relay_3, gu.take_2, gd.relay_2)),
-                                  (0, 3, (gu.take_3, gd.relay_3, gd.take_2)), (1, 0, (gd.from_inner,)),
-                                  (1, 1, (gu.from_twin,)), (1, 2, (gd.from_twin,)), (1, 3, (gu.from_core,))):
-                @pl.when((j == at) & (i == row))
-                def _(todo=todo):
-                    for one in todo:
-                        one()
             after(1, i == 0, lambda k: unit_d(k).from_core())
             after(1, i == 1, lambda k: unit_u(k).from_core())
             after(2, i == 1, lambda k: unit_d(k).from_inner())
@@ -945,31 +920,15 @@
         after(2, always, lambda k: (sent(unit_u(k), "core"), sent(unit_d(k), "core")))
         dterm_s[j % 2] = dot_tn(hid_s[:, cols], gb_s[...]).astype(bf16).reshape(dterm_s.shape[1:])
         unit_d(j).start()
-
-        @pl.when(j == 0)
-        def _():
-            gd.take_3()
-
         after(1, always, lambda k: unit_u(k).from_twin())
         after(2, always, lambda k: unit_u(k).from_inner())
         uterm_s[j % 2] = dot_tn(si_s[...], gi_s[...]).astype(bf16).reshape(uterm_s.shape[1:])
         unit_u(j).start()
         gtok_ref[...] += dot_nt(gi_s[...], upw())
-
-        @pl.when(j == 0)
-        def _():
-            gu.from_inner()
-
-        @pl.when(j == 1)
-        def _():
-            gd.from_core()
-
         return 0
 
     lax.fori_loop(0, BLOCKS, block, 0)
     end, before = BLOCKS - 1, BLOCKS - 2
-    gu.finish()
-    gd.finish()
     third = qkv_all.shape[-1]
     weights = [local(qkv_all.at[j, :, :, :, pl.ds(i * own, own)], up_s.at[i, :, :, :, :, pl.ds(j * third, third)],
                      weight_sem.at[i * PARTS + j]) for i in range(3) for j in range(PARTS)]
@@ -1018,8 +977,13 @@
     for i in range(gub.shape[1] // feat):
         small_s[8 + i:9 + i, :] = gub[0:1, i * feat:(i + 1) * feat]
 
+    ends = image_ends(counts_ref[0], counts_ref[1], rows)
+
     def norm_rows(i, _):
-        sl = pl.ds(pl.multiple_of(i * RB, RB), RB)
+        first = pl.multiple_of(i * RB, RB)
+        sl = pl.ds(first, RB)
+        own_s[sl, :] = mask_lanes((RB, 128), first, ends, 1.0, 0.0)
+        far_s[sl, :] = mask_lanes((RB, 128), first, ends, 0.0, NEG)
         xhat, _q = norm_parts(tokens_ref[sl, :].astype(f32))
         gi_s[sl, wide(0)] = (xhat * gain_one + shift_one).astype(bf16)
         return 0
@@ -1027,7 +991,6 @@
     lax.fori_loop(0, rows // RB, norm_rows, 0)
     for c in take:
         c.wait()
-    ends = image_ends(counts_ref[0], counts_ref[1], rows)
     key_at = lambda e: pl.ds(feat + e * 128, 128)
     dk_at, dv_at = pl.ds(0, 128), pl.ds(128, 128)
 
@@ -1035,8 +998,8 @@
         part = lambda which: pl.ds(pl.multiple_of(which * feat + p * 128, 128), 128)
         cols = part(0)
         keys = hid_s[:, part(1)]
-        for e, x in enumerate(key_lanes(keys, ends)):
-            gi_s[:, key_at(e)] = x
+        for e in range(2):
+            gi_s[:, key_at(e)] = head_lanes(keys, far_s[...], e)
         kt_s[...] = keys.T
         res_s[:, pl.ds(0, 256)] = jnp.zeros((rows, 256), f32)
 
@@ -1052,7 +1015,7 @@
             for e in range(2):
                 mask = (lane < 64) == (e == 0)
                 qm, dom = jnp.where(mask, q, zero), jnp.where(mask, do, zero)
-                s = dot_nt(gi_s[:, key_at(e)], query_lanes(q, first, ends, e))
+                s = dot_nt(gi_s[:, key_at(e)], head_lanes(q, own_s[sl, :], e))
                 probs = jnp.exp(s - lse_ref[p, e:e + 1, sl])
                 dp = dot_nt(v, dom)
                 centre = jnp.sum(probs * dp, axis=0, keepdims=True)
@@ -1171,7 +1134,7 @@
     small.finish()
 
 
-def layer_back(sizes, counts, mixed, tokens, cot, outw, vec, lse, up_all, down_all, up_last, down_own, q, k, v, qkv_all):
+def layer_back(sizes, counts, mixed, tokens, cot, outw, vec, lse, up_all, down_all, q, k, v, qkv_all):
     dp_total, n = sizes
     rows, feat = tokens.shape
     B, pairs = n // 8, dp_total // 2
@@ -1185,13 +1148,13 @@
     copies = (2 * BLOCKS + 1 + heads) * Scatter.count(B, pairs) + Total.count(B, pairs)
     return pl.pallas_call(
         functools.partial(layer_kernel, dp_total, n),
-        in_specs=[pl.BlockSpec(memory_space=pltpu.SMEM), anyspec, vm, anyspec, vm, vm, vm] + [anyspec] * 8,
+        in_specs=[pl.BlockSpec(memory_space=pltpu.SMEM), anyspec, vm, anyspec, vm, vm, vm] + [anyspec] * 6,
         out_specs=[vm] * 9,
         out_shape=[s((rows, feat), bf16), s((rows, feat), f32), s((own, BLOCKS * width), f32),
                    s((BLOCKS * piece, feat), f32)] + [s((own, feat), f32)] * 4 + [s(vec.shape, f32)],
         scratch_shapes=[act(f32), act(bf16), act(bf16), act(bf16), act(bf16, BLOCKS * width), act(bf16, width),
-                        pltpu.VMEM((BLOCKS,) + up_all.shape[1:], bf16), pltpu.VMEM((BLOCKS,) + down_all.shape[1:], bf16),
-                        pltpu.VMEM((128, rows), bf16), pltpu.VMEM((BLOCKS, 8, width), f32),
+                        pltpu.VMEM(up_all.shape, bf16), pltpu.VMEM(down_all.shape, bf16),
+                        pltpu.VMEM((128, rows), bf16), act(bf16, 128), act(bf16, 128), pltpu.VMEM((BLOCKS, 8, width), f32),
                         pltpu.VMEM((BLOCKS, 8, width), f32), pltpu.VMEM((heads, own, 384), f32),
                         pltpu.VMEM(vec.shape, f32),
                         pltpu.VMEM((2,) + up_all.shape[1:], bf16), pltpu.VMEM((2,) + down_all.shape[1:], bf16)]
@@ -1202,11 +1165,10 @@
         + Total.shapes(B, pairs, vec.shape)
         + [pltpu.SemaphoreType.DMA((copies,)), pltpu.SemaphoreType.DMA((copies,)),
            pltpu.SemaphoreType.DMA((2 * BLOCKS + 2,))]
-        + [pltpu.SemaphoreType.DMA((2 * (BLOCKS - EARLY) * Gather.count(B),))] * 2
         + [pltpu.SemaphoreType.DMA((3 * PARTS,))],
         compiler_params=pltpu.CompilerParams(collective_id=2, has_side_effects=True, vmem_limit_bytes=67043328),
         name="layer_back",
-    )(counts, mixed, tokens, cot, outw, vec, lse, up_all, down_all, up_last, down_own, q, k, v, qkv_all)
+    )(counts, mixed, tokens, cot, outw, vec, lse, up_all, down_all, q, k, v, qkv_all)
 
 FSDP="fsdp"
 
@@ -1243,11 +1205,10 @@
     eight = jnp.stack([first_gain, first_shift, query_bias, value_bias, out_bias, second_gain, second_shift, down_bias])
     small = jnp.concatenate([spread(eight, me, n), spread(up_bias[None], me, n).reshape(-1, feat)])
     small = jnp.concatenate([small, jnp.zeros((16 - small.shape[0], feat), bf16)])
-    q, k, v, vec, mixed, lse, up_last, qkv_all, o_all, up_all, down_all, _ = gather_attend(
+    q, k, v, vec, mixed, lse, qkv_all, o_all, up_all, down_all, _ = gather_attend(
         sizes, counts, tokens, small, query_weight, key_weight, value_weight, out_weight, up_weight, down_weight)
     layer_out, gtok, gup, gdown, gq, gk, gv, go, total = layer_back(
-        sizes, counts, mixed, tokens, cotangent, o_all.reshape(feat, feat), vec, lse, up_all, down_all, up_last,
-        down_weight, q, k, v, qkv_all)
+        sizes, counts, mixed, tokens, cotangent, o_all.reshape(feat, feat), vec, lse, up_all, down_all, q, k, v, qkv_all)
     gtok, layer_out, gdown, gup, gq, gk, gv, go = hand_over((gtok, layer_out, gdown), (gup,), (gq, gk, gv, go))
     mine = lax.dynamic_index_in_dim(total[:8].reshape(8, n, own), me, 1, keepdims=False)
     ub_mine = lax.dynamic_index_in_dim(total[8:12].reshape(n, -1), me, 0, keepdims=False)

time: 255 us -> 252 us (0.988)
  Pallas kernels: 250 us -> 246 us
    pallas_call x1, Pallas kernels: 162 us -> 150 us  [layer_back(): pl.pallas_call(functools.partial(layer_kernel, dp_total, n), in_specs=[pl...]
    pallas_call x1, Pallas kernels: 81.9 us -> 90.9 us  [gather_attend(): pl.pallas_call(functools.partial(gather_kernel, dp_total, n), in_specs=[p...]
where the time goes in v8:
time: 252 us; the launch traced here: 251 us
  Pallas kernels  246 us (98%)
  local copies, waits for them, and re-layouts  3.3 us (1%)
    pallas_call x1, Pallas kernels, layer_back(): pl.pallas_call(functools.partial(layer_kernel, dp_total, n), in_specs=[pl...  150 us
    pallas_call x1, Pallas kernels, gather_attend(): pl.pallas_call(functools.partial(gather_kernel, dp_total, n), in_specs=[p...  90.9 us
    pallas_call x1, Pallas kernels, hand_over(): pl.pallas_call(hand_kernel, grid=(steps,), in_specs=specs, out_specs=spec...  5.94 us

profile of v8, /device:TPU:0, one launch (start us, length us, event | category | flops | bytes accessed | tf_op | source)
XLA Modules:
  0.0 251.1 jit_solution(1510892427451937068)
XLA Ops:
  0.7 0.1 broadcast_in_dim.44
  0.7 0.1 broadcast_in_dim.45
  0.8 0.8 stack.35
  1.6 0.1 broadcast_in_dim.48
  1.8 0.1 iota.11
  1.8 0.1 iota.12
  1.9 0.7 broadcast_in_dim.50
  2.6 0.1 broadcast_in_dim.51
  2.7 0.6 pad_maximum_fusion.small_ref
  3.3 90.9 %gather_attend.1 = (bf16[1024,768]{1,0:T(8,128)(2,1)}, bf16[1024,768]{1,0:T(8,128)(2,1)}, bf16[1024,768]{1,0:T(8,128)(2,1)}, f32[16,768]{1,0:T(8,128)}, bf16[102...) custom-call(s32[2]{0:T(128)} %bitcast.30, ...), custom_call_target="tpu_custom_call" | custom-call | tf_op jit(solution)/shard_map/gather_attend/pallas_call | solution.py:780
  94.2 149.6 %layer_back.1 = (bf16[1024,768]{1,0:T(8,128)(2,1)}, f32[1024,768]{1,0:T(8,128)}, f32[48,3072]{1,0:T(8,128)}, f32[192,768]{1,0:T(8,128)}, f32[48,768]{1,0:T(8,128...) custom-call(s32[2]{0:T(128)} %bitcast.31, ...), custom_call_target="tpu_custom_call" | custom-call | tf_op jit(solution)/shard_map/layer_back/pallas_call | solution.py:1149
  243.8 0.0 copy-start
  243.8 5.9 %hand_over.1 = (f32[1024,768]{1,0:T(8,128)}, bf16[1024,768]{1,0:T(8,128)(2,1)}, f32[192,768]{1,0:T(8,128)}, f32[48,3072]{1,0:T(8,128)}, f32[48,768]{1,0:T(8,128)...) custom-call(f32[1024,768]{1,0:T(8,128)} %get-tuple-element.54.refs_0_, ...), custom_call_target="tpu_custom_call" | custom-call | tf_op jit(solution)/shard_map/hand_over/pallas_call | solution.py:1187
  249.8 0.0 copy-done
  249.8 0.1 reshape.79
  249.9 0.6 fusion
  250.5 0.1 reshape.80
  250.6 0.6 constant_dynamic-slice_fusion.7
  (7 shorter events, 0.0 us)
Async XLA Ops:
  243.8 6.0 %copy-start = (f32[16,768]{1,0:T(8,128)S(1)}, f32[16,768]{1,0:T(8,128)}, u32[]{:S(2)}) copy-start(f32[16,768]{1,0:T(8,128)} %get-tuple-element.64) | copy-start | bytes 147460

commit v9 on v8

--- a/solution.py
+++ b/solution.py
@@ -1102,35 +1102,38 @@
     steps = small.steps()
     last(unit_a(heads - 2))
     gup_ref[...] = join_columns([gup_ref[:, j * width:(j + 1) * width] for j in range(BLOCKS)], n)
+
+    def drain(j, _):
+        sent(unit_u(j), *rest_stages)
+        sent(unit_d(j), *rest_stages)
+        return 0
+
+    lax.fori_loop(0, BLOCKS, drain, 0)
+    sent(unit_u(end), "core")
+    sent(unit_d(end), "core")
+    sent(unit_o, "core", *rest_stages)
+
+    def drain_pairs(p, _):
+        sent(unit_a(p), *rest_stages)
+        return 0
+
+    lax.fori_loop(0, heads - 1, drain_pairs, 0)
+
+    def hand_pair(p):
+        for i, ref in enumerate((gq_ref, gk_ref, gv_ref)):
+            ref[:, p * 128:(p + 1) * 128] = gqkv_s[p, :, i * 128:(i + 1) * 128]
+
+    for p in range(heads - 1):
+        hand_pair(p)
     steps[0]()
     unit_a(heads - 1).from_outer()
     steps[1]()
     last(unit_a(heads - 1))
     for one in steps[2:]:
         one()
-    for p in range(heads):
-        for i, ref in enumerate((gq_ref, gk_ref, gv_ref)):
-            ref[:, p * 128:(p + 1) * 128] = gqkv_s[p, :, i * 128:(i + 1) * 128]
-
-    def drain(j, _):
-        sent(unit_u(j), *rest_stages)
-        sent(unit_d(j), *rest_stages)
-        return 0
-
-    lax.fori_loop(0, BLOCKS, drain, 0)
-    sent(unit_u(end), "core")
-    sent(unit_d(end), "core")
-    sent(unit_o, "core", *rest_stages)
-
-    def drain_pairs(p, _):
-        sent(unit_a(p), *rest_stages)
-
-        @pl.when(p >= heads - 2)
-        def _():
-            sent(unit_a(p), "core")
-        return 0
-
-    lax.fori_loop(0, heads, drain_pairs, 0)
+    hand_pair(heads - 1)
+    sent(unit_a(heads - 2), "core")
+    sent(unit_a(heads - 1), "core", *rest_stages)
     small.finish()
 
 
@@ -1179,7 +1182,7 @@
 
 
 def hand_over(by_rows, by_cols, whole):
-    steps = 4
+    steps = 2
     arrays = list(by_rows) + list(by_cols) + list(whole)
     specs = [pl.BlockSpec((a.shape[0] // steps, a.shape[1]), lambda i: (i, 0)) for a in by_rows]
     specs += [pl.BlockSpec((a.shape[0], a.shape[1] // steps), lambda i: (0, i)) for a in by_cols]

time: 252 us -> 250 us (level)
  no operation moved by 1% of the time
where the time goes in v9:
time: 250 us
  Pallas kernels  245 us (98%)
  local copies, waits for them, and re-layouts  3.3 us (1%)
    pallas_call x1, Pallas kernels, layer_back(): pl.pallas_call(functools.partial(layer_kernel, dp_total, n), in_specs=[pl...  149 us
    pallas_call x1, Pallas kernels, gather_attend(): pl.pallas_call(functools.partial(gather_kernel, dp_total, n), in_specs=[p...  90.9 us

profile of v9, /device:TPU:0, one launch (start us, length us, event | category | flops | bytes accessed | tf_op | source)
XLA Modules:
  0.0 250.0 jit_solution(958403918456730481)
XLA Ops:
  0.7 0.1 broadcast_in_dim.44
  0.7 0.1 broadcast_in_dim.45
  0.8 0.8 stack.35
  1.6 0.1 broadcast_in_dim.48
  1.8 0.1 iota.11
  1.8 0.1 iota.12
  1.9 0.7 broadcast_in_dim.50
  2.6 0.1 broadcast_in_dim.51
  2.7 0.6 pad_maximum_fusion.small_ref
  3.3 90.9 %gather_attend.1 = (bf16[1024,768]{1,0:T(8,128)(2,1)}, bf16[1024,768]{1,0:T(8,128)(2,1)}, bf16[1024,768]{1,0:T(8,128)(2,1)}, f32[16,768]{1,0:T(8,128)}, bf16[102...) custom-call(s32[2]{0:T(128)} %bitcast.30, ...), custom_call_target="tpu_custom_call" | custom-call | tf_op jit(solution)/shard_map/gather_attend/pallas_call | solution.py:780
  94.2 149.5 %layer_back.1 = (bf16[1024,768]{1,0:T(8,128)(2,1)}, f32[1024,768]{1,0:T(8,128)}, f32[48,3072]{1,0:T(8,128)}, f32[192,768]{1,0:T(8,128)}, f32[48,768]{1,0:T(8,128...) custom-call(s32[2]{0:T(128)} %bitcast.31, ...), custom_call_target="tpu_custom_call" | custom-call | tf_op jit(solution)/shard_map/layer_back/pallas_call | solution.py:1152
  243.7 0.0 copy-start
  243.7 5.0 %hand_over.1 = (f32[1024,768]{1,0:T(8,128)}, bf16[1024,768]{1,0:T(8,128)(2,1)}, f32[192,768]{1,0:T(8,128)}, f32[48,3072]{1,0:T(8,128)}, f32[48,768]{1,0:T(8,128)...) custom-call(f32[1024,768]{1,0:T(8,128)} %get-tuple-element.54.refs_0_, ...), custom_call_target="tpu_custom_call" | custom-call | tf_op jit(solution)/shard_map/hand_over/pallas_call | solution.py:1190
  248.7 0.0 copy-done
  248.7 0.1 reshape.79
  248.8 0.6 fusion
  249.4 0.1 reshape.80
  249.4 0.6 constant_dynamic-slice_fusion.7
  (7 shorter events, 0.0 us)
Async XLA Ops:
  243.7 5.0 %copy-start = (f32[16,768]{1,0:T(8,128)S(1)}, f32[16,768]{1,0:T(8,128)}, u32[]{:S(2)}) copy-start(f32[16,768]{1,0:T(8,128)} %get-tuple-element.64) | copy-start | bytes 147460
